TPU v7x, 256 devices: a whole 4x4x8 slice. The times are simulated.
256 devices in a mesh: lat: 32 (over z_hi, y, core), chan: 8 (over z_lo, x).
Axes of the slice: x: 4, y: 4, z: 8 (z_hi: 4, z_lo: 2; z = z_hi * 2 + z_lo), core: 2. Of those that a mesh axis runs over, the one named last changes fastest.
Arguments:
- fields: float32 [256, 900, 768], P(('lat', 'chan')), may hold values from -6 to 6
- first_gain: float32 [768], replicated, may hold values from 0.5 to 1.5
- first_shift: float32 [768], replicated, may hold values from -1.5 to 1.5
- filter_one: float32 [8, 2, 96, 96], P('chan'), may hold values from -0.4375 to 0.4375
- filter_one_bias: float32 [8, 2, 96], P('chan'), may hold values from -2.5 to 2.5
- filter_two: float32 [8, 2, 96, 96], P('chan'), may hold values from -0.4375 to 0.4375
- filter_two_bias: float32 [8, 2, 96], P('chan'), may hold values from -2.5 to 2.5
- second_gain: float32 [768], replicated, may hold values from 0.5 to 1.5
- second_shift: float32 [768], replicated, may hold values from -1.5 to 1.5
- dense_weights: bfloat16 [3072, 2, 768], P(('lat', 'chan')), may hold values from -0.21875 to 0.21875
- dense_bias: bfloat16 [3072], P(('lat', 'chan')), may hold values from -2.5 to 2.5
- output_bias: float32 [768], replicated, may hold values from -1.5 to 1.5
Outputs:
- block_output: float32 [256, 900, 768], P(('lat', 'chan'))
All inputs are finite; a program needn't handle non-finite values.
Results may differ from a plain program's by a relative error of at most 0.0025.
Values may be sent and summed in bfloat16 or wider, within the bound.
No kernel may reach another device: no remote copies, remote signals or barrier semaphores. Data moves between devices by JAX's collectives and lax.ppermute only.
A program may use at most 128 MiB of HBM per device.

v0:
```python
import functools

import jax
import jax.numpy as jnp
import numpy as np
from jax import lax
from jax.experimental import pallas as pl
from jax.experimental.pallas import tpu as pltpu
from jax.sharding import Mesh
from jax.sharding import PartitionSpec as P


W = 900
WP = 1024
KW = 256
H = 256
C = 768
BS = 96
NB = 8
TILE = 304
ROWS = 3 * TILE
norm_eps = 1e-05
shrink_level = 0.01
AXES = ("zh", "y", "co", "zl", "x")
bf16 = jnp.bfloat16
f32 = jnp.float32


def split_table(values):
    high = values.astype(np.float32).astype(jnp.bfloat16)
    low = (values - high.astype(np.float64)).astype(np.float32).astype(jnp.bfloat16)
    return high, low


def lon_tables():
    k = np.arange(KW)[:, None]
    w = np.arange(W)[None, :]
    angle = 2 * np.pi * (k * w % W) / W
    forward = np.zeros((KW, 2, WP))
    forward[:, 0, :W] = np.cos(angle)
    forward[:, 1, :W] = -np.sin(angle)
    forward = forward.reshape(2 * KW, WP) * W**-0.5
    factor = np.where(k == 0, 1.0, 2.0)
    backward = np.zeros((ROWS, KW, 2))
    backward[:W, :, 0] = (np.cos(angle) * factor).T
    backward[:W, :, 1] = (-np.sin(angle) * factor).T
    backward = backward.reshape(ROWS, 2 * KW) * W**-0.5
    return split_table(forward), split_table(backward)


def lat_tables():
    m = np.arange(H)[:, None]
    h = np.arange(H)[None, :]
    angle = 2 * np.pi * (m * h % H) / H
    cos, sin = np.cos(angle), np.sin(angle)
    forward = np.zeros((2, H, H, 2))
    forward[0, :, :, 0] = cos
    forward[0, :, :, 1] = sin
    forward[1, :, :, 0] = -sin
    forward[1, :, :, 1] = cos
    forward = forward.reshape(2 * H, 2 * H) * H**-0.5
    return split_table(forward), split_table(forward.T)


def dot(a, b):
    return jnp.dot(a, b, preferred_element_type=f32)


def split(x):
    high = x.astype(bf16)
    return high, (x - high.astype(f32)).astype(bf16)


def row_norm(parts, gain, shift):
    count = len(parts) * 128
    mean = jnp.sum(functools.reduce(jnp.add, parts), axis=-1, keepdims=True) / count
    centered = [p - mean for p in parts]
    square = functools.reduce(jnp.add, [c * c for c in centered])
    scale = lax.rsqrt(jnp.sum(square, axis=-1, keepdims=True) / count + norm_eps)
    return [
        c * scale * gain[j : j + 1, :] + shift[j : j + 1, :]
        for j, c in enumerate(centered)
    ]


def lon_kernel(x_ref, gain_ref, shift_ref, th_ref, tl_ref, modes_ref, base_ref, zh, zl):
    gain = gain_ref[...]
    shift = shift_ref[...]
    for start in range(0, W, 240):
        n = min(240, W - start)
        parts = [x_ref[pl.ds(6 * start + j, n, stride=6), :] for j in range(6)]
        normed = row_norm(parts, gain, shift)
        for j in range(6):
            lanes = slice(128 * j, 128 * j + 128)
            base_ref[start : start + n, lanes] = normed[j] + parts[j]
            high, low = split(normed[j])
            zh[start : start + n, lanes] = high
            zl[start : start + n, lanes] = low
    zh[W:WP, :] = jnp.zeros((WP - W, C), bf16)
    zl[W:WP, :] = jnp.zeros((WP - W, C), bf16)
    base_ref[W:ROWS, :] = jnp.zeros((ROWS - W, C), f32)
    modes = dot(th_ref[...], zh[...]) + dot(th_ref[...], zl[...]) + dot(tl_ref[...], zh[...])
    modes_ref[...] = modes.astype(bf16)


def pack_kernel(one_ref, one_bias_ref, two_ref, two_bias_ref, out_ref):
    for i, (w_ref, b_ref) in enumerate(((one_ref, one_bias_ref), (two_ref, two_bias_ref))):
        real, imag = w_ref[0], w_ref[1]
        top = jnp.concatenate([real, imag], axis=1)
        bottom = jnp.concatenate([-imag, real], axis=1)
        bias = jnp.concatenate([b_ref[0:1], b_ref[1:2]], axis=1)
        high = bias.astype(bf16).astype(f32)
        rows = lax.broadcasted_iota(jnp.int32, (16, 2 * BS), 0)
        tail = jnp.where(rows == 0, high, jnp.where(rows == 1, bias - high, 0.0))
        out_ref[i] = jnp.concatenate([top, bottom, tail], axis=0).astype(bf16)


def mode_kernel(own_ref, x_ref, fh_ref, fl_ref, gh_ref, gl_ref, *refs):
    w_refs, out_ref, w_all, zh, zl = refs[:NB], refs[NB], refs[NB + 1], refs[NB + 2], refs[NB + 3]
    for slot in range(NB):
        w_all[slot] = w_refs[slot][...]
    own = own_ref[0]
    x = x_ref[...]
    y = dot(fh_ref[...], x) + dot(fl_ref[...], x)

    def layer(values, slot, i):
        high, low = split(values)
        weight = w_all[slot, i, 0 : 2 * BS, :]
        bias = w_all[slot, i, 2 * BS : 2 * BS + 16, :].astype(f32)
        return dot(high, weight) + dot(low, weight) + (bias[0:1] + bias[1:2])

    outs = []
    for b in range(NB):
        slot = jnp.bitwise_xor(own, b)
        lanes = slice(BS * b, BS * b + BS)
        values = jnp.concatenate([y[:H, lanes], y[H:, lanes]], axis=1)
        first = jnp.maximum(layer(values, slot, 0), 0.0)
        second = layer(first, slot, 1)
        outs.append(second - jnp.clip(second, -shrink_level, shrink_level))
    for part in range(2):
        joined = jnp.concatenate([o[:, BS * part : BS * part + BS] for o in outs], axis=1)
        high, low = split(joined)
        zh[H * part : H * part + H, :] = high
        zl[H * part : H * part + H, :] = low
    back = dot(gh_ref[...], zh[...]) + dot(gh_ref[...], zl[...]) + dot(gl_ref[...], zh[...])
    out_ref[...] = back.astype(bf16)


def back_kernel(x_ref, th_ref, tl_ref, base_ref, gain_ref, shift_ref, bias_ref, sum_ref, norm_ref):
    gain = gain_ref[...]
    shift = shift_ref[...]
    bias = bias_ref[...]
    x = x_ref[...]
    for t in range(3):
        rows = slice(TILE * t, TILE * t + TILE)
        total = dot(th_ref[rows, :], x) + dot(tl_ref[rows, :], x) + base_ref[rows, :]
        parts = [total[:, 128 * j : 128 * j + 128] for j in range(6)]
        normed = row_norm(parts, gain, shift)
        norm_ref[rows, :] = jnp.concatenate(normed, axis=1).astype(bf16)
        for j in range(6):
            sum_ref[rows, 128 * j : 128 * j + 128] = parts[j] + bias[j : j + 1, :]


def gelu(x):
    return 0.5 * x * (1.0 + lax.erf(x * 0.7071067811865476))


def mlp_body(x_ref, acc_ref, w_refs, store):
    def tile(t, carry):
        rows = pl.ds(pl.multiple_of(t * TILE, 16), TILE)
        x = x_ref[rows, :]
        acc = acc_ref[rows, :]
        for pair in ((w_refs[0], w_refs[1]), (w_refs[2], w_refs[3])):
            w1 = jnp.concatenate([w[q, 0:BS, :] for w in pair for q in range(4)], axis=0)
            w2 = jnp.concatenate([w[q, BS : 2 * BS, :] for w in pair for q in range(4)], axis=0)
            bias = jnp.concatenate(
                [w[q, 2 * BS : 2 * BS + 16, :].astype(f32)[0:1, 0:BS] for w in pair for q in range(4)], axis=1
            )
            for c in range(3):
                span = slice(256 * c, 256 * c + 256)
                pre = lax.dot_general(x, w1[span], (((1,), (1,)), ((), ())), preferred_element_type=f32)
                hidden = gelu(pre + bias[:, span]).astype(bf16)
                acc = acc + dot(hidden, w2[span])
        store(t, rows, acc)
        return carry

    lax.fori_loop(0, 3, tile, 0)


def mlp_half(x_ref, acc_ref, w0, w1, w2, w3, out_ref):
    def store(t, rows, acc):
        out_ref[rows, :] = acc

    mlp_body(x_ref, acc_ref, (w0, w1, w2, w3), store)


def mlp_last(x_ref, acc_ref, w0, w1, w2, w3, out_ref, total):
    def store(t, rows, acc):
        total[rows, :] = acc

    mlp_body(x_ref, acc_ref, (w0, w1, w2, w3), store)
    for start in range(0, W, 240):
        n = min(240, W - start)
        for j in range(6):
            out_ref[pl.ds(6 * start + j, n, stride=6), :] = total[start : start + n, 128 * j : 128 * j + 128]


def vmem(n):
    return [pl.BlockSpec(memory_space=pltpu.VMEM)] * n


params = pltpu.CompilerParams(vmem_limit_bytes=56 * 2**20)


def place(index):
    lat, chan = divmod(index, 8)
    zh, rest = divmod(lat, 8)
    y, core = divmod(rest, 2)
    zl, x = divmod(chan, 4)
    return x, y, zh * 2 + zl, core


def index_of(x, y, z, core):
    return ((z // 2 * 4 + y) * 2 + core) * 8 + z % 2 * 4 + x


def moves(step):
    return [(d, index_of(*step(*place(d)))) for d in range(256)]


def block_moves(bits):
    return [(d, d // 8 * 8 + ((d % 8) ^ bits)) for d in range(256)]


def spread(value, axes):
    copies = jnp.broadcast_to(value[None], (8,) + value.shape)
    return lax.all_to_all(copies, axes, split_axis=0, concat_axis=0, tiled=True)


def near_moves(n):
    return moves(lambda x, y, z, c: (x, (y + n) % 4, z, c) if c == 0 else ((x + n) % 4, y, z, c))


def far_moves(n):
    return moves(lambda x, y, z, c: ((x + n) % 4, y, z, c) if c == 0 else (x, (y + n) % 4, z, c))


core_moves = moves(lambda x, y, z, c: (x, y, z, 1 - c))


def per_device(
    fields,
    first_gain,
    first_shift,
    filter_one,
    filter_one_bias,
    filter_two,
    filter_two_bias,
    second_gain,
    second_shift,
    dense_weights,
    dense_bias,
    output_bias,
):
    (lon_h, lon_l), (back_h, back_l) = lon_tables()
    (lat_h, lat_l), (tal_h, tal_l) = lat_tables()
    shape = jax.ShapeDtypeStruct

    bias_rows = jnp.pad(dense_bias.reshape(1, 1, 12), ((0, 0), (0, 1), (0, C - 12)))
    shard = jnp.concatenate([dense_weights, bias_rows], axis=0)
    stacked = spread(shard, ("zh", "zl"))

    packed = pl.pallas_call(
        pack_kernel,
        out_shape=shape((2, 2 * BS + 16, 2 * BS), bf16),
        in_specs=vmem(4),
        out_specs=vmem(1)[0],
        compiler_params=params,
        name="pack",
    )(filter_one[0], filter_one_bias[0], filter_two[0], filter_two_bias[0])
    filters = [packed] + [lax.ppermute(packed, AXES, block_moves(b)) for b in range(1, 8)]

    modes, base = pl.pallas_call(
        lon_kernel,
        out_shape=(shape((2 * KW, C), bf16), shape((ROWS, C), f32)),
        in_specs=vmem(5),
        out_specs=tuple(vmem(2)),
        scratch_shapes=[pltpu.VMEM((WP, C), bf16), pltpu.VMEM((WP, C), bf16)],
        compiler_params=params,
        name="lon",
    )(fields.reshape(6 * W, 128), first_gain.reshape(6, 128), first_shift.reshape(6, 128), lon_h, lon_l)

    rows_in = stacked[:, :12, 0, :].reshape(BS, C)
    rows_out = stacked[:, :12, 1, :].reshape(BS, C)
    bias_row = jnp.pad(stacked[:, 12, 0, :12].reshape(1, BS), ((0, 15), (0, C - BS)))
    block = jnp.concatenate([rows_in, rows_out, bias_row], axis=0)
    near = [block] + [lax.ppermute(block, AXES, near_moves(n)) for n in (1, -1, 2)]

    moved = lax.all_to_all(modes.reshape(256, 2, C), AXES, split_axis=0, concat_axis=0, tiled=True)

    group = jnp.stack(near)
    far = [group] + [lax.ppermute(group, AXES, far_moves(n)) for n in (1, -1, 2)]

    own = lax.axis_index(("zl", "x")).astype(jnp.int32).reshape(1)
    mixed = pl.pallas_call(
        mode_kernel,
        out_shape=shape((2 * H, C), bf16),
        in_specs=[pl.BlockSpec(memory_space=pltpu.SMEM)] + vmem(5 + NB),
        out_specs=vmem(1)[0],
        scratch_shapes=[
            pltpu.VMEM((NB, 2, 2 * BS + 16, 2 * BS), bf16),
            pltpu.VMEM((2 * H, C), bf16),
            pltpu.VMEM((2 * H, C), bf16),
        ],
        compiler_params=params,
        name="mode",
    )(own, moved.reshape(2 * H, C), lat_h, lat_l, tal_h, tal_l, *filters)

    returned = lax.all_to_all(mixed.reshape(256, 2, C), AXES, split_axis=0, concat_axis=0, tiled=True)
    other = [lax.ppermute(g, AXES, core_moves) for g in far]

    summed, normed = pl.pallas_call(
        back_kernel,
        out_shape=(shape((ROWS, C), f32), shape((ROWS, C), bf16)),
        in_specs=vmem(7),
        out_specs=tuple(vmem(2)),
        compiler_params=params,
        name="back",
    )(returned.reshape(2 * KW, C), back_h, back_l, base, second_gain.reshape(6, 128), second_shift.reshape(6, 128), output_bias.reshape(6, 128))

    half = pl.pallas_call(
        mlp_half,
        out_shape=shape((ROWS, C), f32),
        in_specs=vmem(6),
        out_specs=vmem(1)[0],
        compiler_params=params,
        name="mlp_half",
    )(normed, summed, *far)
    out = pl.pallas_call(
        mlp_last,
        out_shape=shape((6 * W, 128), f32),
        in_specs=vmem(6),
        out_specs=vmem(1)[0],
        scratch_shapes=[pltpu.VMEM((ROWS, C), f32)],
        compiler_params=params,
        name="mlp_last",
    )(normed, half, *other)
    return out.reshape(1, W, C)


def solution(mesh):
    fine = Mesh(mesh.devices.reshape(4, 4, 2, 2, 4), AXES)
    chan = AXES[3:]
    placed = (
        P(AXES, None, None),
        P(),
        P(),
        P(chan, None, None, None),
        P(chan, None, None),
        P(chan, None, None, None),
        P(chan, None, None),
        P(),
        P(),
        P(AXES, None, None),
        P(AXES),
        P(),
    )
    return jax.shard_map(
        per_device, mesh=fine, in_specs=placed, out_specs=P(AXES, None, None), check_vma=False
    )
```

profile of v0, /device:TPU:1, one launch (start us, length us, event | category | flops | bytes accessed | tf_op | source)
XLA Modules:
  0.0 200.2 jit_solution(2114104931758602662)
XLA Ops:
  1.7 9.0 %all-to-all-start.2 = ((bf16[8,13,2,768]{3,2,1,0:T(2,128)(2,1)}), bf16[8,13,2,768]{3,2,1,0:T(2,128)(2,1)S(1)}, u32[]{:S(2)}, u32[]{:S(2)}) async-start(bf16[8,13,2,768]{3,2,1,0:T(2,128)(2,1)} %broadcast_in_dim.2), calls=%async_computation.2 | async-start | bytes 638976 | tf_op jit(solution)/shard_map/all_to_all | solution.py:237
  10.7 7.7 %lon.1 = (bf16[512,768]{1,0:T(8,128)(2,1)}, f32[912,768]{1,0:T(8,128)}) custom-call(f32[5400,128]{1,0:T(8,128)} %bitcast.18, f32[6,128]{1,0:T(8,128)} %bitcast.27, f32[6,128]{1,0:T(8,128)} %bitcast.28, bf16[512,1024]{1,0:T(8,128)(2,1)} %constant.30.clone.th_ref, bf16[512,1024]{1,0:T(8,128)(2,1)} %constant.31.clone.tl_ref), custom_call_target="tpu_custom_call" | custom-call | tf_op jit(solution)/shard_map/lon/pallas_call | solution.py:283
  18.4 2.8 %reshape.44 = bf16[256,2,768]{2,1,0:T(2,128)(2,1)} reshape(bf16[512,768]{1,0:T(8,128)(2,1)} %get-tuple-element.9) | data formatting | bytes 1572864 | tf_op jit(solution)/shard_map/reshape | solution.py:299
  21.3 1.3 all-to-all-done.2
  22.5 12.6 %all-to-all-start = ((bf16[256,2,768]{2,1,0:T(2,128)(2,1)}), bf16[256,2,768]{2,1,0:T(2,128)(2,1)S(1)}, u32[]{:S(2)}, u32[]{:S(2)}) async-start(bf16[256,2,768]{2,1,0:T(2,128)(2,1)} %reshape.44), calls=%async_computation | async-start | bytes 1572864 | tf_op jit(solution)/shard_map/all_to_all | solution.py:299
  35.1 1.3 slice_reduce_fusion.1
  36.7 1.4 collective-permute-start.7
  38.1 1.3 collective-permute-start.8
  39.4 1.6 collective-permute-start.9
  41.1 5.5 %collective-permute-done.7 = bf16[208,768]{1,0:T(8,128)(2,1)S(1)} collective-permute-done((bf16[208,768]{1,0:T(8,128)(2,1)S(1)}, bf16[208,768]{1,0:T(8,128)(2,1)S(1)}, u32[]{:S(2)}, u32[]{:S(2)}) %collective-permute-start.7) | collective-permute-done | bytes 319520 | tf_op jit(solution)/shard_map/ppermute | solution.py:297
  46.9 7.0 %collective-permute-done.9 = bf16[208,768]{1,0:T(8,128)(2,1)S(1)} collective-permute-done((bf16[208,768]{1,0:T(8,128)(2,1)S(1)}, bf16[208,768]{1,0:T(8,128)(2,1)S(1)}, u32[]{:S(2)}, u32[]{:S(2)}) %collective-permute-start.9) | collective-permute-done | bytes 319520 | tf_op jit(solution)/shard_map/ppermute | solution.py:297
  55.1 1.7 collective-permute-start.11
  56.9 1.3 collective-permute-start.12
  58.1 1.7 pack.1.refs_0_
  59.8 1.2 collective-permute-start
  61.0 2.0 collective-permute-start.1
  63.0 4.4 %collective-permute-done.refs_1_ = bf16[2,208,192]{2,1,0:T(8,128)(2,1)S(1)} collective-permute-done((bf16[2,208,192]{2,1,0:T(8,128)(2,1)}, bf16[2,208,192]{2,1,0:T(8,128)(2,1)S(1)}, u32[]{:S(2)}, u32[]{:S(2)}) %collective-permute-start) | collective-permute-done | bytes 159776 | tf_op jit(solution)/shard_map/ppermute | solution.py:281
  67.4 2.0 collective-permute-start.2
  69.4 4.0 %collective-permute-done.1.refs_2_ = bf16[2,208,192]{2,1,0:T(8,128)(2,1)} collective-permute-done((bf16[2,208,192]{2,1,0:T(8,128)(2,1)}, bf16[2,208,192]{2,1,0:T(8,128)(2,1)}, u32[]{:S(2)}, u32[]{:S(2)}) %collective-permute-start.1) | collective-permute-done | bytes 159776 | tf_op jit(solution)/shard_map/ppermute | solution.py:281
  74.0 3.2 %collective-permute-done.2.refs_3_ = bf16[2,208,192]{2,1,0:T(8,128)(2,1)} collective-permute-done((bf16[2,208,192]{2,1,0:T(8,128)(2,1)}, bf16[2,208,192]{2,1,0:T(8,128)(2,1)}, u32[]{:S(2)}, u32[]{:S(2)}) %collective-permute-start.2) | collective-permute-done | bytes 159776 | tf_op jit(solution)/shard_map/ppermute | solution.py:281
  78.5 2.2 %collective-permute-start.5 = (bf16[2,208,192]{2,1,0:T(8,128)(2,1)}, bf16[2,208,192]{2,1,0:T(8,128)(2,1)}, u32[]{:S(2)}, u32[]{:S(2)}) collective-permute-start(bf16[2,208,192]{2,1,0:T(8,128)(2,1)} %pack.1.refs_0_), channel_id=1, source_target_pairs={{0,6},{1,7},{2,4},{3,5},{4,2},{5,3},{6,0},{7,1},{8,14},{9,15},{10,... | collective-permute-start | bytes 479240 | tf_op jit(solution)/shard_map/ppermute | solution.py:281
  80.7 2.7 %collective-permute-done.4.refs_5_ = bf16[2,208,192]{2,1,0:T(8,128)(2,1)} collective-permute-done((bf16[2,208,192]{2,1,0:T(8,128)(2,1)}, bf16[2,208,192]{2,1,0:T(8,128)(2,1)}, u32[]{:S(2)}, u32[]{:S(2)}) %collective-permute-start.4) | collective-permute-done | bytes 159776 | tf_op jit(solution)/shard_map/ppermute | solution.py:281
  83.4 2.2 %collective-permute-start.6 = (bf16[2,208,192]{2,1,0:T(8,128)(2,1)}, bf16[2,208,192]{2,1,0:T(8,128)(2,1)}, u32[]{:S(2)}, u32[]{:S(2)}) collective-permute-start(bf16[2,208,192]{2,1,0:T(8,128)(2,1)} %pack.1.refs_0_), channel_id=1, source_target_pairs={{0,7},{1,6},{2,5},{3,4},{4,3},{5,2},{6,1},{7,0},{8,15},{9,14},{10,... | collective-permute-start | bytes 479240 | tf_op jit(solution)/shard_map/ppermute | solution.py:281
  86.8 6.0 %collective-permute-done.6.refs_7_ = bf16[2,208,192]{2,1,0:T(8,128)(2,1)} collective-permute-done((bf16[2,208,192]{2,1,0:T(8,128)(2,1)}, bf16[2,208,192]{2,1,0:T(8,128)(2,1)}, u32[]{:S(2)}, u32[]{:S(2)}) %collective-permute-start.6) | collective-permute-done | bytes 159776 | tf_op jit(solution)/shard_map/ppermute | solution.py:281
  92.8 7.3 %mode.1 = bf16[512,768]{1,0:T(8,128)(2,1)} custom-call(s32[1]{0:T(128)} %bitcast.own_ref, bf16[512,768]{1,0:T(8,128)(2,1)} %reshape.45.x_ref, bf16[512,512]{1,0:T(8,128)(2,1)} %constant.32.clone.fh_ref, bf16[512,512]{1,0:T(8,128)(2,1)} %constant.33.clone.fl_ref, bf16[512,512]{1,0:T(8,128)(2,1)} %constant.34.clone.gh_ref, ...), custom_call_target="tpu_custom_call" | custom-call | tf_op jit(solution)/shard_map/mode/pallas_call | solution.py:305
  100.1 2.8 %reshape.46 = bf16[256,2,768]{2,1,0:T(2,128)(2,1)} reshape(bf16[512,768]{1,0:T(8,128)(2,1)} %mode.1) | data formatting | bytes 1572864 | tf_op jit(solution)/shard_map/reshape | solution.py:319
  103.0 41.1 %all-to-all-start.1 = ((bf16[256,2,768]{2,1,0:T(2,128)(2,1)}), bf16[256,2,768]{2,1,0:T(2,128)(2,1)S(1)}, u32[]{:S(2)}, u32[]{:S(2)}) async-start(bf16[256,2,768]{2,1,0:T(2,128)(2,1)} %reshape.46), calls=%async_computation.1 | async-start | bytes 1572864 | tf_op jit(solution)/shard_map/all_to_all | solution.py:319
  144.1 2.2 %collective-permute-start.13 = (bf16[4,208,768]{2,1,0:T(8,128)(2,1)S(1)}, bf16[4,208,768]{2,1,0:T(8,128)(2,1)}, u32[]{:S(2)}, u32[]{:S(2)}) collective-permute-start(bf16[4,208,768]{2,1,0:T(8,128)(2,1)S(1)} %pad_maximum_fusion.w0), channel_id=1, source_target_pairs={{0,8},{1,9},{2,10},{3,11},{4,12},{5,13},{6,14},{7,15},{8,0},{9,1},... | collective-permute-start | bytes 3833864 | tf_op jit(solution)/shard_map/ppermute | solution.py:320
  147.2 22.6 %all-to-all-done.1 = bf16[256,2,768]{2,1,0:T(2,128)(2,1)S(1)} async-done(((bf16[256,2,768]{2,1,0:T(2,128)(2,1)}), bf16[256,2,768]{2,1,0:T(2,128)(2,1)S(1)}, u32[]{:S(2)}, u32[]{:S(2)}) %all-to-all-start.1) | async-done | bytes 786464 | tf_op jit(solution)/shard_map/all_to_all | solution.py:319
  171.0 6.3 %back.1 = (f32[912,768]{1,0:T(8,128)}, bf16[912,768]{1,0:T(8,128)(2,1)}) custom-call(bf16[512,768]{1,0:T(8,128)(2,1)} %reshape.47.x_ref, bf16[912,512]{1,0:T(8,128)(2,1)} %constant.36.clone.th_ref, bf16[912,512]{1,0:T(8,128)(2,1)} %constant.37.clone.tl_ref, f32[912,768]{1,0:T(8,128)} %get-tuple-element.10.base_ref, f32[6,128]{1,0:T(8,128)} %bitcast.24, ...), custom_call_target="tpu_custom_call" | custom-call | tf_op jit(solution)/shard_map/back/pallas_call | solution.py:322
  177.2 11.5 %mlp_half.1.acc_ref = f32[912,768]{1,0:T(8,128)} custom-call(bf16[912,768]{1,0:T(8,128)(2,1)} %get-tuple-element.11.x_ref, f32[912,768]{1,0:T(8,128)} %get-tuple-element.12.acc_ref, bf16[4,208,768]{2,1,0:T(8,128)(2,1)} %copy-done, bf16[4,208,768]{2,1,0:T(8,128)(2,1)} %copy-done.1, bf16[4,208,768]{2,1,0:T(8,128)(2,1)} %collective-permute-done.11.w2, ...), custom_call_target="tpu_custom_call" | custom-call | tf_op jit(solution)/shard_map/mlp_half/pallas_call | solution.py:331
  188.7 11.5 %mlp_last.1 = f32[5400,128]{1,0:T(8,128)} custom-call(bf16[912,768]{1,0:T(8,128)(2,1)} %get-tuple-element.11.x_ref, f32[912,768]{1,0:T(8,128)} %mlp_half.1.acc_ref, bf16[4,208,768]{2,1,0:T(8,128)(2,1)} %collective-permute-done.13.w0, bf16[4,208,768]{2,1,0:T(8,128)(2,1)} %collective-permute-done.14.w1, bf16[4,208,768]{2,1,0:T(8,128)(2,1)} %collective-permute-done.15.w2, ...), custom_call_target="tpu_custom_call" | custom-call | tf_op jit(solution)/shard_map/mlp_last/pallas_call | solution.py:339
  (33 shorter events, 8.6 us)
Async XLA Ops:
  1.7 20.8 %all-to-all-start.2 = ((bf16[8,13,2,768]{3,2,1,0:T(2,128)(2,1)}), bf16[8,13,2,768]{3,2,1,0:T(2,128)(2,1)S(1)}, u32[]{:S(2)}, u32[]{:S(2)}) async-start(bf16[8,13,2,768]{3,2,1,0:T(2,128)(2,1)} %broadcast_in_dim.2), calls=%async_computation.2 | async-start | bytes 638976 | tf_op jit(solution)/shard_map/all_to_all | solution.py:237
  22.5 63.0 %all-to-all-start = ((bf16[256,2,768]{2,1,0:T(2,128)(2,1)}), bf16[256,2,768]{2,1,0:T(2,128)(2,1)S(1)}, u32[]{:S(2)}, u32[]{:S(2)}) async-start(bf16[256,2,768]{2,1,0:T(2,128)(2,1)} %reshape.44), calls=%async_computation | async-start | bytes 1572864 | tf_op jit(solution)/shard_map/all_to_all | solution.py:299
  36.7 9.9 %collective-permute-start.7 = (bf16[208,768]{1,0:T(8,128)(2,1)S(1)}, bf16[208,768]{1,0:T(8,128)(2,1)S(1)}, u32[]{:S(2)}, u32[]{:S(2)}) collective-permute-start(bf16[208,768]{1,0:T(8,128)(2,1)S(1)} %get-tuple-element.16), channel_id=1, source_target_pairs={{0,16},{1,17},{2,18},{3,19},{4,20},{5,21},{6,22},{7,23},{8,9},{9,1... | collective-permute-start | bytes 958472 | tf_op jit(solution)/shard_map/ppermute | solution.py:297
  38.1 8.8 %collective-permute-start.8 = (bf16[208,768]{1,0:T(8,128)(2,1)S(1)}, bf16[208,768]{1,0:T(8,128)(2,1)S(1)}, u32[]{:S(2)}, u32[]{:S(2)}) collective-permute-start(bf16[208,768]{1,0:T(8,128)(2,1)S(1)} %get-tuple-element.16), channel_id=1, source_target_pairs={{0,48},{1,49},{2,50},{3,51},{4,52},{5,53},{6,54},{7,55},{8,11},{9,... | collective-permute-start | bytes 958472 | tf_op jit(solution)/shard_map/ppermute | solution.py:297
  39.4 14.5 %collective-permute-start.9 = (bf16[208,768]{1,0:T(8,128)(2,1)S(1)}, bf16[208,768]{1,0:T(8,128)(2,1)S(1)}, u32[]{:S(2)}, u32[]{:S(2)}) collective-permute-start(bf16[208,768]{1,0:T(8,128)(2,1)S(1)} %get-tuple-element.16), channel_id=1, source_target_pairs={{0,32},{1,33},{2,34},{3,35},{4,36},{5,37},{6,38},{7,39},{8,10},{9,... | collective-permute-start | bytes 958472 | tf_op jit(solution)/shard_map/ppermute | solution.py:297
  54.1 90.0 %copy-start = (bf16[4,208,768]{2,1,0:T(8,128)(2,1)}, bf16[4,208,768]{2,1,0:T(8,128)(2,1)S(1)}, u32[]{:S(2)}) copy-start(bf16[4,208,768]{2,1,0:T(8,128)(2,1)S(1)} %pad_maximum_fusion.w0) | copy-start | bytes 3833860
  54.1 92.3 %collective-permute-start.10 = (bf16[4,208,768]{2,1,0:T(8,128)(2,1)S(1)}, bf16[4,208,768]{2,1,0:T(8,128)(2,1)S(1)}, u32[]{:S(2)}, u32[]{:S(2)}) collective-permute-start(bf16[4,208,768]{2,1,0:T(8,128)(2,1)S(1)} %pad_maximum_fusion.w0), channel_id=1, source_target_pairs={{0,1},{1,2},{2,3},{3,0},{4,5},{5,6},{6,7},{7,4},{8,24},{9,25},{10,... | collective-permute-start | bytes 3833864 | tf_op jit(solution)/shard_map/ppermute | solution.py:302
  55.1 91.3 %collective-permute-start.11 = (bf16[4,208,768]{2,1,0:T(8,128)(2,1)S(1)}, bf16[4,208,768]{2,1,0:T(8,128)(2,1)}, u32[]{:S(2)}, u32[]{:S(2)}) collective-permute-start(bf16[4,208,768]{2,1,0:T(8,128)(2,1)S(1)} %pad_maximum_fusion.w0), channel_id=1, source_target_pairs={{0,3},{1,0},{2,1},{3,2},{4,7},{5,4},{6,5},{7,6},{8,56},{9,57},{10,... | collective-permute-start | bytes 3833864 | tf_op jit(solution)/shard_map/ppermute | solution.py:302
  56.9 90.0 %collective-permute-start.12 = (bf16[4,208,768]{2,1,0:T(8,128)(2,1)S(1)}, bf16[4,208,768]{2,1,0:T(8,128)(2,1)}, u32[]{:S(2)}, u32[]{:S(2)}) collective-permute-start(bf16[4,208,768]{2,1,0:T(8,128)(2,1)S(1)} %pad_maximum_fusion.w0), channel_id=1, source_target_pairs={{0,2},{1,3},{2,0},{3,1},{4,6},{5,7},{6,4},{7,5},{8,40},{9,41},{10,... | collective-permute-start | bytes 3833864 | tf_op jit(solution)/shard_map/ppermute | solution.py:302
  59.8 7.6 %collective-permute-start = (bf16[2,208,192]{2,1,0:T(8,128)(2,1)}, bf16[2,208,192]{2,1,0:T(8,128)(2,1)S(1)}, u32[]{:S(2)}, u32[]{:S(2)}) collective-permute-start(bf16[2,208,192]{2,1,0:T(8,128)(2,1)} %pack.1.refs_0_), channel_id=1, source_target_pairs={{0,1},{1,0},{2,3},{3,2},{4,5},{5,4},{6,7},{7,6},{8,9},{9,8},{10,11... | collective-permute-start | bytes 479240 | tf_op jit(solution)/shard_map/ppermute | solution.py:281
  61.0 12.4 %collective-permute-start.1 = (bf16[2,208,192]{2,1,0:T(8,128)(2,1)}, bf16[2,208,192]{2,1,0:T(8,128)(2,1)}, u32[]{:S(2)}, u32[]{:S(2)}) collective-permute-start(bf16[2,208,192]{2,1,0:T(8,128)(2,1)} %pack.1.refs_0_), channel_id=1, source_target_pairs={{0,2},{1,3},{2,0},{3,1},{4,6},{5,7},{6,4},{7,5},{8,10},{9,11},{10,... | collective-permute-start | bytes 479240 | tf_op jit(solution)/shard_map/ppermute | solution.py:281
  67.4 25.4 %copy-start.2 = (bf16[2,208,192]{2,1,0:T(8,128)(2,1)}, bf16[2,208,192]{2,1,0:T(8,128)(2,1)S(1)}, u32[]{:S(2)}) copy-start(bf16[2,208,192]{2,1,0:T(8,128)(2,1)S(1)} %collective-permute-done.refs_1_) | copy-start | bytes 479236
  67.4 9.7 %collective-permute-start.2 = (bf16[2,208,192]{2,1,0:T(8,128)(2,1)}, bf16[2,208,192]{2,1,0:T(8,128)(2,1)}, u32[]{:S(2)}, u32[]{:S(2)}) collective-permute-start(bf16[2,208,192]{2,1,0:T(8,128)(2,1)} %pack.1.refs_0_), channel_id=1, source_target_pairs={{0,3},{1,2},{2,1},{3,0},{4,7},{5,6},{6,5},{7,4},{8,11},{9,10},{10,... | collective-permute-start | bytes 479240 | tf_op jit(solution)/shard_map/ppermute | solution.py:281
  73.4 5.1 %collective-permute-start.3 = (bf16[2,208,192]{2,1,0:T(8,128)(2,1)}, bf16[2,208,192]{2,1,0:T(8,128)(2,1)}, u32[]{:S(2)}, u32[]{:S(2)}) collective-permute-start(bf16[2,208,192]{2,1,0:T(8,128)(2,1)} %pack.1.refs_0_), channel_id=1, source_target_pairs={{0,4},{1,5},{2,6},{3,7},{4,0},{5,1},{6,2},{7,3},{8,12},{9,13},{10,... | collective-permute-start | bytes 479240 | tf_op jit(solution)/shard_map/ppermute | solution.py:281
  77.1 6.3 %collective-permute-start.4 = (bf16[2,208,192]{2,1,0:T(8,128)(2,1)}, bf16[2,208,192]{2,1,0:T(8,128)(2,1)}, u32[]{:S(2)}, u32[]{:S(2)}) collective-permute-start(bf16[2,208,192]{2,1,0:T(8,128)(2,1)} %pack.1.refs_0_), channel_id=1, source_target_pairs={{0,5},{1,4},{2,7},{3,6},{4,1},{5,0},{6,3},{7,2},{8,13},{9,12},{10,... | collective-permute-start | bytes 479240 | tf_op jit(solution)/shard_map/ppermute | solution.py:281
  78.5 8.3 %collective-permute-start.5 = (bf16[2,208,192]{2,1,0:T(8,128)(2,1)}, bf16[2,208,192]{2,1,0:T(8,128)(2,1)}, u32[]{:S(2)}, u32[]{:S(2)}) collective-permute-start(bf16[2,208,192]{2,1,0:T(8,128)(2,1)} %pack.1.refs_0_), channel_id=1, source_target_pairs={{0,6},{1,7},{2,4},{3,5},{4,2},{5,3},{6,0},{7,1},{8,14},{9,15},{10,... | collective-permute-start | bytes 479240 | tf_op jit(solution)/shard_map/ppermute | solution.py:281
  83.4 9.4 %collective-permute-start.6 = (bf16[2,208,192]{2,1,0:T(8,128)(2,1)}, bf16[2,208,192]{2,1,0:T(8,128)(2,1)}, u32[]{:S(2)}, u32[]{:S(2)}) collective-permute-start(bf16[2,208,192]{2,1,0:T(8,128)(2,1)} %pack.1.refs_0_), channel_id=1, source_target_pairs={{0,7},{1,6},{2,5},{3,4},{4,3},{5,2},{6,1},{7,0},{8,15},{9,14},{10,... | collective-permute-start | bytes 479240 | tf_op jit(solution)/shard_map/ppermute | solution.py:281
  103.0 66.8 %all-to-all-start.1 = ((bf16[256,2,768]{2,1,0:T(2,128)(2,1)}), bf16[256,2,768]{2,1,0:T(2,128)(2,1)S(1)}, u32[]{:S(2)}, u32[]{:S(2)}) async-start(bf16[256,2,768]{2,1,0:T(2,128)(2,1)} %reshape.46), calls=%async_computation.1 | async-start | bytes 1572864 | tf_op jit(solution)/shard_map/all_to_all | solution.py:319
  144.1 44.6 %collective-permute-start.13 = (bf16[4,208,768]{2,1,0:T(8,128)(2,1)S(1)}, bf16[4,208,768]{2,1,0:T(8,128)(2,1)}, u32[]{:S(2)}, u32[]{:S(2)}) collective-permute-start(bf16[4,208,768]{2,1,0:T(8,128)(2,1)S(1)} %pad_maximum_fusion.w0), channel_id=1, source_target_pairs={{0,8},{1,9},{2,10},{3,11},{4,12},{5,13},{6,14},{7,15},{8,0},{9,1},... | collective-permute-start | bytes 3833864 | tf_op jit(solution)/shard_map/ppermute | solution.py:320
  146.3 30.9 %copy-start.1 = (bf16[4,208,768]{2,1,0:T(8,128)(2,1)}, bf16[4,208,768]{2,1,0:T(8,128)(2,1)S(1)}, u32[]{:S(2)}) copy-start(bf16[4,208,768]{2,1,0:T(8,128)(2,1)S(1)} %collective-permute-done.10.w1) | copy-start | bytes 3833860
  146.3 42.3 %collective-permute-start.14 = (bf16[4,208,768]{2,1,0:T(8,128)(2,1)S(1)}, bf16[4,208,768]{2,1,0:T(8,128)(2,1)}, u32[]{:S(2)}, u32[]{:S(2)}) collective-permute-start(bf16[4,208,768]{2,1,0:T(8,128)(2,1)S(1)} %collective-permute-done.10.w1), channel_id=1, source_target_pairs={{0,8},{1,9},{2,10},{3,11},{4,12},{5,13},{6,14},{7,15},{8,0},{9,1},... | collective-permute-start | bytes 3833864 | tf_op jit(solution)/shard_map/ppermute | solution.py:320
  146.5 42.2 %collective-permute-start.15 = (bf16[4,208,768]{2,1,0:T(8,128)(2,1)}, bf16[4,208,768]{2,1,0:T(8,128)(2,1)}, u32[]{:S(2)}, u32[]{:S(2)}) collective-permute-start(bf16[4,208,768]{2,1,0:T(8,128)(2,1)} %collective-permute-done.11.w2), channel_id=1, source_target_pairs={{0,8},{1,9},{2,10},{3,11},{4,12},{5,13},{6,14},{7,15},{8,0},{9,1},... | collective-permute-start | bytes 3833864 | tf_op jit(solution)/shard_map/ppermute | solution.py:320
  146.9 41.8 %collective-permute-start.16 = (bf16[4,208,768]{2,1,0:T(8,128)(2,1)}, bf16[4,208,768]{2,1,0:T(8,128)(2,1)}, u32[]{:S(2)}, u32[]{:S(2)}) collective-permute-start(bf16[4,208,768]{2,1,0:T(8,128)(2,1)} %collective-permute-done.12.w3), channel_id=1, source_target_pairs={{0,8},{1,9},{2,10},{3,11},{4,12},{5,13},{6,14},{7,15},{8,0},{9,1},... | collective-permute-start | bytes 3833864 | tf_op jit(solution)/shard_map/ppermute | solution.py:320
where the time goes:
time: 201 us; the launch traced here: 200 us
  starting transfers between devices  84.5 us (42%)
  waiting for transfers between devices  58.2 us (29%)
  Pallas kernels  46 us (23%)
  local copies, waits for them, and re-layouts  10.4 us (5%)
    all_to_all x1, starting transfers between devices, per_device(): lax.all_to_all(mixed.reshape(256, 2, C), AXES, split_axis=0, concat_axis=...  41.1 us
    all_to_all x1, waiting for transfers between devices, per_device(): lax.all_to_all(mixed.reshape(256, 2, C), AXES, split_axis=0, concat_axis=...  22.6 us
    ppermute x7, waiting for transfers between devices, per_device(): lax.ppermute(packed, AXES, block_moves(b))  21.5 us
    ppermute x3, waiting for transfers between devices, per_device(): lax.ppermute(block, AXES, near_moves(n))  12.9 us
    all_to_all x1, starting transfers between devices, per_device(): lax.all_to_all(modes.reshape(256, 2, C), AXES, split_axis=0, concat_axis=...  12.6 us
    pallas_call x1, Pallas kernels, per_device(): pl.pallas_call(mlp_last, out_shape=shape((6 * W, 128), f32), in_specs=vme...  11.5 us
    pallas_call x1, Pallas kernels, per_device(): pl.pallas_call(mlp_half, out_shape=shape((ROWS, C), f32), in_specs=vmem(6...  11.5 us
    ppermute x7, starting transfers between devices, per_device(): lax.ppermute(packed, AXES, block_moves(b))  10.3 us
  transfers between devices with their start and end apart: 20, of which 11 were waited for; matrix products, arithmetic and copies ran while one was open for 5% of the time, Pallas kernels for 17%

commit v1 on v0

v1 whole, which is shorter than its diff:
```python
import functools

import jax
import jax.numpy as jnp
import numpy as np
from jax import lax
from jax.experimental import pallas as pl
from jax.experimental.pallas import tpu as pltpu
from jax.sharding import Mesh
from jax.sharding import PartitionSpec as P


W = 900
WP = 1024
KW = 256
H = 256
C = 768
BS = 96
NB = 8
TILE = 304
ROWS = 3 * TILE
norm_eps = 1e-05
shrink_level = 0.01
AXES = ("zh", "y", "co", "zl", "x")
bf16 = jnp.bfloat16
f32 = jnp.float32


def split_table(values):
    high = values.astype(np.float32).astype(jnp.bfloat16)
    low = (values - high.astype(np.float64)).astype(np.float32).astype(jnp.bfloat16)
    return high, low


def lon_tables():
    k = np.arange(KW)[:, None]
    w = np.arange(W)[None, :]
    angle = 2 * np.pi * (k * w % W) / W
    forward = np.zeros((KW, 2, WP))
    forward[:, 0, :W] = np.cos(angle)
    forward[:, 1, :W] = -np.sin(angle)
    forward = forward.reshape(2 * KW, WP) * W**-0.5
    factor = np.where(k == 0, 1.0, 2.0)
    backward = np.zeros((ROWS, KW, 2))
    backward[:W, :, 0] = (np.cos(angle) * factor).T
    backward[:W, :, 1] = (-np.sin(angle) * factor).T
    backward = backward.reshape(ROWS, 2 * KW) * W**-0.5
    return split_table(forward), split_table(backward)


def lat_tables():
    m = np.arange(H)[:, None]
    h = np.arange(H)[None, :]
    angle = 2 * np.pi * (m * h % H) / H
    cos, sin = np.cos(angle), np.sin(angle)
    forward = np.zeros((2, H, H, 2))
    forward[0, :, :, 0] = cos
    forward[0, :, :, 1] = sin
    forward[1, :, :, 0] = -sin
    forward[1, :, :, 1] = cos
    forward = forward.reshape(2 * H, 2 * H) * H**-0.5
    return split_table(forward), split_table(forward.T)


def dot(a, b):
    return jnp.dot(a, b, preferred_element_type=f32)


def split(x):
    high = x.astype(bf16)
    return high, (x - high.astype(f32)).astype(bf16)


def row_norm(parts, gain, shift):
    count = len(parts) * 128
    mean = jnp.sum(functools.reduce(jnp.add, parts), axis=-1, keepdims=True) / count
    centered = [p - mean for p in parts]
    square = functools.reduce(jnp.add, [c * c for c in centered])
    scale = lax.rsqrt(jnp.sum(square, axis=-1, keepdims=True) / count + norm_eps)
    return [
        c * scale * gain[j : j + 1, :] + shift[j : j + 1, :]
        for j, c in enumerate(centered)
    ]


def start(copies):
    for copy in copies:
        copy.start()


def lon_kernel(x_hbm, gain_ref, shift_ref, th_hbm, tl_hbm, modes_ref, base_hbm, x_ref, th, tl, base, zh, zl, sem, out_sem):
    spans = [(r, min(240, W - r)) for r in range(0, W, 240)]
    loads = [
        pltpu.make_async_copy(x_hbm.at[pl.ds(6 * r, 6 * n)], x_ref.at[pl.ds(6 * r, 6 * n)], sem.at[i])
        for i, (r, n) in enumerate(spans)
    ]
    tables = [pltpu.make_async_copy(th_hbm, th, sem.at[4]), pltpu.make_async_copy(tl_hbm, tl, sem.at[5])]
    start(loads + tables)
    gain = gain_ref[...]
    shift = shift_ref[...]
    stores = []
    for i, (r, n) in enumerate(spans):
        loads[i].wait()
        parts = [x_ref[pl.ds(6 * r + j, n, stride=6), :] for j in range(6)]
        normed = row_norm(parts, gain, shift)
        for j in range(6):
            lanes = slice(128 * j, 128 * j + 128)
            base[r : r + n, lanes] = normed[j] + parts[j]
            high, low = split(normed[j])
            zh[r : r + n, lanes] = high
            zl[r : r + n, lanes] = low
        if r + n == W:
            base[W:ROWS, :] = jnp.zeros((ROWS - W, C), f32)
            n = ROWS - r
        stores.append(pltpu.make_async_copy(base.at[pl.ds(r, n)], base_hbm.at[pl.ds(r, n)], out_sem.at[i]))
        stores[-1].start()
    zh[W:WP, :] = jnp.zeros((WP - W, C), bf16)
    zl[W:WP, :] = jnp.zeros((WP - W, C), bf16)
    tables[0].wait()
    modes = dot(th[...], zh[...]) + dot(th[...], zl[...])
    tables[1].wait()
    modes = modes + dot(tl[...], zh[...])
    modes_ref[...] = modes.astype(bf16).reshape(KW, 2, C)
    for copy in stores:
        copy.wait()


def pack_kernel(one_ref, one_bias_ref, two_ref, two_bias_ref, out_ref):
    for i, (w_ref, b_ref) in enumerate(((one_ref, one_bias_ref), (two_ref, two_bias_ref))):
        top = jnp.concatenate([w_ref[0], w_ref[1]], axis=1)
        bias = jnp.concatenate([b_ref[0:1], b_ref[1:2]], axis=1)
        high = bias.astype(bf16).astype(f32)
        rows = lax.broadcasted_iota(jnp.int32, (16, 2 * BS), 0)
        tail = jnp.where(rows == 0, high, jnp.where(rows == 1, bias - high, 0.0))
        out_ref[i] = jnp.concatenate([top, tail], axis=0).astype(bf16)


def mode_kernel(own_ref, x_hbm, fh_hbm, fl_hbm, gh_hbm, gl_hbm, w0, w1, w2, w3, out_ref, x_ref, fh, fl, gh, gl, w_all, zh, zl, sem):
    pairs = [(x_hbm, x_ref), (fh_hbm, fh), (fl_hbm, fl)] + [(w, w_all.at[d]) for d, w in enumerate((w0, w1, w2, w3))]
    pairs += [(gh_hbm, gh), (gl_hbm, gl)]
    copies = [pltpu.make_async_copy(source, target, sem.at[i]) for i, (source, target) in enumerate(pairs)]
    start(copies)
    own = own_ref[0]
    copies[0].wait()
    copies[1].wait()
    x = x_ref[...].reshape(2 * H, C)
    y = dot(fh[...], x)
    copies[2].wait()
    y = y + dot(fl[...], x)
    for copy in copies[3:7]:
        copy.wait()

    def layer(values, slot, i):
        high, low = split(values)
        packed = w_all[jnp.bitwise_and(slot, 3), lax.shift_right_logical(slot, 2), i]
        top = packed[0:BS]
        bottom = jnp.concatenate([-top[:, BS:], top[:, :BS]], axis=1)
        weight = jnp.concatenate([top, bottom], axis=0)
        bias = packed[BS : BS + 16].astype(f32)
        return dot(high, weight) + dot(low, weight) + (bias[0:1] + bias[1:2])

    outs = []
    for b in range(NB):
        slot = jnp.bitwise_xor(own, b)
        lanes = slice(BS * b, BS * b + BS)
        values = jnp.concatenate([y[:H, lanes], y[H:, lanes]], axis=1)
        first = jnp.maximum(layer(values, slot, 0), 0.0)
        second = layer(first, slot, 1)
        outs.append(second - jnp.clip(second, -shrink_level, shrink_level))
    for part in range(2):
        joined = jnp.concatenate([o[:, BS * part : BS * part + BS] for o in outs], axis=1)
        high, low = split(joined)
        zh[H * part : H * part + H, :] = high
        zl[H * part : H * part + H, :] = low
    copies[7].wait()
    back = dot(gh[...], zh[...]) + dot(gh[...], zl[...])
    copies[8].wait()
    back = back + dot(gl[...], zh[...])
    out_ref[...] = back.astype(bf16).reshape(H, 2, C)


def gelu(x):
    return 0.5 * x * (1.0 + lax.erf(x * 0.7071067811865476))


def tail_kernel(x_hbm, th_hbm, tl_hbm, base_hbm, gain_ref, shift_ref, bias_ref, *refs):
    w_hbm, out_hbm = refs[:8], refs[8]
    x_ref, th, tl, base, weights, normed, result, sem, w_sem, out_sem = refs[9:]
    pairs = [(x_hbm, x_ref), (th_hbm, th), (tl_hbm, tl), (base_hbm, base)]
    copies = [pltpu.make_async_copy(source, target, sem.at[i]) for i, (source, target) in enumerate(pairs)]
    w_copies = [pltpu.make_async_copy(w, weights.at[pl.ds(4 * i, 4)], w_sem.at[i]) for i, w in enumerate(w_hbm)]
    start(copies + w_copies)
    gain = gain_ref[...]
    shift = shift_ref[...]
    out_bias = bias_ref[...]
    for copy in copies:
        copy.wait()
    x = x_ref[...].reshape(2 * KW, C)
    for t in range(3):
        rows = slice(TILE * t, TILE * t + TILE)
        total = dot(th[rows, :], x) + dot(tl[rows, :], x) + base[rows, :]
        parts = [total[:, 128 * j : 128 * j + 128] for j in range(6)]
        normed[rows, :] = jnp.concatenate(row_norm(parts, gain, shift), axis=1).astype(bf16)
        for j in range(6):
            base[rows, 128 * j : 128 * j + 128] = parts[j] + out_bias[j : j + 1, :]
    for copy in w_copies:
        copy.wait()

    def out_copy(t, n):
        span = pl.ds(6 * TILE * t, 6 * n)
        return pltpu.make_async_copy(result.at[span], out_hbm.at[span], out_sem.at[t])

    def tile(t, carry):
        rows = pl.ds(pl.multiple_of(t * TILE, 16), TILE)
        tokens = normed[rows, :]
        acc = base[rows, :]
        for first in range(0, 32, 8):
            w1 = jnp.concatenate([weights[q, 0:BS, :] for q in range(first, first + 8)], axis=0)
            w2 = jnp.concatenate([weights[q, BS : 2 * BS, :] for q in range(first, first + 8)], axis=0)
            bias = jnp.concatenate(
                [weights[q, 2 * BS : 2 * BS + 16, :].astype(f32)[0:1, 0:BS] for q in range(first, first + 8)], axis=1
            )
            for c in range(3):
                span = slice(256 * c, 256 * c + 256)
                pre = lax.dot_general(tokens, w1[span], (((1,), (1,)), ((), ())), preferred_element_type=f32)
                hidden = gelu(pre + bias[:, span]).astype(bf16)
                acc = acc + dot(hidden, w2[span])
        for j in range(6):
            result[pl.ds(6 * TILE * t + j, TILE, stride=6), :] = acc[:, 128 * j : 128 * j + 128]

        @pl.when(t < 2)
        def _():
            out_copy(t, TILE).start()

        return carry

    lax.fori_loop(0, 3, tile, 0)
    last = out_copy(2, W - 2 * TILE)
    last.start()
    out_copy(0, TILE).wait()
    out_copy(1, TILE).wait()
    last.wait()


def vmem(n):
    return [pl.BlockSpec(memory_space=pltpu.VMEM)] * n


def anywhere(n):
    return [pl.BlockSpec(memory_space=pl.ANY)] * n


params = pltpu.CompilerParams(vmem_limit_bytes=56 * 2**20)


def place(index):
    lat, chan = divmod(index, 8)
    zh, rest = divmod(lat, 8)
    y, core = divmod(rest, 2)
    zl, x = divmod(chan, 4)
    return x, y, zh * 2 + zl, core


def index_of(x, y, z, core):
    return ((z // 2 * 4 + y) * 2 + core) * 8 + z % 2 * 4 + x


def moves(step):
    return [(d, index_of(*step(*place(d)))) for d in range(256)]


def block_moves(bits):
    return [(d, d ^ bits) for d in range(256)]


def spread(value, axes):
    copies = jnp.broadcast_to(value[None], (8,) + value.shape)
    return lax.all_to_all(copies, axes, split_axis=0, concat_axis=0, tiled=True)


def near_moves(n):
    return moves(lambda x, y, z, c: (x, (y + n) % 4, z, c) if c == 0 else ((x + n) % 4, y, z, c))


def far_moves(n):
    return moves(lambda x, y, z, c: ((x + n) % 4, y, z, c) if c == 0 else (x, (y + n) % 4, z, c))


core_moves = moves(lambda x, y, z, c: (x, y, z, 1 - c))


def per_device(
    fields,
    first_gain,
    first_shift,
    filter_one,
    filter_one_bias,
    filter_two,
    filter_two_bias,
    second_gain,
    second_shift,
    dense_weights,
    dense_bias,
    output_bias,
):
    (lon_h, lon_l), (back_h, back_l) = lon_tables()
    (lat_h, lat_l), (tal_h, tal_l) = lat_tables()
    shape = jax.ShapeDtypeStruct

    bias_rows = jnp.pad(dense_bias.reshape(1, 1, 12), ((0, 0), (0, 1), (0, C - 12)))
    shard = jnp.concatenate([dense_weights, bias_rows], axis=0)
    stacked = spread(shard, ("zh", "zl"))

    packed = pl.pallas_call(
        pack_kernel,
        out_shape=shape((2, BS + 16, 2 * BS), bf16),
        in_specs=vmem(4),
        out_specs=vmem(1)[0],
        compiler_params=params,
        name="pack",
    )(filter_one[0], filter_one_bias[0], filter_two[0], filter_two_bias[0])
    partner = lax.ppermute(packed, AXES, block_moves(4))

    modes, base = pl.pallas_call(
        lon_kernel,
        out_shape=(shape((KW, 2, C), bf16), shape((ROWS, C), f32)),
        in_specs=anywhere(1) + vmem(2) + anywhere(2),
        out_specs=(vmem(1)[0], anywhere(1)[0]),
        scratch_shapes=[
            pltpu.VMEM((6 * W, 128), f32),
            pltpu.VMEM((2 * KW, WP), bf16),
            pltpu.VMEM((2 * KW, WP), bf16),
            pltpu.VMEM((ROWS, C), f32),
            pltpu.VMEM((WP, C), bf16),
            pltpu.VMEM((WP, C), bf16),
            pltpu.SemaphoreType.DMA((6,)),
            pltpu.SemaphoreType.DMA((4,)),
        ],
        compiler_params=params,
        name="lon",
    )(fields.reshape(6 * W, 128), first_gain.reshape(6, 128), first_shift.reshape(6, 128), lon_h, lon_l)

    pair = jnp.stack([packed, partner])
    filters = [pair] + [lax.ppermute(pair, AXES, block_moves(b)) for b in range(1, 4)]

    rows_in = stacked[:, :12, 0, :].reshape(BS, C)
    rows_out = stacked[:, :12, 1, :].reshape(BS, C)
    bias_row = jnp.pad(stacked[:, 12, 0, :12].reshape(1, BS), ((0, 15), (0, C - BS)))
    block = jnp.concatenate([rows_in, rows_out, bias_row], axis=0)
    near = [block] + [lax.ppermute(block, AXES, near_moves(n)) for n in (1, -1, 2)]

    moved = lax.all_to_all(modes, AXES, split_axis=0, concat_axis=0, tiled=True)

    group = jnp.stack(near)
    far = [group] + [lax.ppermute(group, AXES, far_moves(n)) for n in (1, -1, 2)]

    own = lax.axis_index(("zl", "x")).astype(jnp.int32).reshape(1)
    mixed = pl.pallas_call(
        mode_kernel,
        out_shape=shape((H, 2, C), bf16),
        in_specs=[pl.BlockSpec(memory_space=pltpu.SMEM)] + anywhere(9),
        out_specs=vmem(1)[0],
        scratch_shapes=[pltpu.VMEM((H, 2, C), bf16)]
        + [pltpu.VMEM((2 * H, 2 * H), bf16)] * 4
        + [
            pltpu.VMEM((4, 2, 2, BS + 16, 2 * BS), bf16),
            pltpu.VMEM((2 * H, C), bf16),
            pltpu.VMEM((2 * H, C), bf16),
            pltpu.SemaphoreType.DMA((9,)),
        ],
        compiler_params=params,
        name="mode",
    )(own, moved, lat_h, lat_l, tal_h, tal_l, *filters)

    returned = lax.all_to_all(mixed, AXES, split_axis=0, concat_axis=0, tiled=True)
    other = [lax.ppermute(g, AXES, core_moves) for g in far]

    out = pl.pallas_call(
        tail_kernel,
        out_shape=shape((6 * W, 128), f32),
        in_specs=anywhere(4) + vmem(3) + anywhere(8),
        out_specs=anywhere(1)[0],
        scratch_shapes=[
            pltpu.VMEM((KW, 2, C), bf16),
            pltpu.VMEM((ROWS, 2 * KW), bf16),
            pltpu.VMEM((ROWS, 2 * KW), bf16),
            pltpu.VMEM((ROWS, C), f32),
            pltpu.VMEM((32, 2 * BS + 16, C), bf16),
            pltpu.VMEM((ROWS, C), bf16),
            pltpu.VMEM((6 * ROWS, 128), f32),
            pltpu.SemaphoreType.DMA((4,)),
            pltpu.SemaphoreType.DMA((8,)),
            pltpu.SemaphoreType.DMA((3,)),
        ],
        compiler_params=params,
        name="tail",
    )(
        returned,
        back_h,
        back_l,
        base,
        second_gain.reshape(6, 128),
        second_shift.reshape(6, 128),
        output_bias.reshape(6, 128),
        *far,
        *other,
    )
    return out.reshape(1, W, C)


def solution(mesh):
    fine = Mesh(mesh.devices.reshape(4, 4, 2, 2, 4), AXES)
    chan = AXES[3:]
    placed = (
        P(AXES, None, None),
        P(),
        P(),
        P(chan, None, None, None),
        P(chan, None, None),
        P(chan, None, None, None),
        P(chan, None, None),
        P(),
        P(),
        P(AXES, None, None),
        P(AXES),
        P(),
    )
    return jax.shard_map(
        per_device, mesh=fine, in_specs=placed, out_specs=P(AXES, None, None), check_vma=False
    )
```

time: 201 us -> 168 us (0.84)
  starting transfers between devices: 84.5 us -> 57.4 us
  Pallas kernels: 46 us -> 36.1 us
  waiting for transfers between devices: 58.2 us -> 66.8 us
  local copies, waits for them, and re-layouts: 10.4 us -> 4.12 us
    all_to_all x2, starting transfers between devices: 53.7 us -> 34.5 us  [the longest x1 24.7 us: per_device(): lax.all_to_all(mixed, AXES, split_axis=0, concat_axis=0, tiled=True)]
    pallas_call x6 -> x4, Pallas kernels: 46 us -> 36.1 us  [the longest x1 19.4 us: per_device(): pl.pallas_call(tail_kernel, out_shape=shape((6 * W, 128), f32), in_specs=...]
    reshape x4 -> x0, local copies, waits for them, and re-layouts: 8.05 us -> none  [the longest x1 2.84 us: per_device(): mixed.reshape(256, 2, C)]
    ppermute x7 -> x4, starting transfers between devices: 10.3 us -> 2.33 us  [the longest x3 1.55 us: per_device(): lax.ppermute(pair, AXES, block_moves(b))]
    ppermute x7 -> x4, waiting for transfers between devices: 21.5 us -> 25.4 us  [the longest x3 21.9 us: per_device(): lax.ppermute(pair, AXES, block_moves(b))]
    all_to_all x1, waiting for transfers between devices: 1.28 us -> 4.2 us  [spread(): return lax.all_to_all(copies, axes, split_axis=0, concat_axis=0, tiled=True)]
  transfers between devices with their start and end apart: 20 -> 17, of which waited for: 11 -> 8; matrix products, arithmetic and copies ran while one was open for 5% -> 2% of each run, Pallas kernels for 17% -> 10%
where the time goes in v1:
time: 168 us; the launch traced here: 167 us
  waiting for transfers between devices  66.8 us (40%)
  starting transfers between devices  57.4 us (34%)
  Pallas kernels  36.1 us (21%)
  local copies, waits for them, and re-layouts  4.12 us (2%)
  other arithmetic  2.65 us (2%)
    all_to_all x1, starting transfers between devices, per_device(): lax.all_to_all(mixed, AXES, split_axis=0, concat_axis=0, tiled=True)  24.7 us
    ppermute x3, waiting for transfers between devices, per_device(): lax.ppermute(pair, AXES, block_moves(b))  21.9 us
    all_to_all x1, waiting for transfers between devices, per_device(): lax.all_to_all(mixed, AXES, split_axis=0, concat_axis=0, tiled=True)  20.7 us
    pallas_call x1, Pallas kernels, per_device(): pl.pallas_call(tail_kernel, out_shape=shape((6 * W, 128), f32), in_specs=...  19.4 us
    ppermute x3, waiting for transfers between devices, per_device(): lax.ppermute(block, AXES, near_moves(n))  14.5 us
    all_to_all x1, starting transfers between devices, per_device(): moved = lax.all_to_all(modes, AXES, split_axis=0, concat_axis=0, tiled=True)  9.77 us
    all_to_all x1, starting transfers between devices, spread(): return lax.all_to_all(copies, axes, split_axis=0, concat_axis=0, tiled=True)  9 us
    pallas_call x1, Pallas kernels, per_device(): pl.pallas_call(lon_kernel, out_shape=(shape((KW, 2, C), bf16), shape((ROW...  7.61 us
  transfers between devices with their start and end apart: 17, of which 8 were waited for; matrix products, arithmetic and copies ran while one was open for 2% of the time, Pallas kernels for 10%

profile of v1, /device:TPU:1, one launch (start us, length us, event | category | flops | bytes accessed | tf_op | source)
XLA Modules:
  0.0 167.3 jit_solution(10216676301797516617)
XLA Ops:
  0.0 0.8 fusion.2
  0.8 0.9 broadcast_in_dim.2
  1.7 9.0 %all-to-all-start.2 = ((bf16[8,13,2,768]{3,2,1,0:T(2,128)(2,1)}), bf16[8,13,2,768]{3,2,1,0:T(2,128)(2,1)S(1)}, u32[]{:S(2)}, u32[]{:S(2)}) async-start(bf16[8,13,2,768]{3,2,1,0:T(2,128)(2,1)} %broadcast_in_dim.2), calls=%async_computation.2 | async-start | bytes 638976 | tf_op jit(solution)/shard_map/all_to_all | solution.py:278
  10.7 7.6 %lon.1 = (bf16[256,2,768]{2,1,0:T(2,128)(2,1)}, f32[912,768]{1,0:T(8,128)}) custom-call(f32[5400,128]{1,0:T(8,128)} %bitcast.20, f32[6,128]{1,0:T(8,128)} %bitcast.28, f32[6,128]{1,0:T(8,128)} %bitcast.29, bf16[512,1024]{1,0:T(8,128)(2,1)} %constant.30.clone.th_hbm, bf16[512,1024]{1,0:T(8,128)(2,1)} %constant.31.clone.tl_hbm), custom_call_target="tpu_custom_call" | custom-call | tf_op jit(solution)/shard_map/lon/pallas_call | solution.py:324
  18.4 4.2 %all-to-all-done.2 = bf16[8,13,2,768]{3,2,1,0:T(2,128)(2,1)S(1)} async-done(((bf16[8,13,2,768]{3,2,1,0:T(2,128)(2,1)}), bf16[8,13,2,768]{3,2,1,0:T(2,128)(2,1)S(1)}, u32[]{:S(2)}, u32[]{:S(2)}) %all-to-all-start.2) | async-done | bytes 319520 | tf_op jit(solution)/shard_map/all_to_all | solution.py:278
  22.6 9.8 %all-to-all-start = ((bf16[256,2,768]{2,1,0:T(2,128)(2,1)}), bf16[256,2,768]{2,1,0:T(2,128)(2,1)S(1)}, u32[]{:S(2)}, u32[]{:S(2)}) async-start(bf16[256,2,768]{2,1,0:T(2,128)(2,1)} %get-tuple-element.7), calls=%async_computation | async-start | bytes 1572864 | tf_op jit(solution)/shard_map/all_to_all | solution.py:352
  32.4 1.3 slice_reduce_fusion.1
  33.9 2.6 %collective-permute-start.5 = (bf16[208,768]{1,0:T(8,128)(2,1)S(1)}, bf16[208,768]{1,0:T(8,128)(2,1)S(1)}, u32[]{:S(2)}, u32[]{:S(2)}) collective-permute-start(bf16[208,768]{1,0:T(8,128)(2,1)S(1)} %get-tuple-element.12), channel_id=1, source_target_pairs={{0,48},{1,49},{2,50},{3,51},{4,52},{5,53},{6,54},{7,55},{8,11},{9,... | collective-permute-start | bytes 958472 | tf_op jit(solution)/shard_map/ppermute | solution.py:350
  36.5 1.8 %collective-permute-start.6 = (bf16[208,768]{1,0:T(8,128)(2,1)S(1)}, bf16[208,768]{1,0:T(8,128)(2,1)S(1)}, u32[]{:S(2)}, u32[]{:S(2)}) collective-permute-start(bf16[208,768]{1,0:T(8,128)(2,1)S(1)} %get-tuple-element.12), channel_id=1, source_target_pairs={{0,32},{1,33},{2,34},{3,35},{4,36},{5,37},{6,38},{7,39},{8,10},{9,... | collective-permute-start | bytes 958472 | tf_op jit(solution)/shard_map/ppermute | solution.py:350
  38.3 10.8 %collective-permute-done.5 = bf16[208,768]{1,0:T(8,128)(2,1)S(1)} collective-permute-done((bf16[208,768]{1,0:T(8,128)(2,1)S(1)}, bf16[208,768]{1,0:T(8,128)(2,1)S(1)}, u32[]{:S(2)}, u32[]{:S(2)}) %collective-permute-start.5) | collective-permute-done | bytes 319520 | tf_op jit(solution)/shard_map/ppermute | solution.py:350
  49.1 3.7 %collective-permute-done.4 = bf16[208,768]{1,0:T(8,128)(2,1)S(1)} collective-permute-done((bf16[208,768]{1,0:T(8,128)(2,1)S(1)}, bf16[208,768]{1,0:T(8,128)(2,1)S(1)}, u32[]{:S(2)}, u32[]{:S(2)}) %collective-permute-start.4) | collective-permute-done | bytes 319520 | tf_op jit(solution)/shard_map/ppermute | solution.py:350
  53.0 2.6 %collective-permute-start.9 = (bf16[4,208,768]{2,1,0:T(8,128)(2,1)S(1)}, bf16[4,208,768]{2,1,0:T(8,128)(2,1)S(1)}, u32[]{:S(2)}, u32[]{:S(2)}) collective-permute-start(bf16[4,208,768]{2,1,0:T(8,128)(2,1)S(1)} %pad_maximum_fusion.refs_0_), channel_id=1, source_target_pairs={{0,2},{1,3},{2,0},{3,1},{4,6},{5,7},{6,4},{7,5},{8,40},{9,41},{10,... | collective-permute-start | bytes 3833864 | tf_op jit(solution)/shard_map/ppermute | solution.py:355
  55.6 1.2 collective-permute-start.8
  56.8 0.3 collective-permute-start.7
  57.1 1.7 %pack.1 = bf16[2,112,192]{2,1,0:T(8,128)(2,1)} custom-call(f32[2,96,96]{2,1,0:T(8,128)} %bitcast.26, f32[2,96]{1,0:T(2,128)} %bitcast.33, f32[2,96,96]{2,1,0:T(8,128)} %bitcast.27, f32[2,96]{1,0:T(2,128)} %bitcast.34), custom_call_target="tpu_custom_call" | custom-call | tf_op jit(solution)/shard_map/pack/pallas_call | solution.py:314
  58.8 0.8 collective-permute-start
  59.6 3.5 %collective-permute-done = bf16[2,112,192]{2,1,0:T(8,128)(2,1)S(1)} collective-permute-done((bf16[2,112,192]{2,1,0:T(8,128)(2,1)}, bf16[2,112,192]{2,1,0:T(8,128)(2,1)S(1)}, u32[]{:S(2)}, u32[]{:S(2)}) %collective-permute-start) | collective-permute-done | bytes 86048 | tf_op jit(solution)/shard_map/ppermute | solution.py:322
  63.0 1.6 pad_maximum_fusion.1.w0
  64.8 0.2 collective-permute-start.2
  65.0 15.2 %collective-permute-done.3.w3 = bf16[2,2,112,192]{3,2,1,0:T(8,128)(2,1)} collective-permute-done((bf16[2,2,112,192]{3,2,1,0:T(8,128)(2,1)}, bf16[2,2,112,192]{3,2,1,0:T(8,128)(2,1)}, u32[]{:S(2)}, u32[]{:S(2)}) %collective-permute-start.3) | collective-permute-done | bytes 172064 | tf_op jit(solution)/shard_map/ppermute | solution.py:344
  80.2 1.2 collective-permute-start.1
  81.4 6.7 %collective-permute-done.1.w1 = bf16[2,2,112,192]{3,2,1,0:T(8,128)(2,1)} collective-permute-done((bf16[2,2,112,192]{3,2,1,0:T(8,128)(2,1)}, bf16[2,2,112,192]{3,2,1,0:T(8,128)(2,1)}, u32[]{:S(2)}, u32[]{:S(2)}) %collective-permute-start.1) | collective-permute-done | bytes 172064 | tf_op jit(solution)/shard_map/ppermute | solution.py:344
  88.1 0.9 copy-done.2
  89.0 7.4 %mode.1 = bf16[256,2,768]{2,1,0:T(2,128)(2,1)} custom-call(s32[1]{0:T(128)} %bitcast.own_ref, bf16[256,2,768]{2,1,0:T(2,128)(2,1)} %copy-done.2, bf16[512,512]{1,0:T(8,128)(2,1)} %constant.32.clone.fh_hbm, bf16[512,512]{1,0:T(8,128)(2,1)} %constant.33.clone.fl_hbm, bf16[512,512]{1,0:T(8,128)(2,1)} %constant.34.clone.gh_hbm, ...), custom_call_target="tpu_custom_call" | custom-call | tf_op jit(solution)/shard_map/mode/pallas_call | solution.py:358
  96.4 24.7 %all-to-all-start.1 = ((bf16[256,2,768]{2,1,0:T(2,128)(2,1)}), bf16[256,2,768]{2,1,0:T(2,128)(2,1)S(1)}, u32[]{:S(2)}, u32[]{:S(2)}) async-start(bf16[256,2,768]{2,1,0:T(2,128)(2,1)} %mode.1), calls=%async_computation.1 | async-start | bytes 1572864 | tf_op jit(solution)/shard_map/all_to_all | solution.py:375
  121.2 2.2 %collective-permute-start.10 = (bf16[4,208,768]{2,1,0:T(8,128)(2,1)S(1)}, bf16[4,208,768]{2,1,0:T(8,128)(2,1)}, u32[]{:S(2)}, u32[]{:S(2)}) collective-permute-start(bf16[4,208,768]{2,1,0:T(8,128)(2,1)S(1)} %pad_maximum_fusion.refs_0_), channel_id=1, source_target_pairs={{0,8},{1,9},{2,10},{3,11},{4,12},{5,13},{6,14},{7,15},{8,0},{9,1},... | collective-permute-start | bytes 3833864 | tf_op jit(solution)/shard_map/ppermute | solution.py:376
  123.5 0.4 collective-permute-start.12
  123.9 0.3 collective-permute-start.11
  124.2 1.9 %collective-permute-done.10.refs_4_ = bf16[4,208,768]{2,1,0:T(8,128)(2,1)} collective-permute-done((bf16[4,208,768]{2,1,0:T(8,128)(2,1)S(1)}, bf16[4,208,768]{2,1,0:T(8,128)(2,1)}, u32[]{:S(2)}, u32[]{:S(2)}) %collective-permute-start.10) | collective-permute-done | bytes 1277984 | tf_op jit(solution)/shard_map/ppermute | solution.py:376
  126.1 20.7 %all-to-all-done.1.x_hbm = bf16[256,2,768]{2,1,0:T(2,128)(2,1)S(1)} async-done(((bf16[256,2,768]{2,1,0:T(2,128)(2,1)}), bf16[256,2,768]{2,1,0:T(2,128)(2,1)S(1)}, u32[]{:S(2)}, u32[]{:S(2)}) %all-to-all-start.1) | async-done | bytes 786464 | tf_op jit(solution)/shard_map/all_to_all | solution.py:375
  146.8 0.9 copy-done.1
  147.7 19.4 %tail.1 = f32[5400,128]{1,0:T(8,128)} custom-call(bf16[256,2,768]{2,1,0:T(2,128)(2,1)} %copy-done.1, bf16[912,512]{1,0:T(8,128)(2,1)} %constant.36.clone.th_hbm, bf16[912,512]{1,0:T(8,128)(2,1)} %constant.37.clone.tl_hbm, f32[912,768]{1,0:T(8,128)} %get-tuple-element.8.base_hbm, f32[6,128]{1,0:T(8,128)} %bitcast.30, f32[6,128]{1,0:T(8,128)} %bitcast.31, ...), custom_call_target="tpu_custom_call" | custom-call | tf_op jit(solution)/shard_map/tail/pallas_call | solution.py:378
  (24 shorter events, 0.7 us)
Async XLA Ops:
  1.7 20.8 %all-to-all-start.2 = ((bf16[8,13,2,768]{3,2,1,0:T(2,128)(2,1)}), bf16[8,13,2,768]{3,2,1,0:T(2,128)(2,1)S(1)}, u32[]{:S(2)}, u32[]{:S(2)}) async-start(bf16[8,13,2,768]{3,2,1,0:T(2,128)(2,1)} %broadcast_in_dim.2), calls=%async_computation.2 | async-start | bytes 638976 | tf_op jit(solution)/shard_map/all_to_all | solution.py:278
  22.6 65.6 %all-to-all-start = ((bf16[256,2,768]{2,1,0:T(2,128)(2,1)}), bf16[256,2,768]{2,1,0:T(2,128)(2,1)S(1)}, u32[]{:S(2)}, u32[]{:S(2)}) async-start(bf16[256,2,768]{2,1,0:T(2,128)(2,1)} %get-tuple-element.7), calls=%async_computation | async-start | bytes 1572864 | tf_op jit(solution)/shard_map/all_to_all | solution.py:352
  33.9 15.2 %collective-permute-start.5 = (bf16[208,768]{1,0:T(8,128)(2,1)S(1)}, bf16[208,768]{1,0:T(8,128)(2,1)S(1)}, u32[]{:S(2)}, u32[]{:S(2)}) collective-permute-start(bf16[208,768]{1,0:T(8,128)(2,1)S(1)} %get-tuple-element.12), channel_id=1, source_target_pairs={{0,48},{1,49},{2,50},{3,51},{4,52},{5,53},{6,54},{7,55},{8,11},{9,... | collective-permute-start | bytes 958472 | tf_op jit(solution)/shard_map/ppermute | solution.py:350
  36.5 16.3 %collective-permute-start.4 = (bf16[208,768]{1,0:T(8,128)(2,1)S(1)}, bf16[208,768]{1,0:T(8,128)(2,1)S(1)}, u32[]{:S(2)}, u32[]{:S(2)}) collective-permute-start(bf16[208,768]{1,0:T(8,128)(2,1)S(1)} %get-tuple-element.12), channel_id=1, source_target_pairs={{0,16},{1,17},{2,18},{3,19},{4,20},{5,21},{6,22},{7,23},{8,9},{9,1... | collective-permute-start | bytes 958472 | tf_op jit(solution)/shard_map/ppermute | solution.py:350
  36.5 16.3 %collective-permute-start.6 = (bf16[208,768]{1,0:T(8,128)(2,1)S(1)}, bf16[208,768]{1,0:T(8,128)(2,1)S(1)}, u32[]{:S(2)}, u32[]{:S(2)}) collective-permute-start(bf16[208,768]{1,0:T(8,128)(2,1)S(1)} %get-tuple-element.12), channel_id=1, source_target_pairs={{0,32},{1,33},{2,34},{3,35},{4,36},{5,37},{6,38},{7,39},{8,10},{9,... | collective-permute-start | bytes 958472 | tf_op jit(solution)/shard_map/ppermute | solution.py:350
  53.0 68.2 %copy-start = (bf16[4,208,768]{2,1,0:T(8,128)(2,1)}, bf16[4,208,768]{2,1,0:T(8,128)(2,1)S(1)}, u32[]{:S(2)}) copy-start(bf16[4,208,768]{2,1,0:T(8,128)(2,1)S(1)} %pad_maximum_fusion.refs_0_) | copy-start | bytes 3833860
  53.0 70.4 %collective-permute-start.9 = (bf16[4,208,768]{2,1,0:T(8,128)(2,1)S(1)}, bf16[4,208,768]{2,1,0:T(8,128)(2,1)S(1)}, u32[]{:S(2)}, u32[]{:S(2)}) collective-permute-start(bf16[4,208,768]{2,1,0:T(8,128)(2,1)S(1)} %pad_maximum_fusion.refs_0_), channel_id=1, source_target_pairs={{0,2},{1,3},{2,0},{3,1},{4,6},{5,7},{6,4},{7,5},{8,40},{9,41},{10,... | collective-permute-start | bytes 3833864 | tf_op jit(solution)/shard_map/ppermute | solution.py:355
  55.6 67.9 %collective-permute-start.8 = (bf16[4,208,768]{2,1,0:T(8,128)(2,1)S(1)}, bf16[4,208,768]{2,1,0:T(8,128)(2,1)}, u32[]{:S(2)}, u32[]{:S(2)}) collective-permute-start(bf16[4,208,768]{2,1,0:T(8,128)(2,1)S(1)} %pad_maximum_fusion.refs_0_), channel_id=1, source_target_pairs={{0,3},{1,0},{2,1},{3,2},{4,7},{5,4},{6,5},{7,6},{8,56},{9,57},{10,... | collective-permute-start | bytes 3833864 | tf_op jit(solution)/shard_map/ppermute | solution.py:355
  56.8 67.1 %collective-permute-start.7 = (bf16[4,208,768]{2,1,0:T(8,128)(2,1)S(1)}, bf16[4,208,768]{2,1,0:T(8,128)(2,1)}, u32[]{:S(2)}, u32[]{:S(2)}) collective-permute-start(bf16[4,208,768]{2,1,0:T(8,128)(2,1)S(1)} %pad_maximum_fusion.refs_0_), channel_id=1, source_target_pairs={{0,1},{1,2},{2,3},{3,0},{4,5},{5,6},{6,7},{7,4},{8,24},{9,25},{10,... | collective-permute-start | bytes 3833864 | tf_op jit(solution)/shard_map/ppermute | solution.py:355
  58.8 4.3 %collective-permute-start = (bf16[2,112,192]{2,1,0:T(8,128)(2,1)}, bf16[2,112,192]{2,1,0:T(8,128)(2,1)S(1)}, u32[]{:S(2)}, u32[]{:S(2)}) collective-permute-start(bf16[2,112,192]{2,1,0:T(8,128)(2,1)} %pack.1), channel_id=1, source_target_pairs={{0,4},{1,5},{2,6},{3,7},{4,0},{5,1},{6,2},{7,3},{8,12},{9,13},{10,... | collective-permute-start | bytes 258056 | tf_op jit(solution)/shard_map/ppermute | solution.py:322
  64.7 15.5 %collective-permute-start.3 = (bf16[2,2,112,192]{3,2,1,0:T(8,128)(2,1)}, bf16[2,2,112,192]{3,2,1,0:T(8,128)(2,1)}, u32[]{:S(2)}, u32[]{:S(2)}) collective-permute-start(bf16[2,2,112,192]{3,2,1,0:T(8,128)(2,1)} %pad_maximum_fusion.1.w0), channel_id=1, source_target_pairs={{0,3},{1,2},{2,1},{3,0},{4,7},{5,6},{6,5},{7,4},{8,11},{9,10},{10,... | collective-permute-start | bytes 516104 | tf_op jit(solution)/shard_map/ppermute | solution.py:344
  64.8 16.6 %collective-permute-start.2 = (bf16[2,2,112,192]{3,2,1,0:T(8,128)(2,1)}, bf16[2,2,112,192]{3,2,1,0:T(8,128)(2,1)}, u32[]{:S(2)}, u32[]{:S(2)}) collective-permute-start(bf16[2,2,112,192]{3,2,1,0:T(8,128)(2,1)} %pad_maximum_fusion.1.w0), channel_id=1, source_target_pairs={{0,2},{1,3},{2,0},{3,1},{4,6},{5,7},{6,4},{7,5},{8,10},{9,11},{10,... | collective-permute-start | bytes 516104 | tf_op jit(solution)/shard_map/ppermute | solution.py:344
  80.2 7.9 %collective-permute-start.1 = (bf16[2,2,112,192]{3,2,1,0:T(8,128)(2,1)}, bf16[2,2,112,192]{3,2,1,0:T(8,128)(2,1)}, u32[]{:S(2)}, u32[]{:S(2)}) collective-permute-start(bf16[2,2,112,192]{3,2,1,0:T(8,128)(2,1)} %pad_maximum_fusion.1.w0), channel_id=1, source_target_pairs={{0,1},{1,0},{2,3},{3,2},{4,5},{5,4},{6,7},{7,6},{8,9},{9,8},{10,11... | collective-permute-start | bytes 516104 | tf_op jit(solution)/shard_map/ppermute | solution.py:344
  88.1 0.9 copy-start.2
  96.4 50.4 %all-to-all-start.1 = ((bf16[256,2,768]{2,1,0:T(2,128)(2,1)}), bf16[256,2,768]{2,1,0:T(2,128)(2,1)S(1)}, u32[]{:S(2)}, u32[]{:S(2)}) async-start(bf16[256,2,768]{2,1,0:T(2,128)(2,1)} %mode.1), calls=%async_computation.1 | async-start | bytes 1572864 | tf_op jit(solution)/shard_map/all_to_all | solution.py:375
  121.2 5.0 %collective-permute-start.10 = (bf16[4,208,768]{2,1,0:T(8,128)(2,1)S(1)}, bf16[4,208,768]{2,1,0:T(8,128)(2,1)}, u32[]{:S(2)}, u32[]{:S(2)}) collective-permute-start(bf16[4,208,768]{2,1,0:T(8,128)(2,1)S(1)} %pad_maximum_fusion.refs_0_), channel_id=1, source_target_pairs={{0,8},{1,9},{2,10},{3,11},{4,12},{5,13},{6,14},{7,15},{8,0},{9,1},... | collective-permute-start | bytes 3833864 | tf_op jit(solution)/shard_map/ppermute | solution.py:376
  123.4 23.4 %copy-start.3 = (bf16[4,208,768]{2,1,0:T(8,128)(2,1)}, bf16[4,208,768]{2,1,0:T(8,128)(2,1)S(1)}, u32[]{:S(2)}) copy-start(bf16[4,208,768]{2,1,0:T(8,128)(2,1)S(1)} %collective-permute-done.9.refs_3_) | copy-start | bytes 3833860
  123.4 23.4 %collective-permute-start.13 = (bf16[4,208,768]{2,1,0:T(8,128)(2,1)S(1)}, bf16[4,208,768]{2,1,0:T(8,128)(2,1)}, u32[]{:S(2)}, u32[]{:S(2)}) collective-permute-start(bf16[4,208,768]{2,1,0:T(8,128)(2,1)S(1)} %collective-permute-done.9.refs_3_), channel_id=1, source_target_pairs={{0,8},{1,9},{2,10},{3,11},{4,12},{5,13},{6,14},{7,15},{8,0},{9,1},... | collective-permute-start | bytes 3833864 | tf_op jit(solution)/shard_map/ppermute | solution.py:376
  123.5 23.3 %collective-permute-start.12 = (bf16[4,208,768]{2,1,0:T(8,128)(2,1)}, bf16[4,208,768]{2,1,0:T(8,128)(2,1)}, u32[]{:S(2)}, u32[]{:S(2)}) collective-permute-start(bf16[4,208,768]{2,1,0:T(8,128)(2,1)} %collective-permute-done.8.refs_2_), channel_id=1, source_target_pairs={{0,8},{1,9},{2,10},{3,11},{4,12},{5,13},{6,14},{7,15},{8,0},{9,1},... | collective-permute-start | bytes 3833864 | tf_op jit(solution)/shard_map/ppermute | solution.py:376
  123.9 22.9 %collective-permute-start.11 = (bf16[4,208,768]{2,1,0:T(8,128)(2,1)}, bf16[4,208,768]{2,1,0:T(8,128)(2,1)}, u32[]{:S(2)}, u32[]{:S(2)}) collective-permute-start(bf16[4,208,768]{2,1,0:T(8,128)(2,1)} %collective-permute-done.7.refs_1_), channel_id=1, source_target_pairs={{0,8},{1,9},{2,10},{3,11},{4,12},{5,13},{6,14},{7,15},{8,0},{9,1},... | collective-permute-start | bytes 3833864 | tf_op jit(solution)/shard_map/ppermute | solution.py:376
  146.8 0.9 copy-start.1

commit v2 on v1

v2 whole, which is shorter than its diff:
```python
import functools

import jax
import jax.numpy as jnp
import numpy as np
from jax import lax
from jax.experimental import pallas as pl
from jax.experimental.pallas import tpu as pltpu
from jax.sharding import Mesh
from jax.sharding import PartitionSpec as P


W = 900
HALF = 450
WP = 512
STEP = 149
PART = 152
KW = 256
H = 256
C = 768
BS = 96
NB = 8
TILE = 2 * PART
ROWS = 3 * TILE
norm_eps = 1e-05
shrink_level = 0.01
AXES = ("zh", "y", "co", "zl", "x")
bf16 = jnp.bfloat16
f32 = jnp.float32


def split_table(values):
    high = values.astype(np.float32).astype(jnp.bfloat16)
    low = (values - high.astype(np.float64)).astype(np.float32).astype(jnp.bfloat16)
    return high, low


def lon_tables():
    k = np.arange(KW).reshape(KW // 2, 2).T
    w = np.arange(HALF)
    angle = 2 * np.pi * (k[:, :, None] * w % W) / W
    forward = np.zeros((2, KW // 2, 2, WP))
    forward[:, :, 0, :HALF] = np.cos(angle)
    forward[:, :, 1, :HALF] = -np.sin(angle)
    forward = forward.reshape(2, KW, WP) * W**-0.5
    factor = np.where(k == 0, 1.0, 2.0)[:, :, None]
    waves = np.stack([np.cos(angle) * factor, -np.sin(angle) * factor], axis=2).reshape(2, KW, HALF) * W**-0.5
    backward = np.stack([waves[:, :, STEP * t : STEP * t + PART].transpose(0, 2, 1) for t in range(3)])
    return split_table(forward), split_table(backward)


def lat_tables():
    m = np.arange(H).reshape(H // 2, 2).T.reshape(H)[:, None]
    h = np.arange(H)[None, :]
    angle = 2 * np.pi * (m * h % H) / H
    cos, sin = np.cos(angle), np.sin(angle)
    forward = np.zeros((2, H, H, 2))
    forward[0, :, :, 0] = cos
    forward[0, :, :, 1] = sin
    forward[1, :, :, 0] = -sin
    forward[1, :, :, 1] = cos
    forward = forward * H**-0.5
    parity = forward.reshape(2, 2, H // 2, H, 2)[:, :, :, : H // 2, :]
    backward = parity.transpose(1, 3, 4, 0, 2).reshape(2, H, H)
    return split_table(forward.reshape(2 * H, 2 * H)), split_table(backward)


def dot(a, b):
    return jnp.dot(a, b, preferred_element_type=f32)


def split(x):
    high = x.astype(bf16)
    return high, (x - high.astype(f32)).astype(bf16)


def row_norm(parts, gain, shift):
    count = len(parts) * 128
    mean = jnp.sum(functools.reduce(jnp.add, parts), axis=-1, keepdims=True) / count
    centered = [p - mean for p in parts]
    square = functools.reduce(jnp.add, [c * c for c in centered])
    scale = lax.rsqrt(jnp.sum(square, axis=-1, keepdims=True) / count + norm_eps)
    return [
        c * scale * gain[j : j + 1, :] + shift[j : j + 1, :]
        for j, c in enumerate(centered)
    ]


def start(copies):
    for copy in copies:
        copy.start()


def pack_filters(refs, out_ref):
    for i, (w_ref, b_ref) in enumerate((refs[:2], refs[2:])):
        top = jnp.concatenate([w_ref[0], w_ref[1]], axis=1)
        bias = jnp.concatenate([b_ref[0:1], b_ref[1:2]], axis=1)
        high = bias.astype(bf16).astype(f32)
        rows = lax.broadcasted_iota(jnp.int32, (16, 2 * BS), 0)
        tail = jnp.where(rows == 0, high, jnp.where(rows == 1, bias - high, 0.0))
        out_ref[i] = jnp.concatenate([top, tail], axis=0).astype(bf16)


def lon_kernel(x_hbm, gain_ref, shift_ref, th_hbm, tl_hbm, f0, f1, f2, f3, *refs):
    modes_ref, base_hbm, pack_ref, x_ref, th, tl, base, high, low, sem, out_sem = refs
    cuts = (0, 960, 1920, 2696, 3664, 4624, 5400)
    loads = [
        pltpu.make_async_copy(x_hbm.at[pl.ds(p, q - p)], x_ref.at[pl.ds(p, q - p)], sem.at[i])
        for i, (p, q) in enumerate(zip(cuts[:-1], cuts[1:]))
    ]
    tables = [pltpu.make_async_copy(th_hbm, th, sem.at[6]), pltpu.make_async_copy(tl_hbm, tl, sem.at[7])]
    start([loads[i] for i in (0, 3, 1, 4, 2, 5)] + tables)
    pack_filters((f0, f1, f2, f3), pack_ref)
    gain = gain_ref[...]
    shift = shift_ref[...]
    for parity in range(2):
        high[parity, 448:WP, :] = jnp.zeros((WP - 448, C), bf16)
        low[parity, 448:WP, :] = jnp.zeros((WP - 448, C), bf16)
    for i, (r, n) in enumerate(((0, 160), (160, 160), (320, 130))):
        loads[i].wait()
        loads[i + 3].wait()
        pairs = []
        for first in (r, HALF + r):
            parts = [x_ref[pl.ds(6 * first + j, n, stride=6), :] for j in range(6)]
            normed = row_norm(parts, gain, shift)
            for j in range(6):
                base[pl.ds(6 * first + j, n, stride=6), :] = normed[j] + parts[j]
            pairs.append(normed)
        for j in range(6):
            lanes = slice(128 * j, 128 * j + 128)
            for parity, value in enumerate((pairs[0][j] + pairs[1][j], pairs[0][j] - pairs[1][j])):
                high[parity, r : r + n, lanes], low[parity, r : r + n, lanes] = split(value)
    store = pltpu.make_async_copy(base, base_hbm, out_sem)
    store.start()
    tables[0].wait()
    tables[1].wait()
    for parity in range(2):
        modes = dot(th[parity], high[parity]) + dot(th[parity], low[parity]) + dot(tl[parity], high[parity])
        modes_ref[128 * parity : 128 * parity + 128] = modes.astype(bf16).reshape(KW // 2, 2, C)
    store.wait()


def mode_kernel(own_ref, x_hbm, fh_hbm, fl_hbm, gh_hbm, gl_hbm, w0, w1, w2, w3, out_ref, x_ref, fh, fl, gh, gl, w_all, zh, zl, sem):
    pairs = [(x_hbm, x_ref), (fh_hbm, fh), (fl_hbm, fl)] + [(w, w_all.at[d]) for d, w in enumerate((w0, w1, w2, w3))]
    pairs += [(gh_hbm, gh), (gl_hbm, gl)]
    copies = [pltpu.make_async_copy(source, target, sem.at[i]) for i, (source, target) in enumerate(pairs)]
    start(copies)
    own = own_ref[0]
    copies[0].wait()
    copies[1].wait()
    x = x_ref[...].reshape(2 * H, C)
    y = dot(fh[...], x)
    copies[2].wait()
    y = y + dot(fl[...], x)
    for copy in copies[3:7]:
        copy.wait()

    def layer(values, slot, i):
        high, low = split(values)
        packed = w_all[jnp.bitwise_and(slot, 3), lax.shift_right_logical(slot, 2), i]
        top = packed[0:BS]
        bottom = jnp.concatenate([-top[:, BS:], top[:, :BS]], axis=1)
        weight = jnp.concatenate([top, bottom], axis=0)
        bias = packed[BS : BS + 16].astype(f32)
        return dot(high, weight) + dot(low, weight) + (bias[0:1] + bias[1:2])

    outs = []
    for b in range(NB):
        slot = jnp.bitwise_xor(own, b)
        lanes = slice(BS * b, BS * b + BS)
        values = jnp.concatenate([y[:H, lanes], y[H:, lanes]], axis=1)
        first = jnp.maximum(layer(values, slot, 0), 0.0)
        second = layer(first, slot, 1)
        outs.append(second - jnp.clip(second, -shrink_level, shrink_level))
    for part in range(2):
        joined = jnp.concatenate([o[:, BS * part : BS * part + BS] for o in outs], axis=1)
        high, low = split(joined)
        for parity in range(2):
            rows = slice(H // 2 * parity, H // 2 * parity + H // 2)
            spot = slice(H // 2 * part, H // 2 * part + H // 2)
            zh[parity, spot, :] = high[rows]
            zl[parity, spot, :] = low[rows]
    copies[7].wait()
    copies[8].wait()
    even, odd = [dot(gh[p], zh[p]) + dot(gh[p], zl[p]) + dot(gl[p], zh[p]) for p in range(2)]
    out_ref[0 : H // 2] = (even + odd).astype(bf16).reshape(H // 2, 2, C)
    out_ref[H // 2 : H] = (even - odd).astype(bf16).reshape(H // 2, 2, C)


def gelu(x):
    return 0.5 * x * (1.0 + lax.erf(x * 0.7071067811865476))


def tail_kernel(x_hbm, th_hbm, tl_hbm, base_hbm, gain_ref, shift_ref, bias_ref, *refs):
    w_hbm, out_hbm = refs[:10], refs[10]
    x_ref, th, tl, base, weights, normed, summed, result, sem, w_sem, out_sem = refs[11:]
    pairs = [(x_hbm, x_ref), (th_hbm, th), (tl_hbm, tl), (base_hbm, base)]
    copies = [pltpu.make_async_copy(source, target, sem.at[i]) for i, (source, target) in enumerate(pairs)]
    w_copies = []
    spot = 0
    for i, w in enumerate(w_hbm):
        w_copies.append(pltpu.make_async_copy(w, weights.at[pl.ds(spot, w.shape[0])], w_sem.at[i]))
        spot += w.shape[0]
    start(copies + w_copies)
    gain = gain_ref[...]
    shift = shift_ref[...]
    out_bias = bias_ref[...]
    for copy in copies:
        copy.wait()
    x = x_ref[...].reshape(2 * KW, C)
    for t in range(3):
        even, odd = [dot(th[t, p], x[KW * p : KW * p + KW]) + dot(tl[t, p], x[KW * p : KW * p + KW]) for p in range(2)]
        parts = []
        for j in range(6):
            lanes = slice(128 * j, 128 * j + 128)
            near = base[pl.ds(6 * STEP * t + j, PART, stride=6), :]
            far = base[pl.ds(6 * (STEP * t + HALF) + j, PART, stride=6), :]
            parts.append(
                jnp.concatenate([even[:, lanes] + odd[:, lanes] + near, even[:, lanes] - odd[:, lanes] + far], axis=0)
            )
        rows = slice(TILE * t, TILE * t + TILE)
        normed[rows, :] = jnp.concatenate(row_norm(parts, gain, shift), axis=1).astype(bf16)
        for j in range(6):
            summed[rows, 128 * j : 128 * j + 128] = parts[j] + out_bias[j : j + 1, :]
    for copy in w_copies:
        copy.wait()

    def out_copy(i, first, last):
        span = pl.ds(first, last - first)
        return pltpu.make_async_copy(result.at[span], out_hbm.at[span], out_sem.at[i])

    outs = [out_copy(i, *c) for i, c in enumerate(((0, 1784), (2704, 4488), (1784, 2704), (4488, 5400)))]

    def tile(t, carry):
        rows = pl.ds(pl.multiple_of(t * TILE, 16), TILE)
        tokens = normed[rows, :]
        acc = summed[rows, :]
        for first in range(0, 32, 8):
            w1 = jnp.concatenate([weights[q, 0:BS, :] for q in range(first, first + 8)], axis=0)
            w2 = jnp.concatenate([weights[q, BS : 2 * BS, :] for q in range(first, first + 8)], axis=0)
            bias = jnp.concatenate(
                [weights[q, 2 * BS : 2 * BS + 16, :].astype(f32)[0:1, 0:BS] for q in range(first, first + 8)], axis=1
            )
            for c in range(3):
                span = slice(256 * c, 256 * c + 256)
                pre = lax.dot_general(tokens, w1[span], (((1,), (1,)), ((), ())), preferred_element_type=f32)
                hidden = gelu(pre + bias[:, span]).astype(bf16)
                acc = acc + dot(hidden, w2[span])
        for j in range(6):
            lanes = slice(128 * j, 128 * j + 128)
            result[pl.ds(6 * STEP * t + j, PART, stride=6), :] = acc[:PART, lanes]
            result[pl.ds(6 * STEP * t + 6 * HALF + j, PART, stride=6), :] = acc[PART:, lanes]

        @pl.when(t == 1)
        def _():
            outs[0].start()
            outs[1].start()

        return carry

    lax.fori_loop(0, 3, tile, 0)
    outs[2].start()
    outs[3].start()
    for copy in outs:
        copy.wait()


def vmem(n):
    return [pl.BlockSpec(memory_space=pltpu.VMEM)] * n


def anywhere(n):
    return [pl.BlockSpec(memory_space=pl.ANY)] * n


params = pltpu.CompilerParams(vmem_limit_bytes=56 * 2**20)


def place(index):
    lat, chan = divmod(index, 8)
    zh, rest = divmod(lat, 8)
    y, core = divmod(rest, 2)
    zl, x = divmod(chan, 4)
    return x, y, zh * 2 + zl, core


def index_of(x, y, z, core):
    return ((z // 2 * 4 + y) * 2 + core) * 8 + z % 2 * 4 + x


def moves(step):
    return [(d, index_of(*step(*place(d)))) for d in range(256)]


def block_moves(bits):
    return [(d, d ^ bits) for d in range(256)]


def z_moves(bits):
    return moves(lambda x, y, z, c: (x, y, z ^ bits, c))


def near_moves(n):
    return moves(lambda x, y, z, c: (x, (y + n) % 4, z, c) if c == 0 else ((x + n) % 4, y, z, c))


def far_moves(n):
    return moves(lambda x, y, z, c: ((x + n) % 4, y, z, c) if c == 0 else (x, (y + n) % 4, z, c))


core_moves = moves(lambda x, y, z, c: (x, y, z, 1 - c))


def per_device(
    fields,
    first_gain,
    first_shift,
    filter_one,
    filter_one_bias,
    filter_two,
    filter_two_bias,
    second_gain,
    second_shift,
    dense_weights,
    dense_bias,
    output_bias,
):
    (lon_h, lon_l), (back_h, back_l) = lon_tables()
    (lat_h, lat_l), (tal_h, tal_l) = lat_tables()
    shape = jax.ShapeDtypeStruct

    bias_rows = jnp.pad(dense_bias.reshape(1, 1, 12), ((0, 0), (0, 1), (0, C - 12)))
    shard = jnp.concatenate([dense_weights, bias_rows], axis=0)
    one = lax.ppermute(shard, AXES, z_moves(1))

    modes, base, packed = pl.pallas_call(
        lon_kernel,
        out_shape=(shape((KW, 2, C), bf16), shape((6 * W, 128), f32), shape((2, BS + 16, 2 * BS), bf16)),
        in_specs=anywhere(1) + vmem(2) + anywhere(2) + vmem(4),
        out_specs=(vmem(1)[0], anywhere(1)[0], vmem(1)[0]),
        scratch_shapes=[
            pltpu.VMEM((6 * W, 128), f32),
            pltpu.VMEM((2, KW, WP), bf16),
            pltpu.VMEM((2, KW, WP), bf16),
            pltpu.VMEM((6 * W, 128), f32),
            pltpu.VMEM((2, WP, C), bf16),
            pltpu.VMEM((2, WP, C), bf16),
            pltpu.SemaphoreType.DMA((8,)),
            pltpu.SemaphoreType.DMA,
        ],
        compiler_params=params,
        name="lon",
    )(
        fields.reshape(6 * W, 128),
        first_gain.reshape(6, 128),
        first_shift.reshape(6, 128),
        lon_h,
        lon_l,
        filter_one[0],
        filter_one_bias[0],
        filter_two[0],
        filter_two_bias[0],
    )

    two = jnp.concatenate([shard, one], axis=0)
    four = jnp.concatenate([two, lax.ppermute(two, AXES, z_moves(2))], axis=0)
    eight = jnp.concatenate([four, lax.ppermute(four, AXES, z_moves(4))], axis=0)
    stacked = eight.reshape(8, 13, 2, C)
    partner = lax.ppermute(packed, AXES, block_moves(4))
    pair = jnp.stack([packed, partner])
    filters = [pair] + [lax.ppermute(pair, AXES, block_moves(b)) for b in range(1, 4)]

    rows_in = stacked[:, :12, 0, :].reshape(BS, C)
    rows_out = stacked[:, :12, 1, :].reshape(BS, C)
    bias_row = jnp.pad(stacked[:, 12, 0, :12].reshape(1, BS), ((0, 15), (0, C - BS)))
    block = jnp.concatenate([rows_in, rows_out, bias_row], axis=0)
    near = [block] + [lax.ppermute(block, AXES, near_moves(n)) for n in (1, -1, 2)]

    moved = lax.all_to_all(modes, AXES, split_axis=0, concat_axis=0, tiled=True)

    group = jnp.stack(near)
    left = lax.ppermute(group, AXES, far_moves(1))
    right = lax.ppermute(group, AXES, far_moves(-1))
    across = [lax.ppermute(left[:2], AXES, far_moves(1)), lax.ppermute(right[2:], AXES, far_moves(-1))]
    far = [group, left, right] + across

    own = lax.axis_index(("zl", "x")).astype(jnp.int32).reshape(1)
    mode_call = pl.pallas_call(
        mode_kernel,
        out_shape=shape((H, 2, C), bf16),
        in_specs=[pl.BlockSpec(memory_space=pltpu.SMEM)] + anywhere(9),
        out_specs=vmem(1)[0],
        scratch_shapes=[pltpu.VMEM((H, 2, C), bf16)]
        + [pltpu.VMEM((2 * H, 2 * H), bf16)] * 2
        + [pltpu.VMEM((2, H, H), bf16)] * 2
        + [
            pltpu.VMEM((4, 2, 2, BS + 16, 2 * BS), bf16),
            pltpu.VMEM((2, H, C), bf16),
            pltpu.VMEM((2, H, C), bf16),
            pltpu.SemaphoreType.DMA((9,)),
        ],
        compiler_params=params,
        name="mode",
    )
    mixed = mode_call(own, moved, lat_h, lat_l, tal_h, tal_l, *filters)

    returned = lax.all_to_all(mixed, AXES, split_axis=0, concat_axis=0, tiled=True)
    other = [lax.ppermute(g, AXES, core_moves) for g in far]

    out = pl.pallas_call(
        tail_kernel,
        out_shape=shape((6 * W, 128), f32),
        in_specs=anywhere(4) + vmem(3) + anywhere(10),
        out_specs=anywhere(1)[0],
        scratch_shapes=[
            pltpu.VMEM((KW, 2, C), bf16),
            pltpu.VMEM((3, 2, PART, KW), bf16),
            pltpu.VMEM((3, 2, PART, KW), bf16),
            pltpu.VMEM((6 * W, 128), f32),
            pltpu.VMEM((32, 2 * BS + 16, C), bf16),
            pltpu.VMEM((ROWS, C), bf16),
            pltpu.VMEM((ROWS, C), f32),
            pltpu.VMEM((6 * W, 128), f32),
            pltpu.SemaphoreType.DMA((4,)),
            pltpu.SemaphoreType.DMA((10,)),
            pltpu.SemaphoreType.DMA((4,)),
        ],
        compiler_params=params,
        name="tail",
    )(
        returned,
        back_h,
        back_l,
        base,
        second_gain.reshape(6, 128),
        second_shift.reshape(6, 128),
        output_bias.reshape(6, 128),
        *far,
        *other,
    )
    return out.reshape(1, W, C)


def solution(mesh):
    fine = Mesh(mesh.devices.reshape(4, 4, 2, 2, 4), AXES)
    chan = AXES[3:]
    placed = (
        P(AXES, None, None),
        P(),
        P(),
        P(chan, None, None, None),
        P(chan, None, None),
        P(chan, None, None, None),
        P(chan, None, None),
        P(),
        P(),
        P(AXES, None, None),
        P(AXES),
        P(),
    )
    return jax.shard_map(
        per_device, mesh=fine, in_specs=placed, out_specs=P(AXES, None, None), check_vma=False
    )
```

time: 168 us -> 167 us (level)
  Pallas kernels: 36.1 us -> 32.4 us
  starting transfers between devices: 57.4 us -> 60.8 us
  waiting for transfers between devices: 66.8 us -> 64.4 us
  local copies, waits for them, and re-layouts: 4.12 us -> 6.07 us
    ppermute x3 -> x7, waiting for transfers between devices: 0.01 us -> 37.3 us  [the longest x1 22.4 us: per_device(): lax.ppermute(four, AXES, z_moves(4))]
    all_to_all x1, waiting for transfers between devices: 20.7 us -> 3.63 us  [per_device(): lax.all_to_all(mixed, AXES, split_axis=0, concat_axis=0, tiled=True)]
    ppermute x3 -> x7, starting transfers between devices: 4.07 us -> 16 us  [the longest x1 6.28 us: per_device(): lax.ppermute(four, AXES, z_moves(4))]
    ppermute x3, waiting for transfers between devices: 21.9 us -> 11.4 us  [per_device(): lax.ppermute(pair, AXES, block_moves(b))]
    all_to_all x1 -> x0, starting transfers between devices: 9 us -> none  [spread(): return lax.all_to_all(copies, axes, split_axis=0, concat_axis=0, tiled=True)]
    all_to_all x1, starting transfers between devices: 24.7 us -> 16.8 us  [per_device(): lax.all_to_all(mixed, AXES, split_axis=0, concat_axis=0, tiled=True)]
    ppermute x3, waiting for transfers between devices: 14.5 us -> 9.06 us  [per_device(): lax.ppermute(block, AXES, near_moves(n))]
    all_to_all x1, starting transfers between devices: 9.77 us -> 14.3 us  [per_device(): moved = lax.all_to_all(modes, AXES, split_axis=0, concat_axis=0, tiled=True)]
  transfers between devices with their start and end apart: 17 -> 21, of which waited for: 8 -> 10; matrix products, arithmetic and copies ran while one was open for 2% -> 2% of each run, Pallas kernels for 10% -> 8%
where the time goes in v2:
time: 167 us
  waiting for transfers between devices  64.4 us (39%)
  starting transfers between devices  60.8 us (36%)
  Pallas kernels  32.4 us (19%)
  local copies, waits for them, and re-layouts  6.07 us (4%)
  other arithmetic  2.87 us (2%)
    ppermute x1, waiting for transfers between devices, per_device(): lax.ppermute(four, AXES, z_moves(4))  22.4 us
    pallas_call x1, Pallas kernels, per_device(): pl.pallas_call(tail_kernel, out_shape=shape((6 * W, 128), f32), in_specs=...  19.2 us
    all_to_all x1, starting transfers between devices, per_device(): lax.all_to_all(mixed, AXES, split_axis=0, concat_axis=0, tiled=True)  16.8 us
    all_to_all x1, starting transfers between devices, per_device(): moved = lax.all_to_all(modes, AXES, split_axis=0, concat_axis=0, tiled=True)  14.3 us
    ppermute x3, waiting for transfers between devices, per_device(): lax.ppermute(pair, AXES, block_moves(b))  11.4 us
    ppermute x1, waiting for transfers between devices, per_device(): lax.ppermute(right[2:], AXES, far_moves(-1))  10.7 us
    ppermute x3, waiting for transfers between devices, per_device(): lax.ppermute(block, AXES, near_moves(n))  9.06 us
    pallas_call x1, Pallas kernels, per_device(): mixed = mode_call(own, moved, lat_h, lat_l, tal_h, tal_l, *filters)  6.82 us
  transfers between devices with their start and end apart: 21, of which 10 were waited for; matrix products, arithmetic and copies ran while one was open for 2% of the time, Pallas kernels for 8%

profile of v2, /device:TPU:1, one launch (start us, length us, event | category | flops | bytes accessed | tf_op | source)
XLA Modules:
  0.0 166.9 jit_solution(14981974514792722282)
XLA Ops:
  2.3 2.5 %collective-permute-start.4 = (bf16[13,2,768]{2,1,0:T(2,128)(2,1)S(1)}, bf16[13,2,768]{2,1,0:T(2,128)(2,1)S(1)}, u32[]{:S(2)}, u32[]{:S(2)}) collective-permute-start(bf16[13,2,768]{2,1,0:T(2,128)(2,1)S(1)} %pad_maximum_fusion.4), channel_id=1, source_target_pairs={{0,4},{1,5},{2,6},{3,7},{4,0},{5,1},{6,2},{7,3},{8,12},{9,13},{10,... | collective-permute-start | bytes 119816 | tf_op jit(solution)/shard_map/ppermute | solution.py:334
  4.8 1.4 collective-permute-done.4
  6.2 0.9 pad_maximum_fusion.3
  7.1 3.1 %collective-permute-start.5 = (bf16[26,2,768]{2,1,0:T(2,128)(2,1)S(1)}, bf16[26,2,768]{2,1,0:T(2,128)(2,1)S(1)}, u32[]{:S(2)}, u32[]{:S(2)}) collective-permute-start(bf16[26,2,768]{2,1,0:T(2,128)(2,1)S(1)} %pad_maximum_fusion.3), channel_id=1, source_target_pairs={{0,64},{1,65},{2,66},{3,67},{4,68},{5,69},{6,70},{7,71},{8,72},{9,... | collective-permute-start | bytes 239624 | tf_op jit(solution)/shard_map/ppermute | solution.py:366
  10.2 6.3 %lon.1 = (bf16[256,2,768]{2,1,0:T(2,128)(2,1)}, f32[5400,128]{1,0:T(8,128)}, bf16[2,112,192]{2,1,0:T(8,128)(2,1)}) custom-call(f32[5400,128]{1,0:T(8,128)} %bitcast.21, f32[6,128]{1,0:T(8,128)} %bitcast.31, f32[6,128]{1,0:T(8,128)} %bitcast.32, bf16[2,256,512]{2,1,0:T(8,128)(2,1)} %constant.30.clone.th_hbm, bf16[2,256,512]{2,1,0:T(8,128)(2,1)} %constant.31.clone.tl_hbm, ...), custom_call_target="tpu_custom_call" | custom-call | tf_op jit(solution)/shard_map/lon/pallas_call | solution.py:336
  16.5 14.3 %all-to-all-start = ((bf16[256,2,768]{2,1,0:T(2,128)(2,1)}), bf16[256,2,768]{2,1,0:T(2,128)(2,1)S(1)}, u32[]{:S(2)}, u32[]{:S(2)}) async-start(bf16[256,2,768]{2,1,0:T(2,128)(2,1)} %get-tuple-element.8), calls=%async_computation | async-start | bytes 1572864 | tf_op jit(solution)/shard_map/all_to_all | solution.py:379
  31.1 6.3 %collective-permute-start.6 = (bf16[52,2,768]{2,1,0:T(2,128)(2,1)S(1)}, bf16[52,2,768]{2,1,0:T(2,128)(2,1)S(1)}, u32[]{:S(2)}, u32[]{:S(2)}) collective-permute-start(bf16[52,2,768]{2,1,0:T(2,128)(2,1)S(1)} %pad_maximum_fusion.2), channel_id=1, source_target_pairs={{0,128},{1,129},{2,130},{3,131},{4,132},{5,133},{6,134},{7,135},{8... | collective-permute-start | bytes 479240 | tf_op jit(solution)/shard_map/ppermute | solution.py:367
  37.5 22.4 %collective-permute-done.6 = bf16[52,2,768]{2,1,0:T(2,128)(2,1)S(1)} collective-permute-done((bf16[52,2,768]{2,1,0:T(2,128)(2,1)S(1)}, bf16[52,2,768]{2,1,0:T(2,128)(2,1)S(1)}, u32[]{:S(2)}, u32[]{:S(2)}) %collective-permute-start.6) | collective-permute-done | bytes 159776 | tf_op jit(solution)/shard_map/ppermute | solution.py:367
  60.0 1.3 slice_reduce_fusion.1
  61.5 2.5 %collective-permute-start.8 = (bf16[208,768]{1,0:T(8,128)(2,1)S(1)}, bf16[208,768]{1,0:T(8,128)(2,1)S(1)}, u32[]{:S(2)}, u32[]{:S(2)}) collective-permute-start(bf16[208,768]{1,0:T(8,128)(2,1)S(1)} %get-tuple-element.14), channel_id=1, source_target_pairs={{0,48},{1,49},{2,50},{3,51},{4,52},{5,53},{6,54},{7,55},{8,11},{9,... | collective-permute-start | bytes 958472 | tf_op jit(solution)/shard_map/ppermute | solution.py:377
  64.0 1.7 %collective-permute-start.9 = (bf16[208,768]{1,0:T(8,128)(2,1)S(1)}, bf16[208,768]{1,0:T(8,128)(2,1)S(1)}, u32[]{:S(2)}, u32[]{:S(2)}) collective-permute-start(bf16[208,768]{1,0:T(8,128)(2,1)S(1)} %get-tuple-element.14), channel_id=1, source_target_pairs={{0,32},{1,33},{2,34},{3,35},{4,36},{5,37},{6,38},{7,39},{8,10},{9,... | collective-permute-start | bytes 958472 | tf_op jit(solution)/shard_map/ppermute | solution.py:377
  65.7 5.6 %collective-permute-done.8 = bf16[208,768]{1,0:T(8,128)(2,1)S(1)} collective-permute-done((bf16[208,768]{1,0:T(8,128)(2,1)S(1)}, bf16[208,768]{1,0:T(8,128)(2,1)S(1)}, u32[]{:S(2)}, u32[]{:S(2)}) %collective-permute-start.8) | collective-permute-done | bytes 319520 | tf_op jit(solution)/shard_map/ppermute | solution.py:377
  71.4 3.4 %collective-permute-done.7 = bf16[208,768]{1,0:T(8,128)(2,1)S(1)} collective-permute-done((bf16[208,768]{1,0:T(8,128)(2,1)S(1)}, bf16[208,768]{1,0:T(8,128)(2,1)S(1)}, u32[]{:S(2)}, u32[]{:S(2)}) %collective-permute-start.7) | collective-permute-done | bytes 319520 | tf_op jit(solution)/shard_map/ppermute | solution.py:377
  75.0 2.0 %collective-permute-start.11 = (bf16[4,208,768]{2,1,0:T(8,128)(2,1)S(1)}, bf16[4,208,768]{2,1,0:T(8,128)(2,1)S(1)}, u32[]{:S(2)}, u32[]{:S(2)}) collective-permute-start(bf16[4,208,768]{2,1,0:T(8,128)(2,1)S(1)} %pad_maximum_fusion.refs_0_), channel_id=1, source_target_pairs={{0,3},{1,0},{2,1},{3,2},{4,7},{5,4},{6,5},{7,6},{8,56},{9,57},{10,... | collective-permute-start | bytes 3833864 | tf_op jit(solution)/shard_map/ppermute | solution.py:383
  77.0 0.9 collective-permute-start
  77.9 3.0 %collective-permute-done = bf16[2,112,192]{2,1,0:T(8,128)(2,1)S(1)} collective-permute-done((bf16[2,112,192]{2,1,0:T(8,128)(2,1)S(1)}, bf16[2,112,192]{2,1,0:T(8,128)(2,1)S(1)}, u32[]{:S(2)}, u32[]{:S(2)}) %collective-permute-start) | collective-permute-done | bytes 86048 | tf_op jit(solution)/shard_map/ppermute | solution.py:369
  82.2 2.8 %collective-permute-start.1 = (bf16[2,2,112,192]{3,2,1,0:T(8,128)(2,1)}, bf16[2,2,112,192]{3,2,1,0:T(8,128)(2,1)}, u32[]{:S(2)}, u32[]{:S(2)}) collective-permute-start(bf16[2,2,112,192]{3,2,1,0:T(8,128)(2,1)} %pad_maximum_fusion.1.w0), channel_id=1, source_target_pairs={{0,1},{1,0},{2,3},{3,2},{4,5},{5,4},{6,7},{7,6},{8,9},{9,8},{10,11... | collective-permute-start | bytes 516104 | tf_op jit(solution)/shard_map/ppermute | solution.py:371
  84.9 8.3 %collective-permute-done.3.w3 = bf16[2,2,112,192]{3,2,1,0:T(8,128)(2,1)} collective-permute-done((bf16[2,2,112,192]{3,2,1,0:T(8,128)(2,1)}, bf16[2,2,112,192]{3,2,1,0:T(8,128)(2,1)}, u32[]{:S(2)}, u32[]{:S(2)}) %collective-permute-start.3) | collective-permute-done | bytes 172064 | tf_op jit(solution)/shard_map/ppermute | solution.py:371
  93.3 3.0 %collective-permute-done.1.w1 = bf16[2,2,112,192]{3,2,1,0:T(8,128)(2,1)} collective-permute-done((bf16[2,2,112,192]{3,2,1,0:T(8,128)(2,1)}, bf16[2,2,112,192]{3,2,1,0:T(8,128)(2,1)}, u32[]{:S(2)}, u32[]{:S(2)}) %collective-permute-start.1) | collective-permute-done | bytes 172064 | tf_op jit(solution)/shard_map/ppermute | solution.py:371
  96.3 0.9 copy-done.2
  97.2 6.8 %mode.1 = bf16[256,2,768]{2,1,0:T(2,128)(2,1)} custom-call(s32[1]{0:T(128)} %bitcast.own_ref, bf16[256,2,768]{2,1,0:T(2,128)(2,1)} %copy-done.2, bf16[512,512]{1,0:T(8,128)(2,1)} %constant.32.clone.fh_hbm, bf16[512,512]{1,0:T(8,128)(2,1)} %constant.33.clone.fl_hbm, bf16[2,256,256]{2,1,0:T(8,128)(2,1)} %constant.34.clone.gh_hbm, ...), custom_call_target="tpu_custom_call" | custom-call | tf_op jit(solution)/shard_map/mode/pallas_call | solution.py:405
  104.0 16.8 %all-to-all-start.1 = ((bf16[256,2,768]{2,1,0:T(2,128)(2,1)}), bf16[256,2,768]{2,1,0:T(2,128)(2,1)S(1)}, u32[]{:S(2)}, u32[]{:S(2)}) async-start(bf16[256,2,768]{2,1,0:T(2,128)(2,1)} %mode.1), calls=%async_computation.1 | async-start | bytes 1572864 | tf_op jit(solution)/shard_map/all_to_all | solution.py:407
  120.8 2.4 %collective-permute-start.14 = (bf16[4,208,768]{2,1,0:T(8,128)(2,1)S(1)}, bf16[4,208,768]{2,1,0:T(8,128)(2,1)}, u32[]{:S(2)}, u32[]{:S(2)}) collective-permute-start(bf16[4,208,768]{2,1,0:T(8,128)(2,1)S(1)} %pad_maximum_fusion.refs_0_), channel_id=1, source_target_pairs={{0,8},{1,9},{2,10},{3,11},{4,12},{5,13},{6,14},{7,15},{8,0},{9,1},... | collective-permute-start | bytes 3833864 | tf_op jit(solution)/shard_map/ppermute | solution.py:408
  123.2 0.9 collective-permute-start.13
  124.4 1.1 slice.23
  125.9 1.1 collective-permute-start.12
  127.0 10.7 %collective-permute-done.13.refs_4_ = bf16[2,208,768]{2,1,0:T(8,128)(2,1)} collective-permute-done((bf16[2,208,768]{2,1,0:T(8,128)(2,1)S(1)}, bf16[2,208,768]{2,1,0:T(8,128)(2,1)}, u32[]{:S(2)}, u32[]{:S(2)}) %collective-permute-start.13) | collective-permute-done | bytes 639008 | tf_op jit(solution)/shard_map/ppermute | solution.py:384
  137.7 1.4 collective-permute-start.18
  139.1 2.8 %collective-permute-done.12.refs_3_ = bf16[2,208,768]{2,1,0:T(8,128)(2,1)} collective-permute-done((bf16[2,208,768]{2,1,0:T(8,128)(2,1)S(1)}, bf16[2,208,768]{2,1,0:T(8,128)(2,1)}, u32[]{:S(2)}, u32[]{:S(2)}) %collective-permute-start.12) | collective-permute-done | bytes 639008 | tf_op jit(solution)/shard_map/ppermute | solution.py:384
  141.9 1.1 collective-permute-start.17
  143.0 3.6 %all-to-all-done.1.x_hbm = bf16[256,2,768]{2,1,0:T(2,128)(2,1)S(1)} async-done(((bf16[256,2,768]{2,1,0:T(2,128)(2,1)}), bf16[256,2,768]{2,1,0:T(2,128)(2,1)S(1)}, u32[]{:S(2)}, u32[]{:S(2)}) %all-to-all-start.1) | async-done | bytes 786464 | tf_op jit(solution)/shard_map/all_to_all | solution.py:407
  147.5 19.2 %tail.1 = f32[5400,128]{1,0:T(8,128)} custom-call(bf16[256,2,768]{2,1,0:T(2,128)(2,1)} %copy-done.1, bf16[3,2,152,256]{3,2,1,0:T(8,128)(2,1)} %constant.36.clone.th_hbm, bf16[3,2,152,256]{3,2,1,0:T(8,128)(2,1)} %constant.37.clone.tl_hbm, f32[5400,128]{1,0:T(8,128)} %get-tuple-element.10.base_hbm, f32[6,128]{1,0:T(8,128)} %bitcast.33, f32[6,128]{1,0:T(8,128)} %bitcast.34, ...), custom_call_target="tpu_custom_call" | custom-call | tf_op jit(solution)/shard_map/tail/pallas_call | solution.py:410
  (43 shorter events, 5.9 us)
Async XLA Ops:
  2.3 3.9 %collective-permute-start.4 = (bf16[13,2,768]{2,1,0:T(2,128)(2,1)S(1)}, bf16[13,2,768]{2,1,0:T(2,128)(2,1)S(1)}, u32[]{:S(2)}, u32[]{:S(2)}) collective-permute-start(bf16[13,2,768]{2,1,0:T(2,128)(2,1)S(1)} %pad_maximum_fusion.4), channel_id=1, source_target_pairs={{0,4},{1,5},{2,6},{3,7},{4,0},{5,1},{6,2},{7,3},{8,12},{9,13},{10,... | collective-permute-start | bytes 119816 | tf_op jit(solution)/shard_map/ppermute | solution.py:334
  7.1 23.7 %collective-permute-start.5 = (bf16[26,2,768]{2,1,0:T(2,128)(2,1)S(1)}, bf16[26,2,768]{2,1,0:T(2,128)(2,1)S(1)}, u32[]{:S(2)}, u32[]{:S(2)}) collective-permute-start(bf16[26,2,768]{2,1,0:T(2,128)(2,1)S(1)} %pad_maximum_fusion.3), channel_id=1, source_target_pairs={{0,64},{1,65},{2,66},{3,67},{4,68},{5,69},{6,70},{7,71},{8,72},{9,... | collective-permute-start | bytes 239624 | tf_op jit(solution)/shard_map/ppermute | solution.py:366
  16.5 14.3 %copy-start.4 = (bf16[12,2,768]{2,1,0:T(2,128)(2,1)S(1)}, bf16[12,2,768]{2,1,0:T(2,128)(2,1)}, u32[]{:S(2)}) copy-start(bf16[12,2,768]{2,1,0:T(2,128)(2,1)} %param.29) | copy-start | bytes 110596
  16.5 79.8 %all-to-all-start = ((bf16[256,2,768]{2,1,0:T(2,128)(2,1)}), bf16[256,2,768]{2,1,0:T(2,128)(2,1)S(1)}, u32[]{:S(2)}, u32[]{:S(2)}) async-start(bf16[256,2,768]{2,1,0:T(2,128)(2,1)} %get-tuple-element.8), calls=%async_computation | async-start | bytes 1572864 | tf_op jit(solution)/shard_map/all_to_all | solution.py:379
  31.1 28.8 %collective-permute-start.6 = (bf16[52,2,768]{2,1,0:T(2,128)(2,1)S(1)}, bf16[52,2,768]{2,1,0:T(2,128)(2,1)S(1)}, u32[]{:S(2)}, u32[]{:S(2)}) collective-permute-start(bf16[52,2,768]{2,1,0:T(2,128)(2,1)S(1)} %pad_maximum_fusion.2), channel_id=1, source_target_pairs={{0,128},{1,129},{2,130},{3,131},{4,132},{5,133},{6,134},{7,135},{8... | collective-permute-start | bytes 479240 | tf_op jit(solution)/shard_map/ppermute | solution.py:367
  61.5 9.9 %collective-permute-start.8 = (bf16[208,768]{1,0:T(8,128)(2,1)S(1)}, bf16[208,768]{1,0:T(8,128)(2,1)S(1)}, u32[]{:S(2)}, u32[]{:S(2)}) collective-permute-start(bf16[208,768]{1,0:T(8,128)(2,1)S(1)} %get-tuple-element.14), channel_id=1, source_target_pairs={{0,48},{1,49},{2,50},{3,51},{4,52},{5,53},{6,54},{7,55},{8,11},{9,... | collective-permute-start | bytes 958472 | tf_op jit(solution)/shard_map/ppermute | solution.py:377
  64.0 10.8 %collective-permute-start.7 = (bf16[208,768]{1,0:T(8,128)(2,1)S(1)}, bf16[208,768]{1,0:T(8,128)(2,1)S(1)}, u32[]{:S(2)}, u32[]{:S(2)}) collective-permute-start(bf16[208,768]{1,0:T(8,128)(2,1)S(1)} %get-tuple-element.14), channel_id=1, source_target_pairs={{0,16},{1,17},{2,18},{3,19},{4,20},{5,21},{6,22},{7,23},{8,9},{9,1... | collective-permute-start | bytes 958472 | tf_op jit(solution)/shard_map/ppermute | solution.py:377
  64.0 10.8 %collective-permute-start.9 = (bf16[208,768]{1,0:T(8,128)(2,1)S(1)}, bf16[208,768]{1,0:T(8,128)(2,1)S(1)}, u32[]{:S(2)}, u32[]{:S(2)}) collective-permute-start(bf16[208,768]{1,0:T(8,128)(2,1)S(1)} %get-tuple-element.14), channel_id=1, source_target_pairs={{0,32},{1,33},{2,34},{3,35},{4,36},{5,37},{6,38},{7,39},{8,10},{9,... | collective-permute-start | bytes 958472 | tf_op jit(solution)/shard_map/ppermute | solution.py:377
  74.8 2.2 %copy-start.5 = (bf16[2,112,192]{2,1,0:T(8,128)(2,1)S(1)}, bf16[2,112,192]{2,1,0:T(8,128)(2,1)}, u32[]{:S(2)}) copy-start(bf16[2,112,192]{2,1,0:T(8,128)(2,1)} %get-tuple-element.9) | copy-start | bytes 258052
  75.0 45.9 %copy-start = (bf16[4,208,768]{2,1,0:T(8,128)(2,1)}, bf16[4,208,768]{2,1,0:T(8,128)(2,1)S(1)}, u32[]{:S(2)}) copy-start(bf16[4,208,768]{2,1,0:T(8,128)(2,1)S(1)} %pad_maximum_fusion.refs_0_) | copy-start | bytes 3833860
  75.0 48.2 %collective-permute-start.11 = (bf16[4,208,768]{2,1,0:T(8,128)(2,1)S(1)}, bf16[4,208,768]{2,1,0:T(8,128)(2,1)S(1)}, u32[]{:S(2)}, u32[]{:S(2)}) collective-permute-start(bf16[4,208,768]{2,1,0:T(8,128)(2,1)S(1)} %pad_maximum_fusion.refs_0_), channel_id=1, source_target_pairs={{0,3},{1,0},{2,1},{3,2},{4,7},{5,4},{6,5},{7,6},{8,56},{9,57},{10,... | collective-permute-start | bytes 3833864 | tf_op jit(solution)/shard_map/ppermute | solution.py:383
  77.0 47.4 %collective-permute-start.10 = (bf16[4,208,768]{2,1,0:T(8,128)(2,1)S(1)}, bf16[4,208,768]{2,1,0:T(8,128)(2,1)}, u32[]{:S(2)}, u32[]{:S(2)}) collective-permute-start(bf16[4,208,768]{2,1,0:T(8,128)(2,1)S(1)} %pad_maximum_fusion.refs_0_), channel_id=1, source_target_pairs={{0,1},{1,2},{2,3},{3,0},{4,5},{5,6},{6,7},{7,4},{8,24},{9,25},{10,... | collective-permute-start | bytes 3833864 | tf_op jit(solution)/shard_map/ppermute | solution.py:382
  77.0 3.9 %collective-permute-start = (bf16[2,112,192]{2,1,0:T(8,128)(2,1)S(1)}, bf16[2,112,192]{2,1,0:T(8,128)(2,1)S(1)}, u32[]{:S(2)}, u32[]{:S(2)}) collective-permute-start(bf16[2,112,192]{2,1,0:T(8,128)(2,1)S(1)} %copy-done.5), channel_id=1, source_target_pairs={{0,4},{1,5},{2,6},{3,7},{4,0},{5,1},{6,2},{7,3},{8,12},{9,13},{10,... | collective-permute-start | bytes 258056 | tf_op jit(solution)/shard_map/ppermute | solution.py:369
  81.7 11.6 %collective-permute-start.3 = (bf16[2,2,112,192]{3,2,1,0:T(8,128)(2,1)}, bf16[2,2,112,192]{3,2,1,0:T(8,128)(2,1)}, u32[]{:S(2)}, u32[]{:S(2)}) collective-permute-start(bf16[2,2,112,192]{3,2,1,0:T(8,128)(2,1)} %pad_maximum_fusion.1.w0), channel_id=1, source_target_pairs={{0,3},{1,2},{2,1},{3,0},{4,7},{5,6},{6,5},{7,4},{8,11},{9,10},{10,... | collective-permute-start | bytes 516104 | tf_op jit(solution)/shard_map/ppermute | solution.py:371
  81.7 11.6 %collective-permute-start.2 = (bf16[2,2,112,192]{3,2,1,0:T(8,128)(2,1)}, bf16[2,2,112,192]{3,2,1,0:T(8,128)(2,1)}, u32[]{:S(2)}, u32[]{:S(2)}) collective-permute-start(bf16[2,2,112,192]{3,2,1,0:T(8,128)(2,1)} %pad_maximum_fusion.1.w0), channel_id=1, source_target_pairs={{0,2},{1,3},{2,0},{3,1},{4,6},{5,7},{6,4},{7,5},{8,10},{9,11},{10,... | collective-permute-start | bytes 516104 | tf_op jit(solution)/shard_map/ppermute | solution.py:371
  82.2 14.2 %collective-permute-start.1 = (bf16[2,2,112,192]{3,2,1,0:T(8,128)(2,1)}, bf16[2,2,112,192]{3,2,1,0:T(8,128)(2,1)}, u32[]{:S(2)}, u32[]{:S(2)}) collective-permute-start(bf16[2,2,112,192]{3,2,1,0:T(8,128)(2,1)} %pad_maximum_fusion.1.w0), channel_id=1, source_target_pairs={{0,1},{1,0},{2,3},{3,2},{4,5},{5,4},{6,7},{7,6},{8,9},{9,8},{10,11... | collective-permute-start | bytes 516104 | tf_op jit(solution)/shard_map/ppermute | solution.py:371
  96.3 0.9 copy-start.2
  104.0 42.6 %all-to-all-start.1 = ((bf16[256,2,768]{2,1,0:T(2,128)(2,1)}), bf16[256,2,768]{2,1,0:T(2,128)(2,1)S(1)}, u32[]{:S(2)}, u32[]{:S(2)}) async-start(bf16[256,2,768]{2,1,0:T(2,128)(2,1)} %mode.1), calls=%async_computation.1 | async-start | bytes 1572864 | tf_op jit(solution)/shard_map/all_to_all | solution.py:407
  120.8 22.2 %collective-permute-start.14 = (bf16[4,208,768]{2,1,0:T(8,128)(2,1)S(1)}, bf16[4,208,768]{2,1,0:T(8,128)(2,1)}, u32[]{:S(2)}, u32[]{:S(2)}) collective-permute-start(bf16[4,208,768]{2,1,0:T(8,128)(2,1)S(1)} %pad_maximum_fusion.refs_0_), channel_id=1, source_target_pairs={{0,8},{1,9},{2,10},{3,11},{4,12},{5,13},{6,14},{7,15},{8,0},{9,1},... | collective-permute-start | bytes 3833864 | tf_op jit(solution)/shard_map/ppermute | solution.py:408
  123.2 2.4 %copy-start.3 = (bf16[4,208,768]{2,1,0:T(8,128)(2,1)}, bf16[4,208,768]{2,1,0:T(8,128)(2,1)S(1)}, u32[]{:S(2)}) copy-start(bf16[4,208,768]{2,1,0:T(8,128)(2,1)S(1)} %collective-permute-done.11.refs_2_) | copy-start | bytes 3833860
  123.2 14.5 %collective-permute-start.13 = (bf16[2,208,768]{2,1,0:T(8,128)(2,1)S(1)}, bf16[2,208,768]{2,1,0:T(8,128)(2,1)}, u32[]{:S(2)}, u32[]{:S(2)}) collective-permute-start(bf16[2,208,768]{2,1,0:T(8,128)(2,1)S(1)} %slice.24), channel_id=1, source_target_pairs={{0,3},{1,0},{2,1},{3,2},{4,7},{5,4},{6,5},{7,6},{8,56},{9,57},{10,... | collective-permute-start | bytes 1916936 | tf_op jit(solution)/shard_map/ppermute | solution.py:384
  124.2 22.4 %collective-permute-start.16 = (bf16[4,208,768]{2,1,0:T(8,128)(2,1)S(1)}, bf16[4,208,768]{2,1,0:T(8,128)(2,1)}, u32[]{:S(2)}, u32[]{:S(2)}) collective-permute-start(bf16[4,208,768]{2,1,0:T(8,128)(2,1)S(1)} %collective-permute-done.11.refs_2_), channel_id=1, source_target_pairs={{0,8},{1,9},{2,10},{3,11},{4,12},{5,13},{6,14},{7,15},{8,0},{9,1},... | collective-permute-start | bytes 3833864 | tf_op jit(solution)/shard_map/ppermute | solution.py:408
  125.6 21.0 %collective-permute-start.15 = (bf16[4,208,768]{2,1,0:T(8,128)(2,1)}, bf16[4,208,768]{2,1,0:T(8,128)(2,1)}, u32[]{:S(2)}, u32[]{:S(2)}) collective-permute-start(bf16[4,208,768]{2,1,0:T(8,128)(2,1)} %collective-permute-done.10.refs_1_), channel_id=1, source_target_pairs={{0,8},{1,9},{2,10},{3,11},{4,12},{5,13},{6,14},{7,15},{8,0},{9,1},... | collective-permute-start | bytes 3833864 | tf_op jit(solution)/shard_map/ppermute | solution.py:408
  125.9 16.0 %collective-permute-start.12 = (bf16[2,208,768]{2,1,0:T(8,128)(2,1)S(1)}, bf16[2,208,768]{2,1,0:T(8,128)(2,1)}, u32[]{:S(2)}, u32[]{:S(2)}) collective-permute-start(bf16[2,208,768]{2,1,0:T(8,128)(2,1)S(1)} %slice.23), channel_id=1, source_target_pairs={{0,1},{1,2},{2,3},{3,0},{4,5},{5,6},{6,7},{7,4},{8,24},{9,25},{10,... | collective-permute-start | bytes 1916936 | tf_op jit(solution)/shard_map/ppermute | solution.py:384
  137.7 8.9 %collective-permute-start.18 = (bf16[2,208,768]{2,1,0:T(8,128)(2,1)}, bf16[2,208,768]{2,1,0:T(8,128)(2,1)}, u32[]{:S(2)}, u32[]{:S(2)}) collective-permute-start(bf16[2,208,768]{2,1,0:T(8,128)(2,1)} %collective-permute-done.13.refs_4_), channel_id=1, source_target_pairs={{0,8},{1,9},{2,10},{3,11},{4,12},{5,13},{6,14},{7,15},{8,0},{9,1},... | collective-permute-start | bytes 1916936 | tf_op jit(solution)/shard_map/ppermute | solution.py:408
  141.9 4.7 %collective-permute-start.17 = (bf16[2,208,768]{2,1,0:T(8,128)(2,1)}, bf16[2,208,768]{2,1,0:T(8,128)(2,1)}, u32[]{:S(2)}, u32[]{:S(2)}) collective-permute-start(bf16[2,208,768]{2,1,0:T(8,128)(2,1)} %collective-permute-done.12.refs_3_), channel_id=1, source_target_pairs={{0,8},{1,9},{2,10},{3,11},{4,12},{5,13},{6,14},{7,15},{8,0},{9,1},... | collective-permute-start | bytes 1916936 | tf_op jit(solution)/shard_map/ppermute | solution.py:408
  146.6 0.9 copy-start.1

commit v3 on v2

--- a/solution.py
+++ b/solution.py
@@ -201,12 +201,13 @@
     for i, w in enumerate(w_hbm):
         w_copies.append(pltpu.make_async_copy(w, weights.at[pl.ds(spot, w.shape[0])], w_sem.at[i]))
         spot += w.shape[0]
-    start(copies + w_copies)
+    start(copies)
     gain = gain_ref[...]
     shift = shift_ref[...]
     out_bias = bias_ref[...]
     for copy in copies:
         copy.wait()
+    start(w_copies)
     x = x_ref[...].reshape(2 * KW, C)
     for t in range(3):
         even, odd = [dot(th[t, p], x[KW * p : KW * p + KW]) + dot(tl[t, p], x[KW * p : KW * p + KW]) for p in range(2)]
@@ -222,8 +223,6 @@
         normed[rows, :] = jnp.concatenate(row_norm(parts, gain, shift), axis=1).astype(bf16)
         for j in range(6):
             summed[rows, 128 * j : 128 * j + 128] = parts[j] + out_bias[j : j + 1, :]
-    for copy in w_copies:
-        copy.wait()
 
     def out_copy(i, first, last):
         span = pl.ds(first, last - first)
@@ -235,7 +234,13 @@
         rows = pl.ds(pl.multiple_of(t * TILE, 16), TILE)
         tokens = normed[rows, :]
         acc = summed[rows, :]
-        for first in range(0, 32, 8):
+        for first, ready in zip(range(0, 32, 8), (w_copies[:2], w_copies[2:5], w_copies[5:7], w_copies[7:])):
+
+            @pl.when(t == 0)
+            def _():
+                for copy in ready:
+                    copy.wait()
+
             w1 = jnp.concatenate([weights[q, 0:BS, :] for q in range(first, first + 8)], axis=0)
             w2 = jnp.concatenate([weights[q, BS : 2 * BS, :] for q in range(first, first + 8)], axis=0)
             bias = jnp.concatenate(
@@ -294,10 +299,6 @@
 
 def block_moves(bits):
     return [(d, d ^ bits) for d in range(256)]
-
-
-def z_moves(bits):
-    return moves(lambda x, y, z, c: (x, y, z ^ bits, c))
 
 
 def near_moves(n):
@@ -331,7 +332,8 @@
 
     bias_rows = jnp.pad(dense_bias.reshape(1, 1, 12), ((0, 0), (0, 1), (0, C - 12)))
     shard = jnp.concatenate([dense_weights, bias_rows], axis=0)
-    one = lax.ppermute(shard, AXES, z_moves(1))
+    copies = jnp.broadcast_to(shard[None], (8,) + shard.shape)
+    stacked = lax.all_to_all(copies, ("zh", "zl"), split_axis=0, concat_axis=0, tiled=True)
 
     modes, base, packed = pl.pallas_call(
         lon_kernel,
@@ -362,10 +364,6 @@
         filter_two_bias[0],
     )
 
-    two = jnp.concatenate([shard, one], axis=0)
-    four = jnp.concatenate([two, lax.ppermute(two, AXES, z_moves(2))], axis=0)
-    eight = jnp.concatenate([four, lax.ppermute(four, AXES, z_moves(4))], axis=0)
-    stacked = eight.reshape(8, 13, 2, C)
     partner = lax.ppermute(packed, AXES, block_moves(4))
     pair = jnp.stack([packed, partner])
     filters = [pair] + [lax.ppermute(pair, AXES, block_moves(b)) for b in range(1, 4)]

time: 167 us -> 147 us (0.88)
  waiting for transfers between devices: 64.4 us -> 52.3 us
  starting transfers between devices: 60.8 us -> 54.4 us
    ppermute x3 -> x0, waiting for transfers between devices: 23.7 us -> none  [the longest x1 22.4 us: per_device(): lax.ppermute(four, AXES, z_moves(4))]
    ppermute x3 -> x0, starting transfers between devices: 11.9 us -> none  [the longest x1 6.28 us: per_device(): lax.ppermute(four, AXES, z_moves(4))]
    all_to_all x0 -> x1, starting transfers between devices: none -> 9 us  [per_device(): lax.all_to_all(copies, ('zh', 'zl'), split_axis=0, concat_axis=0, tiled=T...]
    ppermute x3, waiting for transfers between devices: 9.06 us -> 14.5 us  [per_device(): lax.ppermute(block, AXES, near_moves(n))]
    all_to_all x0 -> x1, waiting for transfers between devices: none -> 5.46 us  [per_device(): lax.all_to_all(copies, ('zh', 'zl'), split_axis=0, concat_axis=0, tiled=T...]
    all_to_all x1, starting transfers between devices: 14.3 us -> 9.77 us  [per_device(): moved = lax.all_to_all(modes, AXES, split_axis=0, concat_axis=0, tiled=True)]
  transfers between devices with their start and end apart: 21 -> 19, of which waited for: 10 -> 9; matrix products, arithmetic and copies ran while one was open for 2% -> 2% of each run, Pallas kernels for 8% -> 9%
where the time goes in v3:
time: 147 us
  starting transfers between devices  54.4 us (37%)
  waiting for transfers between devices  52.3 us (36%)
  Pallas kernels  32.9 us (22%)
  local copies, waits for them, and re-layouts  5.29 us (4%)
  other arithmetic  1.76 us (1%)
    pallas_call x1, Pallas kernels, per_device(): pl.pallas_call(tail_kernel, out_shape=shape((6 * W, 128), f32), in_specs=...  19.7 us
    all_to_all x1, starting transfers between devices, per_device(): lax.all_to_all(mixed, AXES, split_axis=0, concat_axis=0, tiled=True)  18 us
    ppermute x3, waiting for transfers between devices, per_device(): lax.ppermute(block, AXES, near_moves(n))  14.5 us
    ppermute x3, waiting for transfers between devices, per_device(): lax.ppermute(pair, AXES, block_moves(b))  11.4 us
    ppermute x1, waiting for transfers between devices, per_device(): lax.ppermute(right[2:], AXES, far_moves(-1))  11.1 us
    all_to_all x1, starting transfers between devices, per_device(): moved = lax.all_to_all(modes, AXES, split_axis=0, concat_axis=0, tiled=True)  9.77 us
    all_to_all x1, starting transfers between devices, per_device(): lax.all_to_all(copies, ('zh', 'zl'), split_axis=0, concat_axis=0, tiled=T...  9 us
    pallas_call x1, Pallas kernels, per_device(): mixed = mode_call(own, moved, lat_h, lat_l, tal_h, tal_l, *filters)  6.84 us
  transfers between devices with their start and end apart: 19, of which 9 were waited for; matrix products, arithmetic and copies ran while one was open for 2% of the time, Pallas kernels for 9%

profile of v3, /device:TPU:1, one launch (start us, length us, event | category | flops | bytes accessed | tf_op | source)
XLA Modules:
  0.0 147.0 jit_solution(7200882059371937150)
XLA Ops:
  0.0 0.8 fusion.2
  0.8 0.9 broadcast_in_dim.2
  1.7 9.0 %all-to-all-start.2 = ((bf16[8,13,2,768]{3,2,1,0:T(2,128)(2,1)}), bf16[8,13,2,768]{3,2,1,0:T(2,128)(2,1)S(1)}, u32[]{:S(2)}, u32[]{:S(2)}) async-start(bf16[8,13,2,768]{3,2,1,0:T(2,128)(2,1)} %broadcast_in_dim.2), calls=%async_computation.2 | async-start | bytes 638976 | tf_op jit(solution)/shard_map/all_to_all | solution.py:336
  10.7 6.4 %lon.1 = (bf16[256,2,768]{2,1,0:T(2,128)(2,1)}, f32[5400,128]{1,0:T(8,128)}, bf16[2,112,192]{2,1,0:T(8,128)(2,1)}) custom-call(f32[5400,128]{1,0:T(8,128)} %bitcast.20, f32[6,128]{1,0:T(8,128)} %bitcast.28, f32[6,128]{1,0:T(8,128)} %bitcast.29, bf16[2,256,512]{2,1,0:T(8,128)(2,1)} %constant.30.clone.th_hbm, bf16[2,256,512]{2,1,0:T(8,128)(2,1)} %constant.31.clone.tl_hbm, ...), custom_call_target="tpu_custom_call" | custom-call | tf_op jit(solution)/shard_map/lon/pallas_call | solution.py:338
  17.1 5.5 %all-to-all-done.2 = bf16[8,13,2,768]{3,2,1,0:T(2,128)(2,1)S(1)} async-done(((bf16[8,13,2,768]{3,2,1,0:T(2,128)(2,1)}), bf16[8,13,2,768]{3,2,1,0:T(2,128)(2,1)S(1)}, u32[]{:S(2)}, u32[]{:S(2)}) %all-to-all-start.2) | async-done | bytes 319520 | tf_op jit(solution)/shard_map/all_to_all | solution.py:336
  22.6 9.8 %all-to-all-start = ((bf16[256,2,768]{2,1,0:T(2,128)(2,1)}), bf16[256,2,768]{2,1,0:T(2,128)(2,1)S(1)}, u32[]{:S(2)}, u32[]{:S(2)}) async-start(bf16[256,2,768]{2,1,0:T(2,128)(2,1)} %get-tuple-element.8), calls=%async_computation | async-start | bytes 1572864 | tf_op jit(solution)/shard_map/all_to_all | solution.py:377
  32.4 1.3 slice_reduce_fusion.1
  33.9 2.6 %collective-permute-start.5 = (bf16[208,768]{1,0:T(8,128)(2,1)S(1)}, bf16[208,768]{1,0:T(8,128)(2,1)S(1)}, u32[]{:S(2)}, u32[]{:S(2)}) collective-permute-start(bf16[208,768]{1,0:T(8,128)(2,1)S(1)} %get-tuple-element.14), channel_id=1, source_target_pairs={{0,48},{1,49},{2,50},{3,51},{4,52},{5,53},{6,54},{7,55},{8,11},{9,... | collective-permute-start | bytes 958472 | tf_op jit(solution)/shard_map/ppermute | solution.py:375
  36.5 1.8 %collective-permute-start.6 = (bf16[208,768]{1,0:T(8,128)(2,1)S(1)}, bf16[208,768]{1,0:T(8,128)(2,1)S(1)}, u32[]{:S(2)}, u32[]{:S(2)}) collective-permute-start(bf16[208,768]{1,0:T(8,128)(2,1)S(1)} %get-tuple-element.14), channel_id=1, source_target_pairs={{0,32},{1,33},{2,34},{3,35},{4,36},{5,37},{6,38},{7,39},{8,10},{9,... | collective-permute-start | bytes 958472 | tf_op jit(solution)/shard_map/ppermute | solution.py:375
  38.3 10.8 %collective-permute-done.5 = bf16[208,768]{1,0:T(8,128)(2,1)S(1)} collective-permute-done((bf16[208,768]{1,0:T(8,128)(2,1)S(1)}, bf16[208,768]{1,0:T(8,128)(2,1)S(1)}, u32[]{:S(2)}, u32[]{:S(2)}) %collective-permute-start.5) | collective-permute-done | bytes 319520 | tf_op jit(solution)/shard_map/ppermute | solution.py:375
  49.1 3.7 %collective-permute-done.4 = bf16[208,768]{1,0:T(8,128)(2,1)S(1)} collective-permute-done((bf16[208,768]{1,0:T(8,128)(2,1)S(1)}, bf16[208,768]{1,0:T(8,128)(2,1)S(1)}, u32[]{:S(2)}, u32[]{:S(2)}) %collective-permute-start.4) | collective-permute-done | bytes 319520 | tf_op jit(solution)/shard_map/ppermute | solution.py:375
  53.0 2.5 %collective-permute-start.8 = (bf16[4,208,768]{2,1,0:T(8,128)(2,1)S(1)}, bf16[4,208,768]{2,1,0:T(8,128)(2,1)S(1)}, u32[]{:S(2)}, u32[]{:S(2)}) collective-permute-start(bf16[4,208,768]{2,1,0:T(8,128)(2,1)S(1)} %pad_maximum_fusion.refs_0_), channel_id=1, source_target_pairs={{0,3},{1,0},{2,1},{3,2},{4,7},{5,4},{6,5},{7,6},{8,56},{9,57},{10,... | collective-permute-start | bytes 3833864 | tf_op jit(solution)/shard_map/ppermute | solution.py:381
  56.1 3.4 %collective-permute-done = bf16[2,112,192]{2,1,0:T(8,128)(2,1)S(1)} collective-permute-done((bf16[2,112,192]{2,1,0:T(8,128)(2,1)S(1)}, bf16[2,112,192]{2,1,0:T(8,128)(2,1)S(1)}, u32[]{:S(2)}, u32[]{:S(2)}) %collective-permute-start) | collective-permute-done | bytes 86048 | tf_op jit(solution)/shard_map/ppermute | solution.py:367
  59.5 0.7 pad_maximum_fusion.1.w0
  60.3 3.2 %collective-permute-start.1 = (bf16[2,2,112,192]{3,2,1,0:T(8,128)(2,1)}, bf16[2,2,112,192]{3,2,1,0:T(8,128)(2,1)}, u32[]{:S(2)}, u32[]{:S(2)}) collective-permute-start(bf16[2,2,112,192]{3,2,1,0:T(8,128)(2,1)} %pad_maximum_fusion.1.w0), channel_id=1, source_target_pairs={{0,1},{1,0},{2,3},{3,2},{4,5},{5,4},{6,7},{7,6},{8,9},{9,8},{10,11... | collective-permute-start | bytes 516104 | tf_op jit(solution)/shard_map/ppermute | solution.py:369
  63.5 8.3 %collective-permute-done.3.w3 = bf16[2,2,112,192]{3,2,1,0:T(8,128)(2,1)} collective-permute-done((bf16[2,2,112,192]{3,2,1,0:T(8,128)(2,1)}, bf16[2,2,112,192]{3,2,1,0:T(8,128)(2,1)}, u32[]{:S(2)}, u32[]{:S(2)}) %collective-permute-start.3) | collective-permute-done | bytes 172064 | tf_op jit(solution)/shard_map/ppermute | solution.py:369
  71.8 3.0 %collective-permute-done.1.w1 = bf16[2,2,112,192]{3,2,1,0:T(8,128)(2,1)} collective-permute-done((bf16[2,2,112,192]{3,2,1,0:T(8,128)(2,1)}, bf16[2,2,112,192]{3,2,1,0:T(8,128)(2,1)}, u32[]{:S(2)}, u32[]{:S(2)}) %collective-permute-start.1) | collective-permute-done | bytes 172064 | tf_op jit(solution)/shard_map/ppermute | solution.py:369
  74.9 0.9 copy-done.2
  75.7 6.8 %mode.1 = bf16[256,2,768]{2,1,0:T(2,128)(2,1)} custom-call(s32[1]{0:T(128)} %bitcast.own_ref, bf16[256,2,768]{2,1,0:T(2,128)(2,1)} %copy-done.2, bf16[512,512]{1,0:T(8,128)(2,1)} %constant.32.clone.fh_hbm, bf16[512,512]{1,0:T(8,128)(2,1)} %constant.33.clone.fl_hbm, bf16[2,256,256]{2,1,0:T(8,128)(2,1)} %constant.34.clone.gh_hbm, ...), custom_call_target="tpu_custom_call" | custom-call | tf_op jit(solution)/shard_map/mode/pallas_call | solution.py:403
  82.6 18.0 %all-to-all-start.1 = ((bf16[256,2,768]{2,1,0:T(2,128)(2,1)}), bf16[256,2,768]{2,1,0:T(2,128)(2,1)S(1)}, u32[]{:S(2)}, u32[]{:S(2)}) async-start(bf16[256,2,768]{2,1,0:T(2,128)(2,1)} %mode.1), calls=%async_computation.1 | async-start | bytes 1572864 | tf_op jit(solution)/shard_map/all_to_all | solution.py:405
  100.6 2.2 %collective-permute-start.11 = (bf16[4,208,768]{2,1,0:T(8,128)(2,1)S(1)}, bf16[4,208,768]{2,1,0:T(8,128)(2,1)}, u32[]{:S(2)}, u32[]{:S(2)}) collective-permute-start(bf16[4,208,768]{2,1,0:T(8,128)(2,1)S(1)} %pad_maximum_fusion.refs_0_), channel_id=1, source_target_pairs={{0,8},{1,9},{2,10},{3,11},{4,12},{5,13},{6,14},{7,15},{8,0},{9,1},... | collective-permute-start | bytes 3833864 | tf_op jit(solution)/shard_map/ppermute | solution.py:406
  102.8 0.9 collective-permute-start.10
  103.8 1.1 slice.23
  104.9 0.7 collective-permute-start.9
  105.6 0.6 collective-permute-start.13
  106.2 11.1 %collective-permute-done.10.refs_4_ = bf16[2,208,768]{2,1,0:T(8,128)(2,1)} collective-permute-done((bf16[2,208,768]{2,1,0:T(8,128)(2,1)S(1)}, bf16[2,208,768]{2,1,0:T(8,128)(2,1)}, u32[]{:S(2)}, u32[]{:S(2)}) %collective-permute-start.10) | collective-permute-done | bytes 639008 | tf_op jit(solution)/shard_map/ppermute | solution.py:382
  117.3 1.4 collective-permute-start.15
  118.7 2.3 %collective-permute-done.9.refs_3_ = bf16[2,208,768]{2,1,0:T(8,128)(2,1)} collective-permute-done((bf16[2,208,768]{2,1,0:T(8,128)(2,1)S(1)}, bf16[2,208,768]{2,1,0:T(8,128)(2,1)}, u32[]{:S(2)}, u32[]{:S(2)}) %collective-permute-start.9) | collective-permute-done | bytes 639008 | tf_op jit(solution)/shard_map/ppermute | solution.py:382
  121.0 1.1 collective-permute-start.14
  122.1 4.1 %all-to-all-done.1.x_hbm = bf16[256,2,768]{2,1,0:T(2,128)(2,1)S(1)} async-done(((bf16[256,2,768]{2,1,0:T(2,128)(2,1)}), bf16[256,2,768]{2,1,0:T(2,128)(2,1)S(1)}, u32[]{:S(2)}, u32[]{:S(2)}) %all-to-all-start.1) | async-done | bytes 786464 | tf_op jit(solution)/shard_map/all_to_all | solution.py:405
  126.3 0.9 copy-done.1
  127.1 19.7 %tail.1 = f32[5400,128]{1,0:T(8,128)} custom-call(bf16[256,2,768]{2,1,0:T(2,128)(2,1)} %copy-done.1, bf16[3,2,152,256]{3,2,1,0:T(8,128)(2,1)} %constant.36.clone.th_hbm, bf16[3,2,152,256]{3,2,1,0:T(8,128)(2,1)} %constant.37.clone.tl_hbm, f32[5400,128]{1,0:T(8,128)} %get-tuple-element.10.base_hbm, f32[6,128]{1,0:T(8,128)} %bitcast.30, f32[6,128]{1,0:T(8,128)} %bitcast.31, ...), custom_call_target="tpu_custom_call" | custom-call | tf_op jit(solution)/shard_map/tail/pallas_call | solution.py:408
  (31 shorter events, 1.1 us)
Async XLA Ops:
  1.7 20.8 %all-to-all-start.2 = ((bf16[8,13,2,768]{3,2,1,0:T(2,128)(2,1)}), bf16[8,13,2,768]{3,2,1,0:T(2,128)(2,1)S(1)}, u32[]{:S(2)}, u32[]{:S(2)}) async-start(bf16[8,13,2,768]{3,2,1,0:T(2,128)(2,1)} %broadcast_in_dim.2), calls=%async_computation.2 | async-start | bytes 638976 | tf_op jit(solution)/shard_map/all_to_all | solution.py:336
  22.6 52.3 %all-to-all-start = ((bf16[256,2,768]{2,1,0:T(2,128)(2,1)}), bf16[256,2,768]{2,1,0:T(2,128)(2,1)S(1)}, u32[]{:S(2)}, u32[]{:S(2)}) async-start(bf16[256,2,768]{2,1,0:T(2,128)(2,1)} %get-tuple-element.8), calls=%async_computation | async-start | bytes 1572864 | tf_op jit(solution)/shard_map/all_to_all | solution.py:377
  33.9 15.2 %collective-permute-start.5 = (bf16[208,768]{1,0:T(8,128)(2,1)S(1)}, bf16[208,768]{1,0:T(8,128)(2,1)S(1)}, u32[]{:S(2)}, u32[]{:S(2)}) collective-permute-start(bf16[208,768]{1,0:T(8,128)(2,1)S(1)} %get-tuple-element.14), channel_id=1, source_target_pairs={{0,48},{1,49},{2,50},{3,51},{4,52},{5,53},{6,54},{7,55},{8,11},{9,... | collective-permute-start | bytes 958472 | tf_op jit(solution)/shard_map/ppermute | solution.py:375
  36.5 16.3 %collective-permute-start.4 = (bf16[208,768]{1,0:T(8,128)(2,1)S(1)}, bf16[208,768]{1,0:T(8,128)(2,1)S(1)}, u32[]{:S(2)}, u32[]{:S(2)}) collective-permute-start(bf16[208,768]{1,0:T(8,128)(2,1)S(1)} %get-tuple-element.14), channel_id=1, source_target_pairs={{0,16},{1,17},{2,18},{3,19},{4,20},{5,21},{6,22},{7,23},{8,9},{9,1... | collective-permute-start | bytes 958472 | tf_op jit(solution)/shard_map/ppermute | solution.py:375
  36.5 16.3 %collective-permute-start.6 = (bf16[208,768]{1,0:T(8,128)(2,1)S(1)}, bf16[208,768]{1,0:T(8,128)(2,1)S(1)}, u32[]{:S(2)}, u32[]{:S(2)}) collective-permute-start(bf16[208,768]{1,0:T(8,128)(2,1)S(1)} %get-tuple-element.14), channel_id=1, source_target_pairs={{0,32},{1,33},{2,34},{3,35},{4,36},{5,37},{6,38},{7,39},{8,10},{9,... | collective-permute-start | bytes 958472 | tf_op jit(solution)/shard_map/ppermute | solution.py:375
  52.8 2.7 %copy-start.4 = (bf16[2,112,192]{2,1,0:T(8,128)(2,1)S(1)}, bf16[2,112,192]{2,1,0:T(8,128)(2,1)}, u32[]{:S(2)}) copy-start(bf16[2,112,192]{2,1,0:T(8,128)(2,1)} %get-tuple-element.9) | copy-start | bytes 258052
  53.0 47.6 %copy-start = (bf16[4,208,768]{2,1,0:T(8,128)(2,1)}, bf16[4,208,768]{2,1,0:T(8,128)(2,1)S(1)}, u32[]{:S(2)}) copy-start(bf16[4,208,768]{2,1,0:T(8,128)(2,1)S(1)} %pad_maximum_fusion.refs_0_) | copy-start | bytes 3833860
  53.0 49.8 %collective-permute-start.8 = (bf16[4,208,768]{2,1,0:T(8,128)(2,1)S(1)}, bf16[4,208,768]{2,1,0:T(8,128)(2,1)S(1)}, u32[]{:S(2)}, u32[]{:S(2)}) collective-permute-start(bf16[4,208,768]{2,1,0:T(8,128)(2,1)S(1)} %pad_maximum_fusion.refs_0_), channel_id=1, source_target_pairs={{0,3},{1,0},{2,1},{3,2},{4,7},{5,4},{6,5},{7,6},{8,56},{9,57},{10,... | collective-permute-start | bytes 3833864 | tf_op jit(solution)/shard_map/ppermute | solution.py:381
  55.5 48.3 %collective-permute-start.7 = (bf16[4,208,768]{2,1,0:T(8,128)(2,1)S(1)}, bf16[4,208,768]{2,1,0:T(8,128)(2,1)}, u32[]{:S(2)}, u32[]{:S(2)}) collective-permute-start(bf16[4,208,768]{2,1,0:T(8,128)(2,1)S(1)} %pad_maximum_fusion.refs_0_), channel_id=1, source_target_pairs={{0,1},{1,2},{2,3},{3,0},{4,5},{5,6},{6,7},{7,4},{8,24},{9,25},{10,... | collective-permute-start | bytes 3833864 | tf_op jit(solution)/shard_map/ppermute | solution.py:380
  55.5 3.9 %collective-permute-start = (bf16[2,112,192]{2,1,0:T(8,128)(2,1)S(1)}, bf16[2,112,192]{2,1,0:T(8,128)(2,1)S(1)}, u32[]{:S(2)}, u32[]{:S(2)}) collective-permute-start(bf16[2,112,192]{2,1,0:T(8,128)(2,1)S(1)} %copy-done.4), channel_id=1, source_target_pairs={{0,4},{1,5},{2,6},{3,7},{4,0},{5,1},{6,2},{7,3},{8,12},{9,13},{10,... | collective-permute-start | bytes 258056 | tf_op jit(solution)/shard_map/ppermute | solution.py:367
  60.2 11.6 %collective-permute-start.3 = (bf16[2,2,112,192]{3,2,1,0:T(8,128)(2,1)}, bf16[2,2,112,192]{3,2,1,0:T(8,128)(2,1)}, u32[]{:S(2)}, u32[]{:S(2)}) collective-permute-start(bf16[2,2,112,192]{3,2,1,0:T(8,128)(2,1)} %pad_maximum_fusion.1.w0), channel_id=1, source_target_pairs={{0,3},{1,2},{2,1},{3,0},{4,7},{5,6},{6,5},{7,4},{8,11},{9,10},{10,... | collective-permute-start | bytes 516104 | tf_op jit(solution)/shard_map/ppermute | solution.py:369
  60.2 11.6 %collective-permute-start.2 = (bf16[2,2,112,192]{3,2,1,0:T(8,128)(2,1)}, bf16[2,2,112,192]{3,2,1,0:T(8,128)(2,1)}, u32[]{:S(2)}, u32[]{:S(2)}) collective-permute-start(bf16[2,2,112,192]{3,2,1,0:T(8,128)(2,1)} %pad_maximum_fusion.1.w0), channel_id=1, source_target_pairs={{0,2},{1,3},{2,0},{3,1},{4,6},{5,7},{6,4},{7,5},{8,10},{9,11},{10,... | collective-permute-start | bytes 516104 | tf_op jit(solution)/shard_map/ppermute | solution.py:369
  60.3 14.6 %collective-permute-start.1 = (bf16[2,2,112,192]{3,2,1,0:T(8,128)(2,1)}, bf16[2,2,112,192]{3,2,1,0:T(8,128)(2,1)}, u32[]{:S(2)}, u32[]{:S(2)}) collective-permute-start(bf16[2,2,112,192]{3,2,1,0:T(8,128)(2,1)} %pad_maximum_fusion.1.w0), channel_id=1, source_target_pairs={{0,1},{1,0},{2,3},{3,2},{4,5},{5,4},{6,7},{7,6},{8,9},{9,8},{10,11... | collective-permute-start | bytes 516104 | tf_op jit(solution)/shard_map/ppermute | solution.py:369
  74.9 0.9 copy-start.2
  82.6 43.6 %all-to-all-start.1 = ((bf16[256,2,768]{2,1,0:T(2,128)(2,1)}), bf16[256,2,768]{2,1,0:T(2,128)(2,1)S(1)}, u32[]{:S(2)}, u32[]{:S(2)}) async-start(bf16[256,2,768]{2,1,0:T(2,128)(2,1)} %mode.1), calls=%async_computation.1 | async-start | bytes 1572864 | tf_op jit(solution)/shard_map/all_to_all | solution.py:405
  100.6 21.5 %collective-permute-start.11 = (bf16[4,208,768]{2,1,0:T(8,128)(2,1)S(1)}, bf16[4,208,768]{2,1,0:T(8,128)(2,1)}, u32[]{:S(2)}, u32[]{:S(2)}) collective-permute-start(bf16[4,208,768]{2,1,0:T(8,128)(2,1)S(1)} %pad_maximum_fusion.refs_0_), channel_id=1, source_target_pairs={{0,8},{1,9},{2,10},{3,11},{4,12},{5,13},{6,14},{7,15},{8,0},{9,1},... | collective-permute-start | bytes 3833864 | tf_op jit(solution)/shard_map/ppermute | solution.py:406
  102.8 2.8 %copy-start.3 = (bf16[4,208,768]{2,1,0:T(8,128)(2,1)}, bf16[4,208,768]{2,1,0:T(8,128)(2,1)S(1)}, u32[]{:S(2)}) copy-start(bf16[4,208,768]{2,1,0:T(8,128)(2,1)S(1)} %collective-permute-done.8.refs_2_) | copy-start | bytes 3833860
  102.8 14.5 %collective-permute-start.10 = (bf16[2,208,768]{2,1,0:T(8,128)(2,1)S(1)}, bf16[2,208,768]{2,1,0:T(8,128)(2,1)}, u32[]{:S(2)}, u32[]{:S(2)}) collective-permute-start(bf16[2,208,768]{2,1,0:T(8,128)(2,1)S(1)} %slice.24), channel_id=1, source_target_pairs={{0,3},{1,0},{2,1},{3,2},{4,7},{5,4},{6,5},{7,6},{8,56},{9,57},{10,... | collective-permute-start | bytes 1916936 | tf_op jit(solution)/shard_map/ppermute | solution.py:382
  104.9 16.1 %collective-permute-start.9 = (bf16[2,208,768]{2,1,0:T(8,128)(2,1)S(1)}, bf16[2,208,768]{2,1,0:T(8,128)(2,1)}, u32[]{:S(2)}, u32[]{:S(2)}) collective-permute-start(bf16[2,208,768]{2,1,0:T(8,128)(2,1)S(1)} %slice.23), channel_id=1, source_target_pairs={{0,1},{1,2},{2,3},{3,0},{4,5},{5,6},{6,7},{7,4},{8,24},{9,25},{10,... | collective-permute-start | bytes 1916936 | tf_op jit(solution)/shard_map/ppermute | solution.py:382
  105.6 20.6 %collective-permute-start.13 = (bf16[4,208,768]{2,1,0:T(8,128)(2,1)S(1)}, bf16[4,208,768]{2,1,0:T(8,128)(2,1)}, u32[]{:S(2)}, u32[]{:S(2)}) collective-permute-start(bf16[4,208,768]{2,1,0:T(8,128)(2,1)S(1)} %collective-permute-done.8.refs_2_), channel_id=1, source_target_pairs={{0,8},{1,9},{2,10},{3,11},{4,12},{5,13},{6,14},{7,15},{8,0},{9,1},... | collective-permute-start | bytes 3833864 | tf_op jit(solution)/shard_map/ppermute | solution.py:406
  106.2 20.1 %collective-permute-start.12 = (bf16[4,208,768]{2,1,0:T(8,128)(2,1)}, bf16[4,208,768]{2,1,0:T(8,128)(2,1)}, u32[]{:S(2)}, u32[]{:S(2)}) collective-permute-start(bf16[4,208,768]{2,1,0:T(8,128)(2,1)} %collective-permute-done.7.refs_1_), channel_id=1, source_target_pairs={{0,8},{1,9},{2,10},{3,11},{4,12},{5,13},{6,14},{7,15},{8,0},{9,1},... | collective-permute-start | bytes 3833864 | tf_op jit(solution)/shard_map/ppermute | solution.py:406
  117.3 8.9 %collective-permute-start.15 = (bf16[2,208,768]{2,1,0:T(8,128)(2,1)}, bf16[2,208,768]{2,1,0:T(8,128)(2,1)}, u32[]{:S(2)}, u32[]{:S(2)}) collective-permute-start(bf16[2,208,768]{2,1,0:T(8,128)(2,1)} %collective-permute-done.10.refs_4_), channel_id=1, source_target_pairs={{0,8},{1,9},{2,10},{3,11},{4,12},{5,13},{6,14},{7,15},{8,0},{9,1},... | collective-permute-start | bytes 1916936 | tf_op jit(solution)/shard_map/ppermute | solution.py:406
  121.0 5.2 %collective-permute-start.14 = (bf16[2,208,768]{2,1,0:T(8,128)(2,1)}, bf16[2,208,768]{2,1,0:T(8,128)(2,1)}, u32[]{:S(2)}, u32[]{:S(2)}) collective-permute-start(bf16[2,208,768]{2,1,0:T(8,128)(2,1)} %collective-permute-done.9.refs_3_), channel_id=1, source_target_pairs={{0,8},{1,9},{2,10},{3,11},{4,12},{5,13},{6,14},{7,15},{8,0},{9,1},... | collective-permute-start | bytes 1916936 | tf_op jit(solution)/shard_map/ppermute | solution.py:406
  126.2 0.9 copy-start.1

commit v4 on v3

--- a/solution.py
+++ b/solution.py
@@ -194,7 +194,9 @@
 def tail_kernel(x_hbm, th_hbm, tl_hbm, base_hbm, gain_ref, shift_ref, bias_ref, *refs):
     w_hbm, out_hbm = refs[:10], refs[10]
     x_ref, th, tl, base, weights, normed, summed, result, sem, w_sem, out_sem = refs[11:]
-    pairs = [(x_hbm, x_ref), (th_hbm, th), (tl_hbm, tl), (base_hbm, base)]
+    pairs = [(x_hbm, x_ref), (th_hbm, th), (tl_hbm, tl)]
+    for p, q in ((0, 912), (2696, 3616), (912, 1808), (3616, 4512), (1808, 2696), (4512, 5400)):
+        pairs.append((base_hbm.at[pl.ds(p, q - p)], base.at[pl.ds(p, q - p)]))
     copies = [pltpu.make_async_copy(source, target, sem.at[i]) for i, (source, target) in enumerate(pairs)]
     w_copies = []
     spot = 0
@@ -205,11 +207,14 @@
     gain = gain_ref[...]
     shift = shift_ref[...]
     out_bias = bias_ref[...]
-    for copy in copies:
+    for copy in copies[:5]:
         copy.wait()
     start(w_copies)
     x = x_ref[...].reshape(2 * KW, C)
     for t in range(3):
+        if t:
+            copies[2 * t + 3].wait()
+            copies[2 * t + 4].wait()
         even, odd = [dot(th[t, p], x[KW * p : KW * p + KW]) + dot(tl[t, p], x[KW * p : KW * p + KW]) for p in range(2)]
         parts = []
         for j in range(6):
@@ -295,6 +300,10 @@
 
 def moves(step):
     return [(d, index_of(*step(*place(d)))) for d in range(256)]
+
+
+def z_moves(bits):
+    return moves(lambda x, y, z, c: (x, y, z ^ bits, c))
 
 
 def block_moves(bits):
@@ -332,8 +341,8 @@
 
     bias_rows = jnp.pad(dense_bias.reshape(1, 1, 12), ((0, 0), (0, 1), (0, C - 12)))
     shard = jnp.concatenate([dense_weights, bias_rows], axis=0)
-    copies = jnp.broadcast_to(shard[None], (8,) + shard.shape)
-    stacked = lax.all_to_all(copies, ("zh", "zl"), split_axis=0, concat_axis=0, tiled=True)
+    shard = lax.optimization_barrier(shard)
+    one = lax.ppermute(shard, AXES, z_moves(4))
 
     modes, base, packed = pl.pallas_call(
         lon_kernel,
@@ -364,6 +373,11 @@
         filter_two_bias[0],
     )
 
+    pair_rows = lax.optimization_barrier(jnp.concatenate([shard, one], axis=0))
+    two = lax.ppermute(pair_rows, AXES, z_moves(2))
+    four_rows = lax.optimization_barrier(jnp.concatenate([pair_rows, two], axis=0))
+    four = lax.ppermute(four_rows, AXES, z_moves(1))
+    stacked = jnp.concatenate([four_rows, four], axis=0).reshape(8, 13, 2, C)
     partner = lax.ppermute(packed, AXES, block_moves(4))
     pair = jnp.stack([packed, partner])
     filters = [pair] + [lax.ppermute(pair, AXES, block_moves(b)) for b in range(1, 4)]
@@ -419,7 +433,7 @@
             pltpu.VMEM((ROWS, C), bf16),
             pltpu.VMEM((ROWS, C), f32),
             pltpu.VMEM((6 * W, 128), f32),
-            pltpu.SemaphoreType.DMA((4,)),
+            pltpu.SemaphoreType.DMA((9,)),
             pltpu.SemaphoreType.DMA((10,)),
             pltpu.SemaphoreType.DMA((4,)),
         ],

time: 147 us -> 153 us (1.041)
  starting transfers between devices: 54.4 us -> 61.7 us
    ppermute x0 -> x3, starting transfers between devices: none -> 9.44 us  [the longest x1 7.81 us: per_device(): one = lax.ppermute(shard, AXES, z_moves(4))]
    all_to_all x1 -> x0, starting transfers between devices: 9 us -> none  [per_device(): lax.all_to_all(copies, ('zh', 'zl'), split_axis=0, concat_axis=0, tiled=T...]
    all_to_all x1, starting transfers between devices: 9.77 us -> 16.1 us  [per_device(): moved = lax.all_to_all(modes, AXES, split_axis=0, concat_axis=0, tiled=True)]
    all_to_all x1 -> x0, waiting for transfers between devices: 5.46 us -> none  [per_device(): lax.all_to_all(copies, ('zh', 'zl'), split_axis=0, concat_axis=0, tiled=T...]
    ppermute x0 -> x3, waiting for transfers between devices: none -> 4.96 us  [the longest x1 3.58 us: per_device(): two = lax.ppermute(pair_rows, AXES, z_moves(2))]
  transfers between devices with their start and end apart: 19 -> 21, of which waited for: 9 -> 10; matrix products, arithmetic and copies ran while one was open for 2% -> 3% of each run, Pallas kernels for 9% -> 9%
where the time goes in v4:
time: 153 us
  starting transfers between devices  61.7 us (40%)
  waiting for transfers between devices  51.1 us (33%)
  Pallas kernels  32.9 us (22%)
  local copies, waits for them, and re-layouts  4.38 us (3%)
  other arithmetic  2.49 us (2%)
    pallas_call x1, Pallas kernels, per_device(): pl.pallas_call(tail_kernel, out_shape=shape((6 * W, 128), f32), in_specs=...  19.7 us
    all_to_all x1, starting transfers between devices, per_device(): lax.all_to_all(mixed, AXES, split_axis=0, concat_axis=0, tiled=True)  18 us
    all_to_all x1, starting transfers between devices, per_device(): moved = lax.all_to_all(modes, AXES, split_axis=0, concat_axis=0, tiled=True)  16.1 us
    ppermute x3, waiting for transfers between devices, per_device(): lax.ppermute(block, AXES, near_moves(n))  14.4 us
    ppermute x3, waiting for transfers between devices, per_device(): lax.ppermute(pair, AXES, block_moves(b))  11.4 us
    ppermute x1, waiting for transfers between devices, per_device(): lax.ppermute(right[2:], AXES, far_moves(-1))  10.7 us
    ppermute x1, starting transfers between devices, per_device(): one = lax.ppermute(shard, AXES, z_moves(4))  7.81 us
    pallas_call x1, Pallas kernels, per_device(): mixed = mode_call(own, moved, lat_h, lat_l, tal_h, tal_l, *filters)  6.83 us
  transfers between devices with their start and end apart: 21, of which 10 were waited for; matrix products, arithmetic and copies ran while one was open for 3% of the time, Pallas kernels for 9%

profile of v4, /device:TPU:1, one launch (start us, length us, event | category | flops | bytes accessed | tf_op | source)
XLA Modules:
  0.0 153.0 jit_solution(15233244428047441500)
XLA Ops:
  0.0 0.8 fusion.2
  0.8 7.8 %collective-permute-start.4 = (bf16[13,2,768]{2,1,0:T(2,128)(2,1)S(1)}, bf16[13,2,768]{2,1,0:T(2,128)(2,1)S(1)}, u32[]{:S(2)}, u32[]{:S(2)}) collective-permute-start(bf16[13,2,768]{2,1,0:T(2,128)(2,1)S(1)} %fusion.2), channel_id=1, source_target_pairs={{0,128},{1,129},{2,130},{3,131},{4,132},{5,133},{6,134},{7,135},{8... | collective-permute-start | bytes 119816 | tf_op jit(solution)/shard_map/ppermute | solution.py:345
  8.6 1.4 collective-permute-done.4
  10.1 1.5 %collective-permute-start.5 = (bf16[26,2,768]{2,1,0:T(2,128)(2,1)S(1)}, bf16[26,2,768]{2,1,0:T(2,128)(2,1)S(1)}, u32[]{:S(2)}, u32[]{:S(2)}) collective-permute-start(bf16[26,2,768]{2,1,0:T(2,128)(2,1)S(1)} %pad_maximum_fusion.4), channel_id=1, source_target_pairs={{0,64},{1,65},{2,66},{3,67},{4,68},{5,69},{6,70},{7,71},{8,72},{9,... | collective-permute-start | bytes 239624 | tf_op jit(solution)/shard_map/ppermute | solution.py:377
  11.7 3.6 %collective-permute-done.5 = bf16[26,2,768]{2,1,0:T(2,128)(2,1)S(1)} collective-permute-done((bf16[26,2,768]{2,1,0:T(2,128)(2,1)S(1)}, bf16[26,2,768]{2,1,0:T(2,128)(2,1)S(1)}, u32[]{:S(2)}, u32[]{:S(2)}) %collective-permute-start.5) | collective-permute-done | bytes 79904 | tf_op jit(solution)/shard_map/ppermute | solution.py:377
  15.6 6.4 %lon.1 = (bf16[256,2,768]{2,1,0:T(2,128)(2,1)}, f32[5400,128]{1,0:T(8,128)}, bf16[2,112,192]{2,1,0:T(8,128)(2,1)}) custom-call(f32[5400,128]{1,0:T(8,128)} %bitcast.21, f32[6,128]{1,0:T(8,128)} %bitcast.31, f32[6,128]{1,0:T(8,128)} %bitcast.32, bf16[2,256,512]{2,1,0:T(8,128)(2,1)} %constant.30.clone.th_hbm, bf16[2,256,512]{2,1,0:T(8,128)(2,1)} %constant.31.clone.tl_hbm, ...), custom_call_target="tpu_custom_call" | custom-call | tf_op jit(solution)/shard_map/lon/pallas_call | solution.py:347
  21.9 16.1 %all-to-all-start = ((bf16[256,2,768]{2,1,0:T(2,128)(2,1)}), bf16[256,2,768]{2,1,0:T(2,128)(2,1)S(1)}, u32[]{:S(2)}, u32[]{:S(2)}) async-start(bf16[256,2,768]{2,1,0:T(2,128)(2,1)} %get-tuple-element.8), calls=%async_computation | async-start | bytes 1572864 | tf_op jit(solution)/shard_map/all_to_all | solution.py:391
  38.5 1.3 slice_reduce_fusion.1
  40.0 2.6 %collective-permute-start.8 = (bf16[208,768]{1,0:T(8,128)(2,1)S(1)}, bf16[208,768]{1,0:T(8,128)(2,1)S(1)}, u32[]{:S(2)}, u32[]{:S(2)}) collective-permute-start(bf16[208,768]{1,0:T(8,128)(2,1)S(1)} %get-tuple-element.14), channel_id=1, source_target_pairs={{0,48},{1,49},{2,50},{3,51},{4,52},{5,53},{6,54},{7,55},{8,11},{9,... | collective-permute-start | bytes 958472 | tf_op jit(solution)/shard_map/ppermute | solution.py:389
  42.7 1.8 %collective-permute-start.9 = (bf16[208,768]{1,0:T(8,128)(2,1)S(1)}, bf16[208,768]{1,0:T(8,128)(2,1)S(1)}, u32[]{:S(2)}, u32[]{:S(2)}) collective-permute-start(bf16[208,768]{1,0:T(8,128)(2,1)S(1)} %get-tuple-element.14), channel_id=1, source_target_pairs={{0,32},{1,33},{2,34},{3,35},{4,36},{5,37},{6,38},{7,39},{8,10},{9,... | collective-permute-start | bytes 958472 | tf_op jit(solution)/shard_map/ppermute | solution.py:389
  44.4 10.6 %collective-permute-done.8 = bf16[208,768]{1,0:T(8,128)(2,1)S(1)} collective-permute-done((bf16[208,768]{1,0:T(8,128)(2,1)S(1)}, bf16[208,768]{1,0:T(8,128)(2,1)S(1)}, u32[]{:S(2)}, u32[]{:S(2)}) %collective-permute-start.8) | collective-permute-done | bytes 319520 | tf_op jit(solution)/shard_map/ppermute | solution.py:389
  55.0 3.8 %collective-permute-done.7 = bf16[208,768]{1,0:T(8,128)(2,1)S(1)} collective-permute-done((bf16[208,768]{1,0:T(8,128)(2,1)S(1)}, bf16[208,768]{1,0:T(8,128)(2,1)S(1)}, u32[]{:S(2)}, u32[]{:S(2)}) %collective-permute-start.7) | collective-permute-done | bytes 319520 | tf_op jit(solution)/shard_map/ppermute | solution.py:389
  59.0 2.5 %collective-permute-start.11 = (bf16[4,208,768]{2,1,0:T(8,128)(2,1)S(1)}, bf16[4,208,768]{2,1,0:T(8,128)(2,1)S(1)}, u32[]{:S(2)}, u32[]{:S(2)}) collective-permute-start(bf16[4,208,768]{2,1,0:T(8,128)(2,1)S(1)} %pad_maximum_fusion.refs_0_), channel_id=1, source_target_pairs={{0,3},{1,0},{2,1},{3,2},{4,7},{5,4},{6,5},{7,6},{8,56},{9,57},{10,... | collective-permute-start | bytes 3833864 | tf_op jit(solution)/shard_map/ppermute | solution.py:395
  62.1 3.3 %collective-permute-done = bf16[2,112,192]{2,1,0:T(8,128)(2,1)S(1)} collective-permute-done((bf16[2,112,192]{2,1,0:T(8,128)(2,1)S(1)}, bf16[2,112,192]{2,1,0:T(8,128)(2,1)S(1)}, u32[]{:S(2)}, u32[]{:S(2)}) %collective-permute-start) | collective-permute-done | bytes 86048 | tf_op jit(solution)/shard_map/ppermute | solution.py:381
  65.4 0.7 pad_maximum_fusion.2.w0
  66.4 3.0 %collective-permute-start.1 = (bf16[2,2,112,192]{3,2,1,0:T(8,128)(2,1)}, bf16[2,2,112,192]{3,2,1,0:T(8,128)(2,1)}, u32[]{:S(2)}, u32[]{:S(2)}) collective-permute-start(bf16[2,2,112,192]{3,2,1,0:T(8,128)(2,1)} %pad_maximum_fusion.2.w0), channel_id=1, source_target_pairs={{0,1},{1,0},{2,3},{3,2},{4,5},{5,4},{6,7},{7,6},{8,9},{9,8},{10,11... | collective-permute-start | bytes 516104 | tf_op jit(solution)/shard_map/ppermute | solution.py:383
  69.4 8.4 %collective-permute-done.3.w3 = bf16[2,2,112,192]{3,2,1,0:T(8,128)(2,1)} collective-permute-done((bf16[2,2,112,192]{3,2,1,0:T(8,128)(2,1)}, bf16[2,2,112,192]{3,2,1,0:T(8,128)(2,1)}, u32[]{:S(2)}, u32[]{:S(2)}) %collective-permute-start.3) | collective-permute-done | bytes 172064 | tf_op jit(solution)/shard_map/ppermute | solution.py:383
  77.8 3.0 %collective-permute-done.1.w1 = bf16[2,2,112,192]{3,2,1,0:T(8,128)(2,1)} collective-permute-done((bf16[2,2,112,192]{3,2,1,0:T(8,128)(2,1)}, bf16[2,2,112,192]{3,2,1,0:T(8,128)(2,1)}, u32[]{:S(2)}, u32[]{:S(2)}) %collective-permute-start.1) | collective-permute-done | bytes 172064 | tf_op jit(solution)/shard_map/ppermute | solution.py:383
  80.8 0.9 copy-done.2
  81.7 6.8 %mode.1 = bf16[256,2,768]{2,1,0:T(2,128)(2,1)} custom-call(s32[1]{0:T(128)} %bitcast.own_ref, bf16[256,2,768]{2,1,0:T(2,128)(2,1)} %copy-done.2, bf16[512,512]{1,0:T(8,128)(2,1)} %constant.32.clone.fh_hbm, bf16[512,512]{1,0:T(8,128)(2,1)} %constant.33.clone.fl_hbm, bf16[2,256,256]{2,1,0:T(8,128)(2,1)} %constant.34.clone.gh_hbm, ...), custom_call_target="tpu_custom_call" | custom-call | tf_op jit(solution)/shard_map/mode/pallas_call | solution.py:417
  88.5 18.0 %all-to-all-start.1 = ((bf16[256,2,768]{2,1,0:T(2,128)(2,1)}), bf16[256,2,768]{2,1,0:T(2,128)(2,1)S(1)}, u32[]{:S(2)}, u32[]{:S(2)}) async-start(bf16[256,2,768]{2,1,0:T(2,128)(2,1)} %mode.1), calls=%async_computation.1 | async-start | bytes 1572864 | tf_op jit(solution)/shard_map/all_to_all | solution.py:419
  106.5 2.2 %collective-permute-start.14 = (bf16[4,208,768]{2,1,0:T(8,128)(2,1)S(1)}, bf16[4,208,768]{2,1,0:T(8,128)(2,1)}, u32[]{:S(2)}, u32[]{:S(2)}) collective-permute-start(bf16[4,208,768]{2,1,0:T(8,128)(2,1)S(1)} %pad_maximum_fusion.refs_0_), channel_id=1, source_target_pairs={{0,8},{1,9},{2,10},{3,11},{4,12},{5,13},{6,14},{7,15},{8,0},{9,1},... | collective-permute-start | bytes 3833864 | tf_op jit(solution)/shard_map/ppermute | solution.py:420
  108.8 0.9 collective-permute-start.13
  110.1 1.1 slice.23
  111.5 1.1 collective-permute-start.12
  112.6 10.7 %collective-permute-done.13.refs_4_ = bf16[2,208,768]{2,1,0:T(8,128)(2,1)} collective-permute-done((bf16[2,208,768]{2,1,0:T(8,128)(2,1)S(1)}, bf16[2,208,768]{2,1,0:T(8,128)(2,1)}, u32[]{:S(2)}, u32[]{:S(2)}) %collective-permute-start.13) | collective-permute-done | bytes 639008 | tf_op jit(solution)/shard_map/ppermute | solution.py:396
  123.3 1.4 collective-permute-start.18
  124.7 2.8 %collective-permute-done.12.refs_3_ = bf16[2,208,768]{2,1,0:T(8,128)(2,1)} collective-permute-done((bf16[2,208,768]{2,1,0:T(8,128)(2,1)S(1)}, bf16[2,208,768]{2,1,0:T(8,128)(2,1)}, u32[]{:S(2)}, u32[]{:S(2)}) %collective-permute-start.12) | collective-permute-done | bytes 639008 | tf_op jit(solution)/shard_map/ppermute | solution.py:396
  127.5 1.1 collective-permute-start.17
  128.5 3.7 %all-to-all-done.1.x_hbm = bf16[256,2,768]{2,1,0:T(2,128)(2,1)S(1)} async-done(((bf16[256,2,768]{2,1,0:T(2,128)(2,1)}), bf16[256,2,768]{2,1,0:T(2,128)(2,1)S(1)}, u32[]{:S(2)}, u32[]{:S(2)}) %all-to-all-start.1) | async-done | bytes 786464 | tf_op jit(solution)/shard_map/all_to_all | solution.py:419
  132.2 0.9 copy-done.1
  133.1 19.7 %tail.1 = f32[5400,128]{1,0:T(8,128)} custom-call(bf16[256,2,768]{2,1,0:T(2,128)(2,1)} %copy-done.1, bf16[3,2,152,256]{3,2,1,0:T(8,128)(2,1)} %constant.36.clone.th_hbm, bf16[3,2,152,256]{3,2,1,0:T(8,128)(2,1)} %constant.37.clone.tl_hbm, f32[5400,128]{1,0:T(8,128)} %get-tuple-element.10.base_hbm, f32[6,128]{1,0:T(8,128)} %bitcast.33, f32[6,128]{1,0:T(8,128)} %bitcast.34, ...), custom_call_target="tpu_custom_call" | custom-call | tf_op jit(solution)/shard_map/tail/pallas_call | solution.py:422
  (37 shorter events, 2.8 us)
Async XLA Ops:
  0.8 9.2 %collective-permute-start.4 = (bf16[13,2,768]{2,1,0:T(2,128)(2,1)S(1)}, bf16[13,2,768]{2,1,0:T(2,128)(2,1)S(1)}, u32[]{:S(2)}, u32[]{:S(2)}) collective-permute-start(bf16[13,2,768]{2,1,0:T(2,128)(2,1)S(1)} %fusion.2), channel_id=1, source_target_pairs={{0,128},{1,129},{2,130},{3,131},{4,132},{5,133},{6,134},{7,135},{8... | collective-permute-start | bytes 119816 | tf_op jit(solution)/shard_map/ppermute | solution.py:345
  10.1 5.1 %collective-permute-start.5 = (bf16[26,2,768]{2,1,0:T(2,128)(2,1)S(1)}, bf16[26,2,768]{2,1,0:T(2,128)(2,1)S(1)}, u32[]{:S(2)}, u32[]{:S(2)}) collective-permute-start(bf16[26,2,768]{2,1,0:T(2,128)(2,1)S(1)} %pad_maximum_fusion.4), channel_id=1, source_target_pairs={{0,64},{1,65},{2,66},{3,67},{4,68},{5,69},{6,70},{7,71},{8,72},{9,... | collective-permute-start | bytes 239624 | tf_op jit(solution)/shard_map/ppermute | solution.py:377
  15.5 22.6 %collective-permute-start.6 = (bf16[52,2,768]{2,1,0:T(2,128)(2,1)S(1)}, bf16[52,2,768]{2,1,0:T(2,128)(2,1)S(1)}, u32[]{:S(2)}, u32[]{:S(2)}) collective-permute-start(bf16[52,2,768]{2,1,0:T(2,128)(2,1)S(1)} %pad_maximum_fusion.3), channel_id=1, source_target_pairs={{0,4},{1,5},{2,6},{3,7},{4,0},{5,1},{6,2},{7,3},{8,12},{9,13},{10,... | collective-permute-start | bytes 479240 | tf_op jit(solution)/shard_map/ppermute | solution.py:379
  21.9 58.9 %all-to-all-start = ((bf16[256,2,768]{2,1,0:T(2,128)(2,1)}), bf16[256,2,768]{2,1,0:T(2,128)(2,1)S(1)}, u32[]{:S(2)}, u32[]{:S(2)}) async-start(bf16[256,2,768]{2,1,0:T(2,128)(2,1)} %get-tuple-element.8), calls=%async_computation | async-start | bytes 1572864 | tf_op jit(solution)/shard_map/all_to_all | solution.py:391
  40.0 15.0 %collective-permute-start.8 = (bf16[208,768]{1,0:T(8,128)(2,1)S(1)}, bf16[208,768]{1,0:T(8,128)(2,1)S(1)}, u32[]{:S(2)}, u32[]{:S(2)}) collective-permute-start(bf16[208,768]{1,0:T(8,128)(2,1)S(1)} %get-tuple-element.14), channel_id=1, source_target_pairs={{0,48},{1,49},{2,50},{3,51},{4,52},{5,53},{6,54},{7,55},{8,11},{9,... | collective-permute-start | bytes 958472 | tf_op jit(solution)/shard_map/ppermute | solution.py:389
  42.7 16.1 %collective-permute-start.7 = (bf16[208,768]{1,0:T(8,128)(2,1)S(1)}, bf16[208,768]{1,0:T(8,128)(2,1)S(1)}, u32[]{:S(2)}, u32[]{:S(2)}) collective-permute-start(bf16[208,768]{1,0:T(8,128)(2,1)S(1)} %get-tuple-element.14), channel_id=1, source_target_pairs={{0,16},{1,17},{2,18},{3,19},{4,20},{5,21},{6,22},{7,23},{8,9},{9,1... | collective-permute-start | bytes 958472 | tf_op jit(solution)/shard_map/ppermute | solution.py:389
  42.7 16.1 %collective-permute-start.9 = (bf16[208,768]{1,0:T(8,128)(2,1)S(1)}, bf16[208,768]{1,0:T(8,128)(2,1)S(1)}, u32[]{:S(2)}, u32[]{:S(2)}) collective-permute-start(bf16[208,768]{1,0:T(8,128)(2,1)S(1)} %get-tuple-element.14), channel_id=1, source_target_pairs={{0,32},{1,33},{2,34},{3,35},{4,36},{5,37},{6,38},{7,39},{8,10},{9,... | collective-permute-start | bytes 958472 | tf_op jit(solution)/shard_map/ppermute | solution.py:389
  58.8 2.7 %copy-start.4 = (bf16[2,112,192]{2,1,0:T(8,128)(2,1)S(1)}, bf16[2,112,192]{2,1,0:T(8,128)(2,1)}, u32[]{:S(2)}) copy-start(bf16[2,112,192]{2,1,0:T(8,128)(2,1)} %get-tuple-element.9) | copy-start | bytes 258052
  59.0 47.6 %copy-start = (bf16[4,208,768]{2,1,0:T(8,128)(2,1)}, bf16[4,208,768]{2,1,0:T(8,128)(2,1)S(1)}, u32[]{:S(2)}) copy-start(bf16[4,208,768]{2,1,0:T(8,128)(2,1)S(1)} %pad_maximum_fusion.refs_0_) | copy-start | bytes 3833860
  59.0 49.8 %collective-permute-start.11 = (bf16[4,208,768]{2,1,0:T(8,128)(2,1)S(1)}, bf16[4,208,768]{2,1,0:T(8,128)(2,1)S(1)}, u32[]{:S(2)}, u32[]{:S(2)}) collective-permute-start(bf16[4,208,768]{2,1,0:T(8,128)(2,1)S(1)} %pad_maximum_fusion.refs_0_), channel_id=1, source_target_pairs={{0,3},{1,0},{2,1},{3,2},{4,7},{5,4},{6,5},{7,6},{8,56},{9,57},{10,... | collective-permute-start | bytes 3833864 | tf_op jit(solution)/shard_map/ppermute | solution.py:395
  61.5 48.6 %collective-permute-start.10 = (bf16[4,208,768]{2,1,0:T(8,128)(2,1)S(1)}, bf16[4,208,768]{2,1,0:T(8,128)(2,1)}, u32[]{:S(2)}, u32[]{:S(2)}) collective-permute-start(bf16[4,208,768]{2,1,0:T(8,128)(2,1)S(1)} %pad_maximum_fusion.refs_0_), channel_id=1, source_target_pairs={{0,1},{1,2},{2,3},{3,0},{4,5},{5,6},{6,7},{7,4},{8,24},{9,25},{10,... | collective-permute-start | bytes 3833864 | tf_op jit(solution)/shard_map/ppermute | solution.py:394
  61.5 3.9 %collective-permute-start = (bf16[2,112,192]{2,1,0:T(8,128)(2,1)S(1)}, bf16[2,112,192]{2,1,0:T(8,128)(2,1)S(1)}, u32[]{:S(2)}, u32[]{:S(2)}) collective-permute-start(bf16[2,112,192]{2,1,0:T(8,128)(2,1)S(1)} %copy-done.4), channel_id=1, source_target_pairs={{0,4},{1,5},{2,6},{3,7},{4,0},{5,1},{6,2},{7,3},{8,12},{9,13},{10,... | collective-permute-start | bytes 258056 | tf_op jit(solution)/shard_map/ppermute | solution.py:381
  66.2 11.6 %collective-permute-start.3 = (bf16[2,2,112,192]{3,2,1,0:T(8,128)(2,1)}, bf16[2,2,112,192]{3,2,1,0:T(8,128)(2,1)}, u32[]{:S(2)}, u32[]{:S(2)}) collective-permute-start(bf16[2,2,112,192]{3,2,1,0:T(8,128)(2,1)} %pad_maximum_fusion.2.w0), channel_id=1, source_target_pairs={{0,3},{1,2},{2,1},{3,0},{4,7},{5,6},{6,5},{7,4},{8,11},{9,10},{10,... | collective-permute-start | bytes 516104 | tf_op jit(solution)/shard_map/ppermute | solution.py:383
  66.2 11.6 %collective-permute-start.2 = (bf16[2,2,112,192]{3,2,1,0:T(8,128)(2,1)}, bf16[2,2,112,192]{3,2,1,0:T(8,128)(2,1)}, u32[]{:S(2)}, u32[]{:S(2)}) collective-permute-start(bf16[2,2,112,192]{3,2,1,0:T(8,128)(2,1)} %pad_maximum_fusion.2.w0), channel_id=1, source_target_pairs={{0,2},{1,3},{2,0},{3,1},{4,6},{5,7},{6,4},{7,5},{8,10},{9,11},{10,... | collective-permute-start | bytes 516104 | tf_op jit(solution)/shard_map/ppermute | solution.py:383
  66.4 14.4 %collective-permute-start.1 = (bf16[2,2,112,192]{3,2,1,0:T(8,128)(2,1)}, bf16[2,2,112,192]{3,2,1,0:T(8,128)(2,1)}, u32[]{:S(2)}, u32[]{:S(2)}) collective-permute-start(bf16[2,2,112,192]{3,2,1,0:T(8,128)(2,1)} %pad_maximum_fusion.2.w0), channel_id=1, source_target_pairs={{0,1},{1,0},{2,3},{3,2},{4,5},{5,4},{6,7},{7,6},{8,9},{9,8},{10,11... | collective-permute-start | bytes 516104 | tf_op jit(solution)/shard_map/ppermute | solution.py:383
  80.8 0.9 copy-start.2
  88.5 43.7 %all-to-all-start.1 = ((bf16[256,2,768]{2,1,0:T(2,128)(2,1)}), bf16[256,2,768]{2,1,0:T(2,128)(2,1)S(1)}, u32[]{:S(2)}, u32[]{:S(2)}) async-start(bf16[256,2,768]{2,1,0:T(2,128)(2,1)} %mode.1), calls=%async_computation.1 | async-start | bytes 1572864 | tf_op jit(solution)/shard_map/all_to_all | solution.py:419
  106.5 22.0 %collective-permute-start.14 = (bf16[4,208,768]{2,1,0:T(8,128)(2,1)S(1)}, bf16[4,208,768]{2,1,0:T(8,128)(2,1)}, u32[]{:S(2)}, u32[]{:S(2)}) collective-permute-start(bf16[4,208,768]{2,1,0:T(8,128)(2,1)S(1)} %pad_maximum_fusion.refs_0_), channel_id=1, source_target_pairs={{0,8},{1,9},{2,10},{3,11},{4,12},{5,13},{6,14},{7,15},{8,0},{9,1},... | collective-permute-start | bytes 3833864 | tf_op jit(solution)/shard_map/ppermute | solution.py:420
  108.8 2.5 %copy-start.3 = (bf16[4,208,768]{2,1,0:T(8,128)(2,1)}, bf16[4,208,768]{2,1,0:T(8,128)(2,1)S(1)}, u32[]{:S(2)}) copy-start(bf16[4,208,768]{2,1,0:T(8,128)(2,1)S(1)} %collective-permute-done.11.refs_2_) | copy-start | bytes 3833860
  108.8 14.5 %collective-permute-start.13 = (bf16[2,208,768]{2,1,0:T(8,128)(2,1)S(1)}, bf16[2,208,768]{2,1,0:T(8,128)(2,1)}, u32[]{:S(2)}, u32[]{:S(2)}) collective-permute-start(bf16[2,208,768]{2,1,0:T(8,128)(2,1)S(1)} %slice.24), channel_id=1, source_target_pairs={{0,3},{1,0},{2,1},{3,2},{4,7},{5,4},{6,5},{7,6},{8,56},{9,57},{10,... | collective-permute-start | bytes 1916936 | tf_op jit(solution)/shard_map/ppermute | solution.py:396
  109.8 22.4 %collective-permute-start.16 = (bf16[4,208,768]{2,1,0:T(8,128)(2,1)S(1)}, bf16[4,208,768]{2,1,0:T(8,128)(2,1)}, u32[]{:S(2)}, u32[]{:S(2)}) collective-permute-start(bf16[4,208,768]{2,1,0:T(8,128)(2,1)S(1)} %collective-permute-done.11.refs_2_), channel_id=1, source_target_pairs={{0,8},{1,9},{2,10},{3,11},{4,12},{5,13},{6,14},{7,15},{8,0},{9,1},... | collective-permute-start | bytes 3833864 | tf_op jit(solution)/shard_map/ppermute | solution.py:420
  111.3 21.0 %collective-permute-start.15 = (bf16[4,208,768]{2,1,0:T(8,128)(2,1)}, bf16[4,208,768]{2,1,0:T(8,128)(2,1)}, u32[]{:S(2)}, u32[]{:S(2)}) collective-permute-start(bf16[4,208,768]{2,1,0:T(8,128)(2,1)} %collective-permute-done.10.refs_1_), channel_id=1, source_target_pairs={{0,8},{1,9},{2,10},{3,11},{4,12},{5,13},{6,14},{7,15},{8,0},{9,1},... | collective-permute-start | bytes 3833864 | tf_op jit(solution)/shard_map/ppermute | solution.py:420
  111.5 16.0 %collective-permute-start.12 = (bf16[2,208,768]{2,1,0:T(8,128)(2,1)S(1)}, bf16[2,208,768]{2,1,0:T(8,128)(2,1)}, u32[]{:S(2)}, u32[]{:S(2)}) collective-permute-start(bf16[2,208,768]{2,1,0:T(8,128)(2,1)S(1)} %slice.23), channel_id=1, source_target_pairs={{0,1},{1,2},{2,3},{3,0},{4,5},{5,6},{6,7},{7,4},{8,24},{9,25},{10,... | collective-permute-start | bytes 1916936 | tf_op jit(solution)/shard_map/ppermute | solution.py:396
  123.3 8.9 %collective-permute-start.18 = (bf16[2,208,768]{2,1,0:T(8,128)(2,1)}, bf16[2,208,768]{2,1,0:T(8,128)(2,1)}, u32[]{:S(2)}, u32[]{:S(2)}) collective-permute-start(bf16[2,208,768]{2,1,0:T(8,128)(2,1)} %collective-permute-done.13.refs_4_), channel_id=1, source_target_pairs={{0,8},{1,9},{2,10},{3,11},{4,12},{5,13},{6,14},{7,15},{8,0},{9,1},... | collective-permute-start | bytes 1916936 | tf_op jit(solution)/shard_map/ppermute | solution.py:420
  127.5 4.7 %collective-permute-start.17 = (bf16[2,208,768]{2,1,0:T(8,128)(2,1)}, bf16[2,208,768]{2,1,0:T(8,128)(2,1)}, u32[]{:S(2)}, u32[]{:S(2)}) collective-permute-start(bf16[2,208,768]{2,1,0:T(8,128)(2,1)} %collective-permute-done.12.refs_3_), channel_id=1, source_target_pairs={{0,8},{1,9},{2,10},{3,11},{4,12},{5,13},{6,14},{7,15},{8,0},{9,1},... | collective-permute-start | bytes 1916936 | tf_op jit(solution)/shard_map/ppermute | solution.py:420
  132.2 0.9 copy-start.1

commit v5 on v4

--- a/solution.py
+++ b/solution.py
@@ -20,6 +20,7 @@
 C = 768
 BS = 96
 NB = 8
+BQ = 48
 TILE = 2 * PART
 ROWS = 3 * TILE
 norm_eps = 1e-05
@@ -192,17 +193,13 @@
 
 
 def tail_kernel(x_hbm, th_hbm, tl_hbm, base_hbm, gain_ref, shift_ref, bias_ref, *refs):
-    w_hbm, out_hbm = refs[:10], refs[10]
-    x_ref, th, tl, base, weights, normed, summed, result, sem, w_sem, out_sem = refs[11:]
+    w_hbm, out_hbm = refs[:8], refs[8]
+    x_ref, th, tl, base, weights, normed, summed, result, sem, w_sem, out_sem = refs[9:]
     pairs = [(x_hbm, x_ref), (th_hbm, th), (tl_hbm, tl)]
     for p, q in ((0, 912), (2696, 3616), (912, 1808), (3616, 4512), (1808, 2696), (4512, 5400)):
         pairs.append((base_hbm.at[pl.ds(p, q - p)], base.at[pl.ds(p, q - p)]))
     copies = [pltpu.make_async_copy(source, target, sem.at[i]) for i, (source, target) in enumerate(pairs)]
-    w_copies = []
-    spot = 0
-    for i, w in enumerate(w_hbm):
-        w_copies.append(pltpu.make_async_copy(w, weights.at[pl.ds(spot, w.shape[0])], w_sem.at[i]))
-        spot += w.shape[0]
+    w_copies = [pltpu.make_async_copy(w, weights.at[pl.ds(8 * i, 8)], w_sem.at[i]) for i, w in enumerate(w_hbm)]
     start(copies)
     gain = gain_ref[...]
     shift = shift_ref[...]
@@ -239,17 +236,18 @@
         rows = pl.ds(pl.multiple_of(t * TILE, 16), TILE)
         tokens = normed[rows, :]
         acc = summed[rows, :]
-        for first, ready in zip(range(0, 32, 8), (w_copies[:2], w_copies[2:5], w_copies[5:7], w_copies[7:])):
+        for first in range(0, 64, 16):
 
             @pl.when(t == 0)
             def _():
-                for copy in ready:
-                    copy.wait()
-
-            w1 = jnp.concatenate([weights[q, 0:BS, :] for q in range(first, first + 8)], axis=0)
-            w2 = jnp.concatenate([weights[q, BS : 2 * BS, :] for q in range(first, first + 8)], axis=0)
+                w_copies[first // 8].wait()
+                w_copies[first // 8 + 1].wait()
+
+            blocks = range(first, first + 16)
+            w1 = jnp.concatenate([weights[q, 0:BQ, :] for q in blocks], axis=0)
+            w2 = jnp.concatenate([weights[q, BQ : 2 * BQ, :] for q in blocks], axis=0)
             bias = jnp.concatenate(
-                [weights[q, 2 * BS : 2 * BS + 16, :].astype(f32)[0:1, 0:BS] for q in range(first, first + 8)], axis=1
+                [weights[q, 2 * BQ : 2 * BQ + 16, :].astype(f32)[0:1, 0:BQ] for q in blocks], axis=1
             )
             for c in range(3):
                 span = slice(256 * c, 256 * c + 256)
@@ -310,8 +308,9 @@
     return [(d, d ^ bits) for d in range(256)]
 
 
-def near_moves(n):
-    return moves(lambda x, y, z, c: (x, (y + n) % 4, z, c) if c == 0 else ((x + n) % 4, y, z, c))
+def near_moves(bits):
+    u, v = bits % 4, bits // 4
+    return moves(lambda x, y, z, c: (x, y ^ u, z ^ v, c) if c == 0 else (x ^ u, y, z ^ v, c))
 
 
 def far_moves(n):
@@ -375,26 +374,21 @@
 
     pair_rows = lax.optimization_barrier(jnp.concatenate([shard, one], axis=0))
     two = lax.ppermute(pair_rows, AXES, z_moves(2))
-    four_rows = lax.optimization_barrier(jnp.concatenate([pair_rows, two], axis=0))
-    four = lax.ppermute(four_rows, AXES, z_moves(1))
-    stacked = jnp.concatenate([four_rows, four], axis=0).reshape(8, 13, 2, C)
+    four_rows = lax.optimization_barrier(jnp.concatenate([pair_rows, two], axis=0)).reshape(4, 13, 2, C)
+    rows_in = four_rows[:, :12, 0, :].reshape(BQ, C)
+    rows_out = four_rows[:, :12, 1, :].reshape(BQ, C)
+    bias_row = jnp.pad(four_rows[:, 12, 0, :12].reshape(1, BQ), ((0, 15), (0, C - BQ)))
+    block = jnp.concatenate([rows_in, rows_out, bias_row], axis=0)
     partner = lax.ppermute(packed, AXES, block_moves(4))
     pair = jnp.stack([packed, partner])
     filters = [pair] + [lax.ppermute(pair, AXES, block_moves(b)) for b in range(1, 4)]
 
-    rows_in = stacked[:, :12, 0, :].reshape(BS, C)
-    rows_out = stacked[:, :12, 1, :].reshape(BS, C)
-    bias_row = jnp.pad(stacked[:, 12, 0, :12].reshape(1, BS), ((0, 15), (0, C - BS)))
-    block = jnp.concatenate([rows_in, rows_out, bias_row], axis=0)
-    near = [block] + [lax.ppermute(block, AXES, near_moves(n)) for n in (1, -1, 2)]
+    near = [block] + [lax.ppermute(block, AXES, near_moves(b)) for b in range(1, 8)]
 
     moved = lax.all_to_all(modes, AXES, split_axis=0, concat_axis=0, tiled=True)
 
     group = jnp.stack(near)
-    left = lax.ppermute(group, AXES, far_moves(1))
-    right = lax.ppermute(group, AXES, far_moves(-1))
-    across = [lax.ppermute(left[:2], AXES, far_moves(1)), lax.ppermute(right[2:], AXES, far_moves(-1))]
-    far = [group, left, right] + across
+    far = [group] + [lax.ppermute(group, AXES, far_moves(n)) for n in (1, -1, 2)]
 
     own = lax.axis_index(("zl", "x")).astype(jnp.int32).reshape(1)
     mode_call = pl.pallas_call(
@@ -422,19 +416,19 @@
     out = pl.pallas_call(
         tail_kernel,
         out_shape=shape((6 * W, 128), f32),
-        in_specs=anywhere(4) + vmem(3) + anywhere(10),
+        in_specs=anywhere(4) + vmem(3) + anywhere(8),
         out_specs=anywhere(1)[0],
         scratch_shapes=[
             pltpu.VMEM((KW, 2, C), bf16),
             pltpu.VMEM((3, 2, PART, KW), bf16),
             pltpu.VMEM((3, 2, PART, KW), bf16),
             pltpu.VMEM((6 * W, 128), f32),
-            pltpu.VMEM((32, 2 * BS + 16, C), bf16),
+            pltpu.VMEM((64, 2 * BQ + 16, C), bf16),
             pltpu.VMEM((ROWS, C), bf16),
             pltpu.VMEM((ROWS, C), f32),
             pltpu.VMEM((6 * W, 128), f32),
             pltpu.SemaphoreType.DMA((9,)),
-            pltpu.SemaphoreType.DMA((10,)),
+            pltpu.SemaphoreType.DMA((8,)),
             pltpu.SemaphoreType.DMA((4,)),
         ],
         compiler_params=params,

time: 153 us -> 190 us (1.24)
  waiting for transfers between devices: 51.1 us -> 78.1 us
  starting transfers between devices: 61.7 us -> 72.2 us
    ppermute x3, waiting for transfers between devices: 11.4 us -> 24.3 us  [per_device(): lax.ppermute(pair, AXES, block_moves(b))]
    all_to_all x1, waiting for transfers between devices: 3.65 us -> 14.6 us  [per_device(): lax.all_to_all(mixed, AXES, split_axis=0, concat_axis=0, tiled=True)]
    all_to_all x1, starting transfers between devices: 18 us -> 25.9 us  [per_device(): lax.all_to_all(mixed, AXES, split_axis=0, concat_axis=0, tiled=True)]
    ppermute x8 -> x10, starting transfers between devices: 9.03 us -> 16 us  [the longest x7 11.9 us: per_device(): lax.ppermute(block, AXES, near_moves(b))]
    ppermute x5 -> x4, waiting for transfers between devices: 0.01 us -> 6.84 us  [per_device(): other = [lax.ppermute(g, AXES, core_moves) for g in far]]
    ppermute x8 -> x10, waiting for transfers between devices: 27.9 us -> 23.5 us  [the longest x7 23.4 us: per_device(): lax.ppermute(block, AXES, near_moves(b))]
    ppermute x5 -> x4, starting transfers between devices: 5.28 us -> 3.06 us  [per_device(): other = [lax.ppermute(g, AXES, core_moves) for g in far]]
  transfers between devices with their start and end apart: 21 -> 22, of which waited for: 10 -> 14; matrix products, arithmetic and copies ran while one was open for 3% -> 0% of each run, Pallas kernels for 9% -> 7%
where the time goes in v5:
time: 190 us; the launch traced here: 189 us
  waiting for transfers between devices  78.1 us (41%)
  starting transfers between devices  72.2 us (38%)
  Pallas kernels  32.8 us (17%)
  local copies, waits for them, and re-layouts  3.75 us (2%)
  other arithmetic  1.91 us (1%)
    all_to_all x1, starting transfers between devices, per_device(): lax.all_to_all(mixed, AXES, split_axis=0, concat_axis=0, tiled=True)  25.9 us
    ppermute x3, waiting for transfers between devices, per_device(): lax.ppermute(pair, AXES, block_moves(b))  24.3 us
    ppermute x7, waiting for transfers between devices, per_device(): lax.ppermute(block, AXES, near_moves(b))  23.4 us
    pallas_call x1, Pallas kernels, per_device(): pl.pallas_call(tail_kernel, out_shape=shape((6 * W, 128), f32), in_specs=...  19.7 us
    all_to_all x1, starting transfers between devices, per_device(): moved = lax.all_to_all(modes, AXES, split_axis=0, concat_axis=0, tiled=True)  14.8 us
    all_to_all x1, waiting for transfers between devices, per_device(): lax.all_to_all(mixed, AXES, split_axis=0, concat_axis=0, tiled=True)  14.6 us
    ppermute x7, starting transfers between devices, per_device(): lax.ppermute(block, AXES, near_moves(b))  11.9 us
    ppermute x1, starting transfers between devices, per_device(): one = lax.ppermute(shard, AXES, z_moves(4))  7.81 us
  transfers between devices with their start and end apart: 22, of which 14 were waited for; matrix products, arithmetic and copies ran while one was open for 0% of the time, Pallas kernels for 7%

profile of v5, /device:TPU:1, one launch (start us, length us, event | category | flops | bytes accessed | tf_op | source)
XLA Modules:
  0.0 189.2 jit_solution(6955826856179467464)
XLA Ops:
  0.8 7.8 %collective-permute-start.4 = (bf16[13,2,768]{2,1,0:T(2,128)(2,1)S(1)}, bf16[13,2,768]{2,1,0:T(2,128)(2,1)S(1)}, u32[]{:S(2)}, u32[]{:S(2)}) collective-permute-start(bf16[13,2,768]{2,1,0:T(2,128)(2,1)S(1)} %fusion.2), channel_id=1, source_target_pairs={{0,128},{1,129},{2,130},{3,131},{4,132},{5,133},{6,134},{7,135},{8... | collective-permute-start | bytes 119816 | tf_op jit(solution)/shard_map/ppermute | solution.py:344
  8.6 1.4 collective-permute-done.4
  10.1 1.5 collective-permute-start.5
  11.7 3.6 %collective-permute-done.5 = bf16[26,2,768]{2,1,0:T(2,128)(2,1)S(1)} collective-permute-done((bf16[26,2,768]{2,1,0:T(2,128)(2,1)S(1)}, bf16[26,2,768]{2,1,0:T(2,128)(2,1)S(1)}, u32[]{:S(2)}, u32[]{:S(2)}) %collective-permute-start.5) | collective-permute-done | bytes 79904 | tf_op jit(solution)/shard_map/ppermute | solution.py:376
  16.3 1.3 collective-permute-start.6
  17.6 6.3 %lon.1 = (bf16[256,2,768]{2,1,0:T(2,128)(2,1)}, f32[5400,128]{1,0:T(8,128)}, bf16[2,112,192]{2,1,0:T(8,128)(2,1)}) custom-call(f32[5400,128]{1,0:T(8,128)} %bitcast.32, f32[6,128]{1,0:T(8,128)} %bitcast.42, f32[6,128]{1,0:T(8,128)} %bitcast.43, bf16[2,256,512]{2,1,0:T(8,128)(2,1)} %constant.30.clone.th_hbm, bf16[2,256,512]{2,1,0:T(8,128)(2,1)} %constant.31.clone.tl_hbm, ...), custom_call_target="tpu_custom_call" | custom-call | tf_op jit(solution)/shard_map/lon/pallas_call | solution.py:346
  23.9 14.8 %all-to-all-start = ((bf16[256,2,768]{2,1,0:T(2,128)(2,1)}), bf16[256,2,768]{2,1,0:T(2,128)(2,1)S(1)}, u32[]{:S(2)}, u32[]{:S(2)}) async-start(bf16[256,2,768]{2,1,0:T(2,128)(2,1)} %get-tuple-element.8), calls=%async_computation | async-start | bytes 1572864 | tf_op jit(solution)/shard_map/all_to_all | solution.py:388
  38.7 4.0 %collective-permute-start.11 = (bf16[112,768]{1,0:T(8,128)(2,1)S(1)}, bf16[112,768]{1,0:T(8,128)(2,1)S(1)}, u32[]{:S(2)}, u32[]{:S(2)}) collective-permute-start(bf16[112,768]{1,0:T(8,128)(2,1)S(1)} %fusion.1), channel_id=1, source_target_pairs={{0,36},{1,37},{2,38},{3,39},{4,32},{5,33},{6,34},{7,35},{8,14},{9,... | collective-permute-start | bytes 516104 | tf_op jit(solution)/shard_map/ppermute | solution.py:386
  42.9 1.4 collective-permute-start.9
  44.5 2.8 %collective-permute-start.7 = (bf16[112,768]{1,0:T(8,128)(2,1)S(1)}, bf16[112,768]{1,0:T(8,128)(2,1)S(1)}, u32[]{:S(2)}, u32[]{:S(2)}) collective-permute-start(bf16[112,768]{1,0:T(8,128)(2,1)S(1)} %fusion.1), channel_id=1, source_target_pairs={{0,32},{1,33},{2,34},{3,35},{4,36},{5,37},{6,38},{7,39},{8,10},{9,... | collective-permute-start | bytes 516104 | tf_op jit(solution)/shard_map/ppermute | solution.py:386
  47.3 4.9 %collective-permute-done.7 = bf16[112,768]{1,0:T(8,128)(2,1)S(1)} collective-permute-done((bf16[112,768]{1,0:T(8,128)(2,1)S(1)}, bf16[112,768]{1,0:T(8,128)(2,1)S(1)}, u32[]{:S(2)}, u32[]{:S(2)}) %collective-permute-start.7) | collective-permute-done | bytes 172064 | tf_op jit(solution)/shard_map/ppermute | solution.py:386
  52.3 2.1 %collective-permute-start.12 = (bf16[112,768]{1,0:T(8,128)(2,1)S(1)}, bf16[112,768]{1,0:T(8,128)(2,1)S(1)}, u32[]{:S(2)}, u32[]{:S(2)}) collective-permute-start(bf16[112,768]{1,0:T(8,128)(2,1)S(1)} %fusion.1), channel_id=1, source_target_pairs={{0,52},{1,53},{2,54},{3,55},{4,48},{5,49},{6,50},{7,51},{8,15},{9,... | collective-permute-start | bytes 516104 | tf_op jit(solution)/shard_map/ppermute | solution.py:386
  54.9 12.2 %collective-permute-done.9 = bf16[112,768]{1,0:T(8,128)(2,1)S(1)} collective-permute-done((bf16[112,768]{1,0:T(8,128)(2,1)S(1)}, bf16[112,768]{1,0:T(8,128)(2,1)S(1)}, u32[]{:S(2)}, u32[]{:S(2)}) %collective-permute-start.9) | collective-permute-done | bytes 172064 | tf_op jit(solution)/shard_map/ppermute | solution.py:386
  67.2 5.8 %collective-permute-done.12 = bf16[112,768]{1,0:T(8,128)(2,1)S(1)} collective-permute-done((bf16[112,768]{1,0:T(8,128)(2,1)S(1)}, bf16[112,768]{1,0:T(8,128)(2,1)S(1)}, u32[]{:S(2)}, u32[]{:S(2)}) %collective-permute-start.12) | collective-permute-done | bytes 172064 | tf_op jit(solution)/shard_map/ppermute | solution.py:386
  73.0 2.6 %collective-permute-start.15 = (bf16[8,112,768]{2,1,0:T(8,128)(2,1)S(1)}, bf16[8,112,768]{2,1,0:T(8,128)(2,1)S(1)}, u32[]{:S(2)}, u32[]{:S(2)}) collective-permute-start(bf16[8,112,768]{2,1,0:T(8,128)(2,1)S(1)} %bitcast_dynamic-update-slice_fusion.refs_0_), channel_id=1, source_target_pairs={{0,2},{1,3},{2,0},{3,1},{4,6},{5,7},{6,4},{7,5},{8,40},{9,41},{10,... | collective-permute-start | bytes 4128776 | tf_op jit(solution)/shard_map/ppermute | solution.py:391
  77.1 3.9 %collective-permute-done = bf16[2,112,192]{2,1,0:T(8,128)(2,1)S(1)} collective-permute-done((bf16[2,112,192]{2,1,0:T(8,128)(2,1)S(1)}, bf16[2,112,192]{2,1,0:T(8,128)(2,1)S(1)}, u32[]{:S(2)}, u32[]{:S(2)}) %collective-permute-start) | collective-permute-done | bytes 86048 | tf_op jit(solution)/shard_map/ppermute | solution.py:382
  81.8 1.8 collective-permute-start.2
  83.6 17.6 %collective-permute-done.3.w3 = bf16[2,2,112,192]{3,2,1,0:T(8,128)(2,1)} collective-permute-done((bf16[2,2,112,192]{3,2,1,0:T(8,128)(2,1)}, bf16[2,2,112,192]{3,2,1,0:T(8,128)(2,1)}, u32[]{:S(2)}, u32[]{:S(2)}) %collective-permute-start.3) | collective-permute-done | bytes 172064 | tf_op jit(solution)/shard_map/ppermute | solution.py:384
  101.2 1.2 collective-permute-start.1
  102.4 6.7 %collective-permute-done.1.w1 = bf16[2,2,112,192]{3,2,1,0:T(8,128)(2,1)} collective-permute-done((bf16[2,2,112,192]{3,2,1,0:T(8,128)(2,1)}, bf16[2,2,112,192]{3,2,1,0:T(8,128)(2,1)}, u32[]{:S(2)}, u32[]{:S(2)}) %collective-permute-start.1) | collective-permute-done | bytes 172064 | tf_op jit(solution)/shard_map/ppermute | solution.py:384
  109.1 0.9 copy-done.1
  110.0 6.8 %mode.1 = bf16[256,2,768]{2,1,0:T(2,128)(2,1)} custom-call(s32[1]{0:T(128)} %bitcast.own_ref, bf16[256,2,768]{2,1,0:T(2,128)(2,1)} %copy-done.1, bf16[512,512]{1,0:T(8,128)(2,1)} %constant.32.clone.fh_hbm, bf16[512,512]{1,0:T(8,128)(2,1)} %constant.33.clone.fl_hbm, bf16[2,256,256]{2,1,0:T(8,128)(2,1)} %constant.34.clone.gh_hbm, ...), custom_call_target="tpu_custom_call" | custom-call | tf_op jit(solution)/shard_map/mode/pallas_call | solution.py:411
  116.9 25.9 %all-to-all-start.1 = ((bf16[256,2,768]{2,1,0:T(2,128)(2,1)}), bf16[256,2,768]{2,1,0:T(2,128)(2,1)S(1)}, u32[]{:S(2)}, u32[]{:S(2)}) async-start(bf16[256,2,768]{2,1,0:T(2,128)(2,1)} %mode.1), calls=%async_computation.1 | async-start | bytes 1572864 | tf_op jit(solution)/shard_map/all_to_all | solution.py:413
  142.8 2.2 %collective-permute-start.16 = (bf16[8,112,768]{2,1,0:T(8,128)(2,1)S(1)}, bf16[8,112,768]{2,1,0:T(8,128)(2,1)S(1)}, u32[]{:S(2)}, u32[]{:S(2)}) collective-permute-start(bf16[8,112,768]{2,1,0:T(8,128)(2,1)S(1)} %bitcast_dynamic-update-slice_fusion.refs_0_), channel_id=1, source_target_pairs={{0,8},{1,9},{2,10},{3,11},{4,12},{5,13},{6,14},{7,15},{8,0},{9,1},... | collective-permute-start | bytes 4128776 | tf_op jit(solution)/shard_map/ppermute | solution.py:414
  145.9 1.9 %collective-permute-done.16.refs_4_ = bf16[8,112,768]{2,1,0:T(8,128)(2,1)S(1)} collective-permute-done((bf16[8,112,768]{2,1,0:T(8,128)(2,1)S(1)}, bf16[8,112,768]{2,1,0:T(8,128)(2,1)S(1)}, u32[]{:S(2)}, u32[]{:S(2)}) %collective-permute-start.16) | collective-permute-done | bytes 1376288 | tf_op jit(solution)/shard_map/ppermute | solution.py:414
  147.8 2.0 %collective-permute-done.19.refs_7_ = bf16[8,112,768]{2,1,0:T(8,128)(2,1)S(1)} collective-permute-done((bf16[8,112,768]{2,1,0:T(8,128)(2,1)S(1)}, bf16[8,112,768]{2,1,0:T(8,128)(2,1)S(1)}, u32[]{:S(2)}, u32[]{:S(2)}) %collective-permute-start.19) | collective-permute-done | bytes 1376288 | tf_op jit(solution)/shard_map/ppermute | solution.py:414
  149.8 2.0 %collective-permute-done.18.refs_6_ = bf16[8,112,768]{2,1,0:T(8,128)(2,1)S(1)} collective-permute-done((bf16[8,112,768]{2,1,0:T(8,128)(2,1)}, bf16[8,112,768]{2,1,0:T(8,128)(2,1)S(1)}, u32[]{:S(2)}, u32[]{:S(2)}) %collective-permute-start.18) | collective-permute-done | bytes 1376288 | tf_op jit(solution)/shard_map/ppermute | solution.py:414
  151.7 1.1 copy-done.6
  152.8 1.0 collective-permute-done.17.refs_5_
  153.8 14.6 %all-to-all-done.1.x_hbm = bf16[256,2,768]{2,1,0:T(2,128)(2,1)S(1)} async-done(((bf16[256,2,768]{2,1,0:T(2,128)(2,1)}), bf16[256,2,768]{2,1,0:T(2,128)(2,1)S(1)}, u32[]{:S(2)}, u32[]{:S(2)}) %all-to-all-start.1) | async-done | bytes 786464 | tf_op jit(solution)/shard_map/all_to_all | solution.py:413
  168.5 0.9 copy-done
  169.4 19.7 %tail.1 = f32[5400,128]{1,0:T(8,128)} custom-call(bf16[256,2,768]{2,1,0:T(2,128)(2,1)} %copy-done, bf16[3,2,152,256]{3,2,1,0:T(8,128)(2,1)} %constant.36.clone.th_hbm, bf16[3,2,152,256]{3,2,1,0:T(8,128)(2,1)} %constant.37.clone.tl_hbm, f32[5400,128]{1,0:T(8,128)} %get-tuple-element.10.base_hbm, f32[6,128]{1,0:T(8,128)} %bitcast.39, f32[6,128]{1,0:T(8,128)} %bitcast.40, ...), custom_call_target="tpu_custom_call" | custom-call | tf_op jit(solution)/shard_map/tail/pallas_call | solution.py:416
  (49 shorter events, 6.0 us)
Async XLA Ops:
  0.8 9.2 %collective-permute-start.4 = (bf16[13,2,768]{2,1,0:T(2,128)(2,1)S(1)}, bf16[13,2,768]{2,1,0:T(2,128)(2,1)S(1)}, u32[]{:S(2)}, u32[]{:S(2)}) collective-permute-start(bf16[13,2,768]{2,1,0:T(2,128)(2,1)S(1)} %fusion.2), channel_id=1, source_target_pairs={{0,128},{1,129},{2,130},{3,131},{4,132},{5,133},{6,134},{7,135},{8... | collective-permute-start | bytes 119816 | tf_op jit(solution)/shard_map/ppermute | solution.py:344
  10.1 5.1 %collective-permute-start.5 = (bf16[26,2,768]{2,1,0:T(2,128)(2,1)S(1)}, bf16[26,2,768]{2,1,0:T(2,128)(2,1)S(1)}, u32[]{:S(2)}, u32[]{:S(2)}) collective-permute-start(bf16[26,2,768]{2,1,0:T(2,128)(2,1)S(1)} %pad_maximum_fusion.2), channel_id=1, source_target_pairs={{0,64},{1,65},{2,66},{3,67},{4,68},{5,69},{6,70},{7,71},{8,72},{9,... | collective-permute-start | bytes 239624 | tf_op jit(solution)/shard_map/ppermute | solution.py:376
  16.3 28.2 %collective-permute-start.6 = (bf16[112,768]{1,0:T(8,128)(2,1)S(1)}, bf16[112,768]{1,0:T(8,128)(2,1)S(1)}, u32[]{:S(2)}, u32[]{:S(2)}) collective-permute-start(bf16[112,768]{1,0:T(8,128)(2,1)S(1)} %fusion.1), channel_id=1, source_target_pairs={{0,16},{1,17},{2,18},{3,19},{4,20},{5,21},{6,22},{7,23},{8,9},{9,8... | collective-permute-start | bytes 516104 | tf_op jit(solution)/shard_map/ppermute | solution.py:386
  23.9 85.2 %all-to-all-start = ((bf16[256,2,768]{2,1,0:T(2,128)(2,1)}), bf16[256,2,768]{2,1,0:T(2,128)(2,1)S(1)}, u32[]{:S(2)}, u32[]{:S(2)}) async-start(bf16[256,2,768]{2,1,0:T(2,128)(2,1)} %get-tuple-element.8), calls=%async_computation | async-start | bytes 1572864 | tf_op jit(solution)/shard_map/all_to_all | solution.py:388
  38.7 38.4 %copy-start.7 = (bf16[2,112,192]{2,1,0:T(8,128)(2,1)S(1)}, bf16[2,112,192]{2,1,0:T(8,128)(2,1)}, u32[]{:S(2)}) copy-start(bf16[2,112,192]{2,1,0:T(8,128)(2,1)} %get-tuple-element.9) | copy-start | bytes 258052
  38.7 28.4 %collective-permute-start.11 = (bf16[112,768]{1,0:T(8,128)(2,1)S(1)}, bf16[112,768]{1,0:T(8,128)(2,1)S(1)}, u32[]{:S(2)}, u32[]{:S(2)}) collective-permute-start(bf16[112,768]{1,0:T(8,128)(2,1)S(1)} %fusion.1), channel_id=1, source_target_pairs={{0,36},{1,37},{2,38},{3,39},{4,32},{5,33},{6,34},{7,35},{8,14},{9,... | collective-permute-start | bytes 516104 | tf_op jit(solution)/shard_map/ppermute | solution.py:386
  42.8 24.4 %collective-permute-start.10 = (bf16[112,768]{1,0:T(8,128)(2,1)S(1)}, bf16[112,768]{1,0:T(8,128)(2,1)S(1)}, u32[]{:S(2)}, u32[]{:S(2)}) collective-permute-start(bf16[112,768]{1,0:T(8,128)(2,1)S(1)} %fusion.1), channel_id=1, source_target_pairs={{0,20},{1,21},{2,22},{3,23},{4,16},{5,17},{6,18},{7,19},{8,13},{9,... | collective-permute-start | bytes 516104 | tf_op jit(solution)/shard_map/ppermute | solution.py:386
  42.9 24.3 %collective-permute-start.9 = (bf16[112,768]{1,0:T(8,128)(2,1)S(1)}, bf16[112,768]{1,0:T(8,128)(2,1)S(1)}, u32[]{:S(2)}, u32[]{:S(2)}) collective-permute-start(bf16[112,768]{1,0:T(8,128)(2,1)S(1)} %fusion.1), channel_id=1, source_target_pairs={{0,4},{1,5},{2,6},{3,7},{4,0},{5,1},{6,2},{7,3},{8,12},{9,13},{10,... | collective-permute-start | bytes 516104 | tf_op jit(solution)/shard_map/ppermute | solution.py:386
  44.2 10.6 %collective-permute-start.8 = (bf16[112,768]{1,0:T(8,128)(2,1)S(1)}, bf16[112,768]{1,0:T(8,128)(2,1)S(1)}, u32[]{:S(2)}, u32[]{:S(2)}) collective-permute-start(bf16[112,768]{1,0:T(8,128)(2,1)S(1)} %fusion.1), channel_id=1, source_target_pairs={{0,48},{1,49},{2,50},{3,51},{4,52},{5,53},{6,54},{7,55},{8,11},{9,... | collective-permute-start | bytes 516104 | tf_op jit(solution)/shard_map/ppermute | solution.py:386
  44.5 7.8 %collective-permute-start.7 = (bf16[112,768]{1,0:T(8,128)(2,1)S(1)}, bf16[112,768]{1,0:T(8,128)(2,1)S(1)}, u32[]{:S(2)}, u32[]{:S(2)}) collective-permute-start(bf16[112,768]{1,0:T(8,128)(2,1)S(1)} %fusion.1), channel_id=1, source_target_pairs={{0,32},{1,33},{2,34},{3,35},{4,36},{5,37},{6,38},{7,39},{8,10},{9,... | collective-permute-start | bytes 516104 | tf_op jit(solution)/shard_map/ppermute | solution.py:386
  52.3 20.7 %collective-permute-start.12 = (bf16[112,768]{1,0:T(8,128)(2,1)S(1)}, bf16[112,768]{1,0:T(8,128)(2,1)S(1)}, u32[]{:S(2)}, u32[]{:S(2)}) collective-permute-start(bf16[112,768]{1,0:T(8,128)(2,1)S(1)} %fusion.1), channel_id=1, source_target_pairs={{0,52},{1,53},{2,54},{3,55},{4,48},{5,49},{6,50},{7,51},{8,15},{9,... | collective-permute-start | bytes 516104 | tf_op jit(solution)/shard_map/ppermute | solution.py:386
  73.0 95.5 %copy-start.2 = (bf16[8,112,768]{2,1,0:T(8,128)(2,1)}, bf16[8,112,768]{2,1,0:T(8,128)(2,1)S(1)}, u32[]{:S(2)}) copy-start(bf16[8,112,768]{2,1,0:T(8,128)(2,1)S(1)} %bitcast_dynamic-update-slice_fusion.refs_0_) | copy-start | bytes 4128772
  73.0 72.0 %collective-permute-start.15 = (bf16[8,112,768]{2,1,0:T(8,128)(2,1)S(1)}, bf16[8,112,768]{2,1,0:T(8,128)(2,1)S(1)}, u32[]{:S(2)}, u32[]{:S(2)}) collective-permute-start(bf16[8,112,768]{2,1,0:T(8,128)(2,1)S(1)} %bitcast_dynamic-update-slice_fusion.refs_0_), channel_id=1, source_target_pairs={{0,2},{1,3},{2,0},{3,1},{4,6},{5,7},{6,4},{7,5},{8,40},{9,41},{10,... | collective-permute-start | bytes 4128776 | tf_op jit(solution)/shard_map/ppermute | solution.py:391
  75.6 69.5 %collective-permute-start.14 = (bf16[8,112,768]{2,1,0:T(8,128)(2,1)S(1)}, bf16[8,112,768]{2,1,0:T(8,128)(2,1)}, u32[]{:S(2)}, u32[]{:S(2)}) collective-permute-start(bf16[8,112,768]{2,1,0:T(8,128)(2,1)S(1)} %bitcast_dynamic-update-slice_fusion.refs_0_), channel_id=1, source_target_pairs={{0,3},{1,0},{2,1},{3,2},{4,7},{5,4},{6,5},{7,6},{8,56},{9,57},{10,... | collective-permute-start | bytes 4128776 | tf_op jit(solution)/shard_map/ppermute | solution.py:391
  76.4 69.1 %collective-permute-start.13 = (bf16[8,112,768]{2,1,0:T(8,128)(2,1)S(1)}, bf16[8,112,768]{2,1,0:T(8,128)(2,1)}, u32[]{:S(2)}, u32[]{:S(2)}) collective-permute-start(bf16[8,112,768]{2,1,0:T(8,128)(2,1)S(1)} %bitcast_dynamic-update-slice_fusion.refs_0_), channel_id=1, source_target_pairs={{0,1},{1,2},{2,3},{3,0},{4,5},{5,6},{6,7},{7,4},{8,24},{9,25},{10,... | collective-permute-start | bytes 4128776 | tf_op jit(solution)/shard_map/ppermute | solution.py:391
  77.1 3.9 %collective-permute-start = (bf16[2,112,192]{2,1,0:T(8,128)(2,1)S(1)}, bf16[2,112,192]{2,1,0:T(8,128)(2,1)S(1)}, u32[]{:S(2)}, u32[]{:S(2)}) collective-permute-start(bf16[2,112,192]{2,1,0:T(8,128)(2,1)S(1)} %copy-done.7), channel_id=1, source_target_pairs={{0,4},{1,5},{2,6},{3,7},{4,0},{5,1},{6,2},{7,3},{8,12},{9,13},{10,... | collective-permute-start | bytes 258056 | tf_op jit(solution)/shard_map/ppermute | solution.py:382
  81.8 19.4 %collective-permute-start.3 = (bf16[2,2,112,192]{3,2,1,0:T(8,128)(2,1)}, bf16[2,2,112,192]{3,2,1,0:T(8,128)(2,1)}, u32[]{:S(2)}, u32[]{:S(2)}) collective-permute-start(bf16[2,2,112,192]{3,2,1,0:T(8,128)(2,1)} %pad_maximum_fusion.w0), channel_id=1, source_target_pairs={{0,3},{1,2},{2,1},{3,0},{4,7},{5,6},{6,5},{7,4},{8,11},{9,10},{10,... | collective-permute-start | bytes 516104 | tf_op jit(solution)/shard_map/ppermute | solution.py:384
  81.8 20.6 %collective-permute-start.2 = (bf16[2,2,112,192]{3,2,1,0:T(8,128)(2,1)}, bf16[2,2,112,192]{3,2,1,0:T(8,128)(2,1)}, u32[]{:S(2)}, u32[]{:S(2)}) collective-permute-start(bf16[2,2,112,192]{3,2,1,0:T(8,128)(2,1)} %pad_maximum_fusion.w0), channel_id=1, source_target_pairs={{0,2},{1,3},{2,0},{3,1},{4,6},{5,7},{6,4},{7,5},{8,10},{9,11},{10,... | collective-permute-start | bytes 516104 | tf_op jit(solution)/shard_map/ppermute | solution.py:384
  101.2 7.9 %collective-permute-start.1 = (bf16[2,2,112,192]{3,2,1,0:T(8,128)(2,1)}, bf16[2,2,112,192]{3,2,1,0:T(8,128)(2,1)}, u32[]{:S(2)}, u32[]{:S(2)}) collective-permute-start(bf16[2,2,112,192]{3,2,1,0:T(8,128)(2,1)} %pad_maximum_fusion.w0), channel_id=1, source_target_pairs={{0,1},{1,0},{2,3},{3,2},{4,5},{5,4},{6,7},{7,6},{8,9},{9,8},{10,11... | collective-permute-start | bytes 516104 | tf_op jit(solution)/shard_map/ppermute | solution.py:384
  109.1 0.9 copy-start.1
  116.9 51.6 %all-to-all-start.1 = ((bf16[256,2,768]{2,1,0:T(2,128)(2,1)}), bf16[256,2,768]{2,1,0:T(2,128)(2,1)S(1)}, u32[]{:S(2)}, u32[]{:S(2)}) async-start(bf16[256,2,768]{2,1,0:T(2,128)(2,1)} %mode.1), calls=%async_computation.1 | async-start | bytes 1572864 | tf_op jit(solution)/shard_map/all_to_all | solution.py:413
  142.8 5.0 %collective-permute-start.16 = (bf16[8,112,768]{2,1,0:T(8,128)(2,1)S(1)}, bf16[8,112,768]{2,1,0:T(8,128)(2,1)S(1)}, u32[]{:S(2)}, u32[]{:S(2)}) collective-permute-start(bf16[8,112,768]{2,1,0:T(8,128)(2,1)S(1)} %bitcast_dynamic-update-slice_fusion.refs_0_), channel_id=1, source_target_pairs={{0,8},{1,9},{2,10},{3,11},{4,12},{5,13},{6,14},{7,15},{8,0},{9,1},... | collective-permute-start | bytes 4128776 | tf_op jit(solution)/shard_map/ppermute | solution.py:414
  145.0 23.4 %copy-start.3 = (bf16[8,112,768]{2,1,0:T(8,128)(2,1)}, bf16[8,112,768]{2,1,0:T(8,128)(2,1)S(1)}, u32[]{:S(2)}) copy-start(bf16[8,112,768]{2,1,0:T(8,128)(2,1)S(1)} %collective-permute-done.15.refs_3_) | copy-start | bytes 4128772
  145.0 4.7 %collective-permute-start.19 = (bf16[8,112,768]{2,1,0:T(8,128)(2,1)S(1)}, bf16[8,112,768]{2,1,0:T(8,128)(2,1)S(1)}, u32[]{:S(2)}, u32[]{:S(2)}) collective-permute-start(bf16[8,112,768]{2,1,0:T(8,128)(2,1)S(1)} %collective-permute-done.15.refs_3_), channel_id=1, source_target_pairs={{0,8},{1,9},{2,10},{3,11},{4,12},{5,13},{6,14},{7,15},{8,0},{9,1},... | collective-permute-start | bytes 4128776 | tf_op jit(solution)/shard_map/ppermute | solution.py:414
  145.2 6.6 %collective-permute-start.18 = (bf16[8,112,768]{2,1,0:T(8,128)(2,1)}, bf16[8,112,768]{2,1,0:T(8,128)(2,1)S(1)}, u32[]{:S(2)}, u32[]{:S(2)}) collective-permute-start(bf16[8,112,768]{2,1,0:T(8,128)(2,1)} %collective-permute-done.14.refs_2_), channel_id=1, source_target_pairs={{0,8},{1,9},{2,10},{3,11},{4,12},{5,13},{6,14},{7,15},{8,0},{9,1},... | collective-permute-start | bytes 4128776 | tf_op jit(solution)/shard_map/ppermute | solution.py:414
  145.6 8.3 %collective-permute-start.17 = (bf16[8,112,768]{2,1,0:T(8,128)(2,1)}, bf16[8,112,768]{2,1,0:T(8,128)(2,1)}, u32[]{:S(2)}, u32[]{:S(2)}) collective-permute-start(bf16[8,112,768]{2,1,0:T(8,128)(2,1)} %collective-permute-done.13.refs_1_), channel_id=1, source_target_pairs={{0,8},{1,9},{2,10},{3,11},{4,12},{5,13},{6,14},{7,15},{8,0},{9,1},... | collective-permute-start | bytes 4128776 | tf_op jit(solution)/shard_map/ppermute | solution.py:414
  147.8 3.9 %copy-start.4 = (bf16[8,112,768]{2,1,0:T(8,128)(2,1)}, bf16[8,112,768]{2,1,0:T(8,128)(2,1)S(1)}, u32[]{:S(2)}) copy-start(bf16[8,112,768]{2,1,0:T(8,128)(2,1)S(1)} %collective-permute-done.16.refs_4_) | copy-start | bytes 4128772
  149.8 2.0 %copy-start.5 = (bf16[8,112,768]{2,1,0:T(8,128)(2,1)}, bf16[8,112,768]{2,1,0:T(8,128)(2,1)S(1)}, u32[]{:S(2)}) copy-start(bf16[8,112,768]{2,1,0:T(8,128)(2,1)S(1)} %collective-permute-done.19.refs_7_) | copy-start | bytes 4128772
  151.7 1.1 copy-start.6
  168.5 0.9 copy-start

commit v6 on v4

--- a/solution.py
+++ b/solution.py
@@ -140,19 +140,18 @@
     store.wait()
 
 
-def mode_kernel(own_ref, x_hbm, fh_hbm, fl_hbm, gh_hbm, gl_hbm, w0, w1, w2, w3, out_ref, x_ref, fh, fl, gh, gl, w_all, zh, zl, sem):
-    pairs = [(x_hbm, x_ref), (fh_hbm, fh), (fl_hbm, fl)] + [(w, w_all.at[d]) for d, w in enumerate((w0, w1, w2, w3))]
+def mode_kernel(own_ref, x_ref, fh_hbm, fl_hbm, gh_hbm, gl_hbm, w0, w1, w2, w3, out_ref, fh, fl, gh, gl, w_all, zh, zl, sem):
+    pairs = [(fh_hbm, fh), (fl_hbm, fl)] + [(w, w_all.at[d]) for d, w in enumerate((w0, w1, w2, w3))]
     pairs += [(gh_hbm, gh), (gl_hbm, gl)]
     copies = [pltpu.make_async_copy(source, target, sem.at[i]) for i, (source, target) in enumerate(pairs)]
     start(copies)
     own = own_ref[0]
     copies[0].wait()
-    copies[1].wait()
     x = x_ref[...].reshape(2 * H, C)
     y = dot(fh[...], x)
-    copies[2].wait()
+    copies[1].wait()
     y = y + dot(fl[...], x)
-    for copy in copies[3:7]:
+    for copy in copies[2:6]:
         copy.wait()
 
     def layer(values, slot, i):
@@ -180,8 +179,8 @@
             spot = slice(H // 2 * part, H // 2 * part + H // 2)
             zh[parity, spot, :] = high[rows]
             zl[parity, spot, :] = low[rows]
+    copies[6].wait()
     copies[7].wait()
-    copies[8].wait()
     even, odd = [dot(gh[p], zh[p]) + dot(gh[p], zl[p]) + dot(gl[p], zh[p]) for p in range(2)]
     out_ref[0 : H // 2] = (even + odd).astype(bf16).reshape(H // 2, 2, C)
     out_ref[H // 2 : H] = (even - odd).astype(bf16).reshape(H // 2, 2, C)
@@ -191,10 +190,10 @@
     return 0.5 * x * (1.0 + lax.erf(x * 0.7071067811865476))
 
 
-def tail_kernel(x_hbm, th_hbm, tl_hbm, base_hbm, gain_ref, shift_ref, bias_ref, *refs):
+def tail_kernel(x_ref, th_hbm, tl_hbm, base_hbm, gain_ref, shift_ref, bias_ref, *refs):
     w_hbm, out_hbm = refs[:10], refs[10]
-    x_ref, th, tl, base, weights, normed, summed, result, sem, w_sem, out_sem = refs[11:]
-    pairs = [(x_hbm, x_ref), (th_hbm, th), (tl_hbm, tl)]
+    th, tl, base, weights, normed, summed, result, sem, w_sem, out_sem = refs[11:]
+    pairs = [(th_hbm, th), (tl_hbm, tl)]
     for p, q in ((0, 912), (2696, 3616), (912, 1808), (3616, 4512), (1808, 2696), (4512, 5400)):
         pairs.append((base_hbm.at[pl.ds(p, q - p)], base.at[pl.ds(p, q - p)]))
     copies = [pltpu.make_async_copy(source, target, sem.at[i]) for i, (source, target) in enumerate(pairs)]
@@ -207,14 +206,14 @@
     gain = gain_ref[...]
     shift = shift_ref[...]
     out_bias = bias_ref[...]
-    for copy in copies[:5]:
+    for copy in copies[:4]:
         copy.wait()
     start(w_copies)
     x = x_ref[...].reshape(2 * KW, C)
     for t in range(3):
         if t:
+            copies[2 * t + 2].wait()
             copies[2 * t + 3].wait()
-            copies[2 * t + 4].wait()
         even, odd = [dot(th[t, p], x[KW * p : KW * p + KW]) + dot(tl[t, p], x[KW * p : KW * p + KW]) for p in range(2)]
         parts = []
         for j in range(6):
@@ -286,6 +285,10 @@
 params = pltpu.CompilerParams(vmem_limit_bytes=56 * 2**20)
 
 
+def held(value):
+    return pltpu.with_memory_space_constraint(value, pltpu.VMEM)
+
+
 def place(index):
     lat, chan = divmod(index, 8)
     zh, rest = divmod(lat, 8)
@@ -311,7 +314,7 @@
 
 
 def near_moves(n):
-    return moves(lambda x, y, z, c: (x, (y + n) % 4, z, c) if c == 0 else ((x + n) % 4, y, z, c))
+    return moves(lambda x, y, z, c: (x, y ^ n, z, c) if c == 0 else (x ^ n, y, z, c))
 
 
 def far_moves(n):
@@ -386,7 +389,7 @@
     rows_out = stacked[:, :12, 1, :].reshape(BS, C)
     bias_row = jnp.pad(stacked[:, 12, 0, :12].reshape(1, BS), ((0, 15), (0, C - BS)))
     block = jnp.concatenate([rows_in, rows_out, bias_row], axis=0)
-    near = [block] + [lax.ppermute(block, AXES, near_moves(n)) for n in (1, -1, 2)]
+    near = [block] + [lax.ppermute(block, AXES, near_moves(n)) for n in (1, 3, 2)]
 
     moved = lax.all_to_all(modes, AXES, split_axis=0, concat_axis=0, tiled=True)
 
@@ -400,21 +403,20 @@
     mode_call = pl.pallas_call(
         mode_kernel,
         out_shape=shape((H, 2, C), bf16),
-        in_specs=[pl.BlockSpec(memory_space=pltpu.SMEM)] + anywhere(9),
+        in_specs=[pl.BlockSpec(memory_space=pltpu.SMEM)] + vmem(1) + anywhere(8),
         out_specs=vmem(1)[0],
-        scratch_shapes=[pltpu.VMEM((H, 2, C), bf16)]
-        + [pltpu.VMEM((2 * H, 2 * H), bf16)] * 2
+        scratch_shapes=[pltpu.VMEM((2 * H, 2 * H), bf16)] * 2
         + [pltpu.VMEM((2, H, H), bf16)] * 2
         + [
             pltpu.VMEM((4, 2, 2, BS + 16, 2 * BS), bf16),
             pltpu.VMEM((2, H, C), bf16),
             pltpu.VMEM((2, H, C), bf16),
-            pltpu.SemaphoreType.DMA((9,)),
+            pltpu.SemaphoreType.DMA((8,)),
         ],
         compiler_params=params,
         name="mode",
     )
-    mixed = mode_call(own, moved, lat_h, lat_l, tal_h, tal_l, *filters)
+    mixed = mode_call(own, held(moved), lat_h, lat_l, tal_h, tal_l, *filters)
 
     returned = lax.all_to_all(mixed, AXES, split_axis=0, concat_axis=0, tiled=True)
     other = [lax.ppermute(g, AXES, core_moves) for g in far]
@@ -422,10 +424,9 @@
     out = pl.pallas_call(
         tail_kernel,
         out_shape=shape((6 * W, 128), f32),
-        in_specs=anywhere(4) + vmem(3) + anywhere(10),
+        in_specs=vmem(1) + anywhere(3) + vmem(3) + anywhere(10),
         out_specs=anywhere(1)[0],
         scratch_shapes=[
-            pltpu.VMEM((KW, 2, C), bf16),
             pltpu.VMEM((3, 2, PART, KW), bf16),
             pltpu.VMEM((3, 2, PART, KW), bf16),
             pltpu.VMEM((6 * W, 128), f32),
@@ -433,14 +434,14 @@
             pltpu.VMEM((ROWS, C), bf16),
             pltpu.VMEM((ROWS, C), f32),
             pltpu.VMEM((6 * W, 128), f32),
-            pltpu.SemaphoreType.DMA((9,)),
+            pltpu.SemaphoreType.DMA((8,)),
             pltpu.SemaphoreType.DMA((10,)),
             pltpu.SemaphoreType.DMA((4,)),
         ],
         compiler_params=params,
         name="tail",
     )(
-        returned,
+        held(returned),
         back_h,
         back_l,
         base,

time: 153 us -> 152 us (level)
  starting transfers between devices: 61.7 us -> 63.5 us
  local copies, waits for them, and re-layouts: 4.38 us -> 2.64 us
    unnamed x10 -> x6, local copies, waits for them, and re-layouts: 1.75 us -> 0.01 us
    all_to_all x1, starting transfers between devices: 18 us -> 19.7 us  [per_device(): lax.all_to_all(mixed, AXES, split_axis=0, concat_axis=0, tiled=True)]
  transfers between devices with their start and end apart: 21 -> 21, of which waited for: 10 -> 11; matrix products, arithmetic and copies ran while one was open for 3% -> 3% of each run, Pallas kernels for 9% -> 9%
where the time goes in v6:
time: 152 us; the launch traced here: 151 us
  starting transfers between devices  63.5 us (42%)
  waiting for transfers between devices  50.1 us (33%)
  Pallas kernels  32.4 us (21%)
  local copies, waits for them, and re-layouts  2.64 us (2%)
  other arithmetic  2.49 us (2%)
    all_to_all x1, starting transfers between devices, per_device(): lax.all_to_all(mixed, AXES, split_axis=0, concat_axis=0, tiled=True)  19.7 us
    pallas_call x1, Pallas kernels, per_device(): pl.pallas_call(tail_kernel, out_shape=shape((6 * W, 128), f32), in_specs=...  19.5 us
    all_to_all x1, starting transfers between devices, per_device(): moved = lax.all_to_all(modes, AXES, split_axis=0, concat_axis=0, tiled=True)  16.1 us
    ppermute x3, waiting for transfers between devices, per_device(): lax.ppermute(block, AXES, near_moves(n))  13.6 us
    ppermute x3, waiting for transfers between devices, per_device(): lax.ppermute(pair, AXES, block_moves(b))  11.4 us
    ppermute x1, waiting for transfers between devices, per_device(): lax.ppermute(right[2:], AXES, far_moves(-1))  10.7 us
    ppermute x1, starting transfers between devices, per_device(): one = lax.ppermute(shard, AXES, z_moves(4))  7.81 us
    pallas_call x1, Pallas kernels, per_device(): mixed = mode_call(own, held(moved), lat_h, lat_l, tal_h, tal_l, *filters)  6.58 us
  transfers between devices with their start and end apart: 21, of which 11 were waited for; matrix products, arithmetic and copies ran while one was open for 3% of the time, Pallas kernels for 9%

profile of v6, /device:TPU:1, one launch (start us, length us, event | category | flops | bytes accessed | tf_op | source)
XLA Modules:
  0.0 151.4 jit_solution(10720607395894845667)
XLA Ops:
  0.0 0.8 fusion.2
  0.8 7.8 %collective-permute-start.4 = (bf16[13,2,768]{2,1,0:T(2,128)(2,1)S(1)}, bf16[13,2,768]{2,1,0:T(2,128)(2,1)S(1)}, u32[]{:S(2)}, u32[]{:S(2)}) collective-permute-start(bf16[13,2,768]{2,1,0:T(2,128)(2,1)S(1)} %fusion.2), channel_id=1, source_target_pairs={{0,128},{1,129},{2,130},{3,131},{4,132},{5,133},{6,134},{7,135},{8... | collective-permute-start | bytes 119816 | tf_op jit(solution)/shard_map/ppermute | solution.py:348
  8.6 1.4 collective-permute-done.4
  10.1 1.5 %collective-permute-start.5 = (bf16[26,2,768]{2,1,0:T(2,128)(2,1)S(1)}, bf16[26,2,768]{2,1,0:T(2,128)(2,1)S(1)}, u32[]{:S(2)}, u32[]{:S(2)}) collective-permute-start(bf16[26,2,768]{2,1,0:T(2,128)(2,1)S(1)} %pad_maximum_fusion.4), channel_id=1, source_target_pairs={{0,64},{1,65},{2,66},{3,67},{4,68},{5,69},{6,70},{7,71},{8,72},{9,... | collective-permute-start | bytes 239624 | tf_op jit(solution)/shard_map/ppermute | solution.py:380
  11.7 3.6 %collective-permute-done.5 = bf16[26,2,768]{2,1,0:T(2,128)(2,1)S(1)} collective-permute-done((bf16[26,2,768]{2,1,0:T(2,128)(2,1)S(1)}, bf16[26,2,768]{2,1,0:T(2,128)(2,1)S(1)}, u32[]{:S(2)}, u32[]{:S(2)}) %collective-permute-start.5) | collective-permute-done | bytes 79904 | tf_op jit(solution)/shard_map/ppermute | solution.py:380
  15.6 6.4 %lon.1 = (bf16[256,2,768]{2,1,0:T(2,128)(2,1)}, f32[5400,128]{1,0:T(8,128)}, bf16[2,112,192]{2,1,0:T(8,128)(2,1)}) custom-call(f32[5400,128]{1,0:T(8,128)} %bitcast.21, f32[6,128]{1,0:T(8,128)} %bitcast.31, f32[6,128]{1,0:T(8,128)} %bitcast.32, bf16[2,256,512]{2,1,0:T(8,128)(2,1)} %constant.30.clone.th_hbm, bf16[2,256,512]{2,1,0:T(8,128)(2,1)} %constant.31.clone.tl_hbm, ...), custom_call_target="tpu_custom_call" | custom-call | tf_op jit(solution)/shard_map/lon/pallas_call | solution.py:350
  21.9 16.1 %all-to-all-start = ((bf16[256,2,768]{2,1,0:T(2,128)(2,1)}), bf16[256,2,768]{2,1,0:T(2,128)(2,1)S(1)}, u32[]{:S(2)}, u32[]{:S(2)}) async-start(bf16[256,2,768]{2,1,0:T(2,128)(2,1)} %get-tuple-element.8), calls=%async_computation | async-start | bytes 1572864 | tf_op jit(solution)/shard_map/all_to_all | solution.py:394
  38.5 1.3 slice_reduce_fusion.1
  40.0 2.7 %collective-permute-start.8 = (bf16[208,768]{1,0:T(8,128)(2,1)S(1)}, bf16[208,768]{1,0:T(8,128)(2,1)S(1)}, u32[]{:S(2)}, u32[]{:S(2)}) collective-permute-start(bf16[208,768]{1,0:T(8,128)(2,1)S(1)} %get-tuple-element.14), channel_id=1, source_target_pairs={{0,48},{1,49},{2,50},{3,51},{4,52},{5,53},{6,54},{7,55},{8,11},{9,... | collective-permute-start | bytes 958472 | tf_op jit(solution)/shard_map/ppermute | solution.py:392
  42.7 1.3 collective-permute-start.9
  44.0 5.9 %collective-permute-done.8 = bf16[208,768]{1,0:T(8,128)(2,1)S(1)} collective-permute-done((bf16[208,768]{1,0:T(8,128)(2,1)S(1)}, bf16[208,768]{1,0:T(8,128)(2,1)S(1)}, u32[]{:S(2)}, u32[]{:S(2)}) %collective-permute-start.8) | collective-permute-done | bytes 319520 | tf_op jit(solution)/shard_map/ppermute | solution.py:392
  49.9 1.5 %collective-permute-done.7 = bf16[208,768]{1,0:T(8,128)(2,1)S(1)} collective-permute-done((bf16[208,768]{1,0:T(8,128)(2,1)S(1)}, bf16[208,768]{1,0:T(8,128)(2,1)S(1)}, u32[]{:S(2)}, u32[]{:S(2)}) %collective-permute-start.7) | collective-permute-done | bytes 319520 | tf_op jit(solution)/shard_map/ppermute | solution.py:392
  51.4 6.2 %collective-permute-done.9 = bf16[208,768]{1,0:T(8,128)(2,1)S(1)} collective-permute-done((bf16[208,768]{1,0:T(8,128)(2,1)S(1)}, bf16[208,768]{1,0:T(8,128)(2,1)S(1)}, u32[]{:S(2)}, u32[]{:S(2)}) %collective-permute-start.9) | collective-permute-done | bytes 319520 | tf_op jit(solution)/shard_map/ppermute | solution.py:392
  57.8 2.7 %collective-permute-start.11 = (bf16[4,208,768]{2,1,0:T(8,128)(2,1)S(1)}, bf16[4,208,768]{2,1,0:T(8,128)(2,1)S(1)}, u32[]{:S(2)}, u32[]{:S(2)}) collective-permute-start(bf16[4,208,768]{2,1,0:T(8,128)(2,1)S(1)} %pad_maximum_fusion.refs_0_), channel_id=1, source_target_pairs={{0,3},{1,0},{2,1},{3,2},{4,7},{5,4},{6,5},{7,6},{8,56},{9,57},{10,... | collective-permute-start | bytes 3833864 | tf_op jit(solution)/shard_map/ppermute | solution.py:398
  60.5 1.0 collective-permute-start
  61.5 2.9 %collective-permute-done = bf16[2,112,192]{2,1,0:T(8,128)(2,1)S(1)} collective-permute-done((bf16[2,112,192]{2,1,0:T(8,128)(2,1)S(1)}, bf16[2,112,192]{2,1,0:T(8,128)(2,1)S(1)}, u32[]{:S(2)}, u32[]{:S(2)}) %collective-permute-start) | collective-permute-done | bytes 86048 | tf_op jit(solution)/shard_map/ppermute | solution.py:384
  65.2 2.2 %collective-permute-start.3 = (bf16[2,2,112,192]{3,2,1,0:T(8,128)(2,1)}, bf16[2,2,112,192]{3,2,1,0:T(8,128)(2,1)}, u32[]{:S(2)}, u32[]{:S(2)}) collective-permute-start(bf16[2,2,112,192]{3,2,1,0:T(8,128)(2,1)} %pad_maximum_fusion.2.w0), channel_id=1, source_target_pairs={{0,3},{1,2},{2,1},{3,0},{4,7},{5,6},{6,5},{7,4},{8,11},{9,10},{10,... | collective-permute-start | bytes 516104 | tf_op jit(solution)/shard_map/ppermute | solution.py:386
  67.4 1.0 collective-permute-start.1
  68.4 8.3 %collective-permute-done.3.w3 = bf16[2,2,112,192]{3,2,1,0:T(8,128)(2,1)} collective-permute-done((bf16[2,2,112,192]{3,2,1,0:T(8,128)(2,1)}, bf16[2,2,112,192]{3,2,1,0:T(8,128)(2,1)}, u32[]{:S(2)}, u32[]{:S(2)}) %collective-permute-start.3) | collective-permute-done | bytes 172064 | tf_op jit(solution)/shard_map/ppermute | solution.py:386
  76.7 3.1 %collective-permute-done.1.w1 = bf16[2,2,112,192]{3,2,1,0:T(8,128)(2,1)} collective-permute-done((bf16[2,2,112,192]{3,2,1,0:T(8,128)(2,1)}, bf16[2,2,112,192]{3,2,1,0:T(8,128)(2,1)}, u32[]{:S(2)}, u32[]{:S(2)}) %collective-permute-start.1) | collective-permute-done | bytes 172064 | tf_op jit(solution)/shard_map/ppermute | solution.py:386
  79.8 6.6 %mode.1 = bf16[256,2,768]{2,1,0:T(2,128)(2,1)} custom-call(s32[1]{0:T(128)} %bitcast.own_ref, bf16[256,2,768]{2,1,0:T(2,128)(2,1)S(1)} %all-to-all-done.x_ref, bf16[512,512]{1,0:T(8,128)(2,1)} %constant.32.clone.fh_hbm, bf16[512,512]{1,0:T(8,128)(2,1)} %constant.33.clone.fl_hbm, bf16[2,256,256]{2,1,0:T(8,128)(2,1)} %constant.34.clone.gh_hbm, ...), custom_call_target="tpu_custom_call" | custom-call | tf_op jit(solution)/shard_map/mode/pallas_call | solution.py:419
  86.4 19.7 %all-to-all-start.1 = ((bf16[256,2,768]{2,1,0:T(2,128)(2,1)}), bf16[256,2,768]{2,1,0:T(2,128)(2,1)S(1)}, u32[]{:S(2)}, u32[]{:S(2)}) async-start(bf16[256,2,768]{2,1,0:T(2,128)(2,1)} %mode.1), calls=%async_computation.1 | async-start | bytes 1572864 | tf_op jit(solution)/shard_map/all_to_all | solution.py:421
  106.1 2.2 %collective-permute-start.14 = (bf16[4,208,768]{2,1,0:T(8,128)(2,1)S(1)}, bf16[4,208,768]{2,1,0:T(8,128)(2,1)}, u32[]{:S(2)}, u32[]{:S(2)}) collective-permute-start(bf16[4,208,768]{2,1,0:T(8,128)(2,1)S(1)} %pad_maximum_fusion.refs_0_), channel_id=1, source_target_pairs={{0,8},{1,9},{2,10},{3,11},{4,12},{5,13},{6,14},{7,15},{8,0},{9,1},... | collective-permute-start | bytes 3833864 | tf_op jit(solution)/shard_map/ppermute | solution.py:422
  108.4 0.9 collective-permute-start.13
  109.7 1.1 slice.23
  111.1 1.1 collective-permute-start.12
  112.2 10.7 %collective-permute-done.13.refs_4_ = bf16[2,208,768]{2,1,0:T(8,128)(2,1)} collective-permute-done((bf16[2,208,768]{2,1,0:T(8,128)(2,1)S(1)}, bf16[2,208,768]{2,1,0:T(8,128)(2,1)}, u32[]{:S(2)}, u32[]{:S(2)}) %collective-permute-start.13) | collective-permute-done | bytes 639008 | tf_op jit(solution)/shard_map/ppermute | solution.py:399
  122.9 1.4 collective-permute-start.18
  124.3 2.8 %collective-permute-done.12.refs_3_ = bf16[2,208,768]{2,1,0:T(8,128)(2,1)} collective-permute-done((bf16[2,208,768]{2,1,0:T(8,128)(2,1)S(1)}, bf16[2,208,768]{2,1,0:T(8,128)(2,1)}, u32[]{:S(2)}, u32[]{:S(2)}) %collective-permute-start.12) | collective-permute-done | bytes 639008 | tf_op jit(solution)/shard_map/ppermute | solution.py:399
  127.1 1.1 collective-permute-start.17
  128.1 3.6 %all-to-all-done.1.x_ref = bf16[256,2,768]{2,1,0:T(2,128)(2,1)S(1)} async-done(((bf16[256,2,768]{2,1,0:T(2,128)(2,1)}), bf16[256,2,768]{2,1,0:T(2,128)(2,1)S(1)}, u32[]{:S(2)}, u32[]{:S(2)}) %all-to-all-start.1) | async-done | bytes 786464 | tf_op jit(solution)/shard_map/all_to_all | solution.py:421
  131.8 19.5 %tail.1 = f32[5400,128]{1,0:T(8,128)} custom-call(bf16[256,2,768]{2,1,0:T(2,128)(2,1)S(1)} %all-to-all-done.1.x_ref, bf16[3,2,152,256]{3,2,1,0:T(8,128)(2,1)} %constant.36.clone.th_hbm, bf16[3,2,152,256]{3,2,1,0:T(8,128)(2,1)} %constant.37.clone.tl_hbm, f32[5400,128]{1,0:T(8,128)} %get-tuple-element.10.base_hbm, f32[6,128]{1,0:T(8,128)} %bitcast.33, ...), custom_call_target="tpu_custom_call" | custom-call | tf_op jit(solution)/shard_map/tail/pallas_call | solution.py:424
  (33 shorter events, 2.6 us)
Async XLA Ops:
  0.8 9.2 %collective-permute-start.4 = (bf16[13,2,768]{2,1,0:T(2,128)(2,1)S(1)}, bf16[13,2,768]{2,1,0:T(2,128)(2,1)S(1)}, u32[]{:S(2)}, u32[]{:S(2)}) collective-permute-start(bf16[13,2,768]{2,1,0:T(2,128)(2,1)S(1)} %fusion.2), channel_id=1, source_target_pairs={{0,128},{1,129},{2,130},{3,131},{4,132},{5,133},{6,134},{7,135},{8... | collective-permute-start | bytes 119816 | tf_op jit(solution)/shard_map/ppermute | solution.py:348
  10.1 5.1 %collective-permute-start.5 = (bf16[26,2,768]{2,1,0:T(2,128)(2,1)S(1)}, bf16[26,2,768]{2,1,0:T(2,128)(2,1)S(1)}, u32[]{:S(2)}, u32[]{:S(2)}) collective-permute-start(bf16[26,2,768]{2,1,0:T(2,128)(2,1)S(1)} %pad_maximum_fusion.4), channel_id=1, source_target_pairs={{0,64},{1,65},{2,66},{3,67},{4,68},{5,69},{6,70},{7,71},{8,72},{9,... | collective-permute-start | bytes 239624 | tf_op jit(solution)/shard_map/ppermute | solution.py:380
  15.5 22.6 %collective-permute-start.6 = (bf16[52,2,768]{2,1,0:T(2,128)(2,1)S(1)}, bf16[52,2,768]{2,1,0:T(2,128)(2,1)S(1)}, u32[]{:S(2)}, u32[]{:S(2)}) collective-permute-start(bf16[52,2,768]{2,1,0:T(2,128)(2,1)S(1)} %pad_maximum_fusion.3), channel_id=1, source_target_pairs={{0,4},{1,5},{2,6},{3,7},{4,0},{5,1},{6,2},{7,3},{8,12},{9,13},{10,... | collective-permute-start | bytes 479240 | tf_op jit(solution)/shard_map/ppermute | solution.py:382
  21.9 57.9 %all-to-all-start = ((bf16[256,2,768]{2,1,0:T(2,128)(2,1)}), bf16[256,2,768]{2,1,0:T(2,128)(2,1)S(1)}, u32[]{:S(2)}, u32[]{:S(2)}) async-start(bf16[256,2,768]{2,1,0:T(2,128)(2,1)} %get-tuple-element.8), calls=%async_computation | async-start | bytes 1572864 | tf_op jit(solution)/shard_map/all_to_all | solution.py:394
  40.0 9.8 %collective-permute-start.8 = (bf16[208,768]{1,0:T(8,128)(2,1)S(1)}, bf16[208,768]{1,0:T(8,128)(2,1)S(1)}, u32[]{:S(2)}, u32[]{:S(2)}) collective-permute-start(bf16[208,768]{1,0:T(8,128)(2,1)S(1)} %get-tuple-element.14), channel_id=1, source_target_pairs={{0,48},{1,49},{2,50},{3,51},{4,52},{5,53},{6,54},{7,55},{8,11},{9,... | collective-permute-start | bytes 958472 | tf_op jit(solution)/shard_map/ppermute | solution.py:392
  42.7 8.7 %collective-permute-start.7 = (bf16[208,768]{1,0:T(8,128)(2,1)S(1)}, bf16[208,768]{1,0:T(8,128)(2,1)S(1)}, u32[]{:S(2)}, u32[]{:S(2)}) collective-permute-start(bf16[208,768]{1,0:T(8,128)(2,1)S(1)} %get-tuple-element.14), channel_id=1, source_target_pairs={{0,16},{1,17},{2,18},{3,19},{4,20},{5,21},{6,22},{7,23},{8,9},{9,8... | collective-permute-start | bytes 958472 | tf_op jit(solution)/shard_map/ppermute | solution.py:392
  42.7 14.9 %collective-permute-start.9 = (bf16[208,768]{1,0:T(8,128)(2,1)S(1)}, bf16[208,768]{1,0:T(8,128)(2,1)S(1)}, u32[]{:S(2)}, u32[]{:S(2)}) collective-permute-start(bf16[208,768]{1,0:T(8,128)(2,1)S(1)} %get-tuple-element.14), channel_id=1, source_target_pairs={{0,32},{1,33},{2,34},{3,35},{4,36},{5,37},{6,38},{7,39},{8,10},{9,... | collective-permute-start | bytes 958472 | tf_op jit(solution)/shard_map/ppermute | solution.py:392
  57.6 2.9 %copy-start.2 = (bf16[2,112,192]{2,1,0:T(8,128)(2,1)S(1)}, bf16[2,112,192]{2,1,0:T(8,128)(2,1)}, u32[]{:S(2)}) copy-start(bf16[2,112,192]{2,1,0:T(8,128)(2,1)} %get-tuple-element.9) | copy-start | bytes 258052
  57.8 48.3 %copy-start = (bf16[4,208,768]{2,1,0:T(8,128)(2,1)}, bf16[4,208,768]{2,1,0:T(8,128)(2,1)S(1)}, u32[]{:S(2)}) copy-start(bf16[4,208,768]{2,1,0:T(8,128)(2,1)S(1)} %pad_maximum_fusion.refs_0_) | copy-start | bytes 3833860
  57.8 50.6 %collective-permute-start.11 = (bf16[4,208,768]{2,1,0:T(8,128)(2,1)S(1)}, bf16[4,208,768]{2,1,0:T(8,128)(2,1)S(1)}, u32[]{:S(2)}, u32[]{:S(2)}) collective-permute-start(bf16[4,208,768]{2,1,0:T(8,128)(2,1)S(1)} %pad_maximum_fusion.refs_0_), channel_id=1, source_target_pairs={{0,3},{1,0},{2,1},{3,2},{4,7},{5,4},{6,5},{7,6},{8,56},{9,57},{10,... | collective-permute-start | bytes 3833864 | tf_op jit(solution)/shard_map/ppermute | solution.py:398
  60.5 49.2 %collective-permute-start.10 = (bf16[4,208,768]{2,1,0:T(8,128)(2,1)S(1)}, bf16[4,208,768]{2,1,0:T(8,128)(2,1)}, u32[]{:S(2)}, u32[]{:S(2)}) collective-permute-start(bf16[4,208,768]{2,1,0:T(8,128)(2,1)S(1)} %pad_maximum_fusion.refs_0_), channel_id=1, source_target_pairs={{0,1},{1,2},{2,3},{3,0},{4,5},{5,6},{6,7},{7,4},{8,24},{9,25},{10,... | collective-permute-start | bytes 3833864 | tf_op jit(solution)/shard_map/ppermute | solution.py:397
  60.5 3.9 %collective-permute-start = (bf16[2,112,192]{2,1,0:T(8,128)(2,1)S(1)}, bf16[2,112,192]{2,1,0:T(8,128)(2,1)S(1)}, u32[]{:S(2)}, u32[]{:S(2)}) collective-permute-start(bf16[2,112,192]{2,1,0:T(8,128)(2,1)S(1)} %copy-done.2), channel_id=1, source_target_pairs={{0,4},{1,5},{2,6},{3,7},{4,0},{5,1},{6,2},{7,3},{8,12},{9,13},{10,... | collective-permute-start | bytes 258056 | tf_op jit(solution)/shard_map/ppermute | solution.py:384
  65.2 11.5 %collective-permute-start.3 = (bf16[2,2,112,192]{3,2,1,0:T(8,128)(2,1)}, bf16[2,2,112,192]{3,2,1,0:T(8,128)(2,1)}, u32[]{:S(2)}, u32[]{:S(2)}) collective-permute-start(bf16[2,2,112,192]{3,2,1,0:T(8,128)(2,1)} %pad_maximum_fusion.2.w0), channel_id=1, source_target_pairs={{0,3},{1,2},{2,1},{3,0},{4,7},{5,6},{6,5},{7,4},{8,11},{9,10},{10,... | collective-permute-start | bytes 516104 | tf_op jit(solution)/shard_map/ppermute | solution.py:386
  67.4 9.3 %collective-permute-start.2 = (bf16[2,2,112,192]{3,2,1,0:T(8,128)(2,1)}, bf16[2,2,112,192]{3,2,1,0:T(8,128)(2,1)}, u32[]{:S(2)}, u32[]{:S(2)}) collective-permute-start(bf16[2,2,112,192]{3,2,1,0:T(8,128)(2,1)} %pad_maximum_fusion.2.w0), channel_id=1, source_target_pairs={{0,2},{1,3},{2,0},{3,1},{4,6},{5,7},{6,4},{7,5},{8,10},{9,11},{10,... | collective-permute-start | bytes 516104 | tf_op jit(solution)/shard_map/ppermute | solution.py:386
  67.4 12.4 %collective-permute-start.1 = (bf16[2,2,112,192]{3,2,1,0:T(8,128)(2,1)}, bf16[2,2,112,192]{3,2,1,0:T(8,128)(2,1)}, u32[]{:S(2)}, u32[]{:S(2)}) collective-permute-start(bf16[2,2,112,192]{3,2,1,0:T(8,128)(2,1)} %pad_maximum_fusion.2.w0), channel_id=1, source_target_pairs={{0,1},{1,0},{2,3},{3,2},{4,5},{5,4},{6,7},{7,6},{8,9},{9,8},{10,11... | collective-permute-start | bytes 516104 | tf_op jit(solution)/shard_map/ppermute | solution.py:386
  86.4 45.4 %all-to-all-start.1 = ((bf16[256,2,768]{2,1,0:T(2,128)(2,1)}), bf16[256,2,768]{2,1,0:T(2,128)(2,1)S(1)}, u32[]{:S(2)}, u32[]{:S(2)}) async-start(bf16[256,2,768]{2,1,0:T(2,128)(2,1)} %mode.1), calls=%async_computation.1 | async-start | bytes 1572864 | tf_op jit(solution)/shard_map/all_to_all | solution.py:421
  106.1 22.0 %collective-permute-start.14 = (bf16[4,208,768]{2,1,0:T(8,128)(2,1)S(1)}, bf16[4,208,768]{2,1,0:T(8,128)(2,1)}, u32[]{:S(2)}, u32[]{:S(2)}) collective-permute-start(bf16[4,208,768]{2,1,0:T(8,128)(2,1)S(1)} %pad_maximum_fusion.refs_0_), channel_id=1, source_target_pairs={{0,8},{1,9},{2,10},{3,11},{4,12},{5,13},{6,14},{7,15},{8,0},{9,1},... | collective-permute-start | bytes 3833864 | tf_op jit(solution)/shard_map/ppermute | solution.py:422
  108.4 2.5 %copy-start.1 = (bf16[4,208,768]{2,1,0:T(8,128)(2,1)}, bf16[4,208,768]{2,1,0:T(8,128)(2,1)S(1)}, u32[]{:S(2)}) copy-start(bf16[4,208,768]{2,1,0:T(8,128)(2,1)S(1)} %collective-permute-done.11.refs_2_) | copy-start | bytes 3833860
  108.4 14.5 %collective-permute-start.13 = (bf16[2,208,768]{2,1,0:T(8,128)(2,1)S(1)}, bf16[2,208,768]{2,1,0:T(8,128)(2,1)}, u32[]{:S(2)}, u32[]{:S(2)}) collective-permute-start(bf16[2,208,768]{2,1,0:T(8,128)(2,1)S(1)} %slice.24), channel_id=1, source_target_pairs={{0,3},{1,0},{2,1},{3,2},{4,7},{5,4},{6,5},{7,6},{8,56},{9,57},{10,... | collective-permute-start | bytes 1916936 | tf_op jit(solution)/shard_map/ppermute | solution.py:399
  109.3 22.4 %collective-permute-start.16 = (bf16[4,208,768]{2,1,0:T(8,128)(2,1)S(1)}, bf16[4,208,768]{2,1,0:T(8,128)(2,1)}, u32[]{:S(2)}, u32[]{:S(2)}) collective-permute-start(bf16[4,208,768]{2,1,0:T(8,128)(2,1)S(1)} %collective-permute-done.11.refs_2_), channel_id=1, source_target_pairs={{0,8},{1,9},{2,10},{3,11},{4,12},{5,13},{6,14},{7,15},{8,0},{9,1},... | collective-permute-start | bytes 3833864 | tf_op jit(solution)/shard_map/ppermute | solution.py:422
  110.8 21.0 %collective-permute-start.15 = (bf16[4,208,768]{2,1,0:T(8,128)(2,1)}, bf16[4,208,768]{2,1,0:T(8,128)(2,1)}, u32[]{:S(2)}, u32[]{:S(2)}) collective-permute-start(bf16[4,208,768]{2,1,0:T(8,128)(2,1)} %collective-permute-done.10.refs_1_), channel_id=1, source_target_pairs={{0,8},{1,9},{2,10},{3,11},{4,12},{5,13},{6,14},{7,15},{8,0},{9,1},... | collective-permute-start | bytes 3833864 | tf_op jit(solution)/shard_map/ppermute | solution.py:422
  111.1 16.0 %collective-permute-start.12 = (bf16[2,208,768]{2,1,0:T(8,128)(2,1)S(1)}, bf16[2,208,768]{2,1,0:T(8,128)(2,1)}, u32[]{:S(2)}, u32[]{:S(2)}) collective-permute-start(bf16[2,208,768]{2,1,0:T(8,128)(2,1)S(1)} %slice.23), channel_id=1, source_target_pairs={{0,1},{1,2},{2,3},{3,0},{4,5},{5,6},{6,7},{7,4},{8,24},{9,25},{10,... | collective-permute-start | bytes 1916936 | tf_op jit(solution)/shard_map/ppermute | solution.py:399
  122.9 8.9 %collective-permute-start.18 = (bf16[2,208,768]{2,1,0:T(8,128)(2,1)}, bf16[2,208,768]{2,1,0:T(8,128)(2,1)}, u32[]{:S(2)}, u32[]{:S(2)}) collective-permute-start(bf16[2,208,768]{2,1,0:T(8,128)(2,1)} %collective-permute-done.13.refs_4_), channel_id=1, source_target_pairs={{0,8},{1,9},{2,10},{3,11},{4,12},{5,13},{6,14},{7,15},{8,0},{9,1},... | collective-permute-start | bytes 1916936 | tf_op jit(solution)/shard_map/ppermute | solution.py:422
  127.1 4.7 %collective-permute-start.17 = (bf16[2,208,768]{2,1,0:T(8,128)(2,1)}, bf16[2,208,768]{2,1,0:T(8,128)(2,1)}, u32[]{:S(2)}, u32[]{:S(2)}) collective-permute-start(bf16[2,208,768]{2,1,0:T(8,128)(2,1)} %collective-permute-done.12.refs_3_), channel_id=1, source_target_pairs={{0,8},{1,9},{2,10},{3,11},{4,12},{5,13},{6,14},{7,15},{8,0},{9,1},... | collective-permute-start | bytes 1916936 | tf_op jit(solution)/shard_map/ppermute | solution.py:422
